TPU v7x, 256 devices: a whole 4x4x8 slice. The times are simulated.
256 devices in a mesh: grp: 8 (over z), blk: 32 (over y, x, core).
Axes of the slice: x: 4, y: 4, z: 8, core: 2. Of those that a mesh axis runs over, the one named last changes fastest.
Arguments:
- embeddings: bfloat16 [8, 2048, 1024], P('grp', 'blk'), may hold values from -72 to 72
- cluster_ids: int32 [8, 2048], P('grp', 'blk'), may hold values from 0 to 63, never falling along the last dimension, each value on 1 to 128 neighbouring positions
- block_list: int32 [8, 256, 2], P('grp', 'blk'), may hold values from 0 to 31, as said below
- block_counts: int32 [8, 32], P('grp', 'blk'), may hold values from 1 to 8, as said below
- pair_targets: float32 [8, 256, 4096], P('grp', 'blk'), may hold values from -6 to 6
- w_left: bfloat16 [1024, 512], replicated, may hold values from -0.125 to 0.125
- w_right: bfloat16 [1024, 512], replicated, may hold values from -0.125 to 0.125
- hidden_bias: float32 [512], replicated, may hold values from -3 to 3
- w_middle: bfloat16 [512, 128], replicated, may hold values from -0.25 to 0.25
- w_final: float32 [128], replicated, may hold values from -0.5 to 0.5
Outputs:
- grad_embeddings: float32 [8, 2048, 1024], P('grp', 'blk')
- grad_left: float32 [1024, 512], replicated
- grad_right: float32 [1024, 512], replicated
- grad_bias: float32 [512], replicated
- grad_middle: float32 [512, 128], replicated
- grad_final: float32 [128], replicated
Inputs may be any that keep to these rules, and one draw needn't show every extreme that they name: `block_list`: entries are panels of the device's own group; the column panel lies within one of the row panel. `block_counts`: slots of a device at and beyond its count are unused; in every group one device has exactly 8.
All inputs are finite; a program needn't handle non-finite values.
Results may differ from a plain program's by a relative error of at most 0.012.
Values may be sent and summed in bfloat16 or wider, within the bound.
No kernel may reach another device: no remote copies, remote signals or barrier semaphores. Data moves between devices by JAX's collectives and lax.ppermute only.
A program may use at most 128 MiB of HBM per device.

v0:
```python
import math

import jax
import jax.numpy as jnp
from jax import lax
from jax.sharding import PartitionSpec as P

PANEL = 64
B_DEV = 8


def silu_slope(value):
    sigmoid_value = jax.nn.sigmoid(value)
    return sigmoid_value * (1.0 + value * (1.0 - sigmoid_value))


def pair_block(
    left_rows,
    right_rows,
    left_ids,
    right_ids,
    row_start,
    col_start,
    pair_target,
    hidden_bias,
    w_middle,
    w_final,
):
    panel_rows = left_rows.shape[0]
    hidden_width = left_rows.shape[1]
    pre_hidden = (
        left_rows.astype(jnp.float32)[:, None, :]
        + right_rows.astype(jnp.float32)[None, :, :]
        + hidden_bias
    )
    hidden = (
        jax.nn.silu(pre_hidden).astype(jnp.bfloat16).reshape(panel_rows * panel_rows, hidden_width)
    )
    pre_upper = jnp.dot(hidden, w_middle, preferred_element_type=jnp.float32)
    upper_act = jax.nn.silu(pre_upper)
    predicted = jnp.sum(upper_act * w_final, axis=1)
    left_pos = row_start + jnp.arange(panel_rows, dtype=jnp.int32)
    right_pos = col_start + jnp.arange(panel_rows, dtype=jnp.int32)
    same_cluster = (left_ids[:, None] == right_ids[None, :]) & (
        left_pos[:, None] != right_pos[None, :]
    )
    residual = jnp.where(same_cluster.reshape(-1), predicted - pair_target, 0.0)
    pair_slope = 16.0 * residual
    grad_final = jnp.sum(upper_act * pair_slope[:, None], axis=0)
    grad_second = (pair_slope[:, None] * w_final[None, :] * silu_slope(pre_upper)).astype(
        jnp.bfloat16
    )
    grad_middle = lax.dot_general(
        hidden, grad_second, (((0,), (0,)), ((), ())), preferred_element_type=jnp.float32
    )
    grad_hidden = lax.dot_general(
        grad_second, w_middle, (((1,), (1,)), ((), ())), preferred_element_type=jnp.float32
    )
    grad_first = grad_hidden.reshape(panel_rows, panel_rows, hidden_width) * silu_slope(pre_hidden)
    return (
        jnp.sum(grad_first, axis=1),
        jnp.sum(grad_first, axis=0),
        jnp.sum(grad_first, axis=(0, 1)),
        grad_middle,
        grad_final,
    )


def local(
    embeddings,
    cluster_ids,
    block_list,
    block_counts,
    pair_targets,
    w_left,
    w_right,
    hidden_bias,
    w_middle,
    w_final,
):
    local_emb = embeddings[0]
    whole_emb, group_ids = (
        lax.all_gather(embeddings, "blk", axis=1, tiled=True),
        lax.all_gather(cluster_ids, "blk", axis=1, tiled=True),
    )
    whole_emb = whole_emb[0]

    def fetch_panels(row_start, col_start):
        row_emb = lax.dynamic_slice_in_dim(whole_emb, row_start, PANEL, 0)
        col_emb = lax.dynamic_slice_in_dim(whole_emb, col_start, PANEL, 0)
        return (
            jnp.dot(row_emb, w_left, preferred_element_type=jnp.float32).astype(jnp.bfloat16),
            jnp.dot(col_emb, w_right, preferred_element_type=jnp.float32).astype(jnp.bfloat16),
        )

    group_ids = group_ids[0]
    local_blocks = block_list[0]
    local_targets = pair_targets[0]
    molecules = group_ids.shape[0]
    hidden_width = w_left.shape[1]

    def slot_step(slot, carry):
        part_left, part_right, sum_bias, sum_middle, sum_final = carry
        entry = lax.dynamic_index_in_dim(local_blocks, slot, 0, keepdims=False)
        row_start = entry[0] * PANEL
        col_start = entry[1] * PANEL
        pair_target = lax.dynamic_index_in_dim(local_targets, slot, 0, keepdims=False)
        left_rows, right_rows = fetch_panels(row_start, col_start)
        grad_rows, grad_cols, grad_bias, grad_middle, grad_final = pair_block(
            left_rows,
            right_rows,
            lax.dynamic_slice_in_dim(group_ids, row_start, PANEL, 0),
            lax.dynamic_slice_in_dim(group_ids, col_start, PANEL, 0),
            row_start,
            col_start,
            pair_target,
            hidden_bias,
            w_middle,
            w_final,
        )
        current = lax.dynamic_slice_in_dim(part_left, row_start, PANEL, 0)
        part_left = lax.dynamic_update_slice_in_dim(part_left, current + grad_rows, row_start, 0)
        current = lax.dynamic_slice_in_dim(part_right, col_start, PANEL, 0)
        part_right = lax.dynamic_update_slice_in_dim(part_right, current + grad_cols, col_start, 0)
        return (
            part_left,
            part_right,
            sum_bias + grad_bias,
            sum_middle + grad_middle,
            sum_final + grad_final,
        )

    empty = jnp.zeros((molecules, hidden_width), jnp.float32)
    start_state = (
        empty,
        empty,
        jnp.zeros((hidden_width,), jnp.float32),
        jnp.zeros(w_middle.shape, jnp.float32),
        jnp.zeros(w_final.shape, jnp.float32),
    )
    part_left, part_right, sum_bias, sum_middle, sum_final = lax.fori_loop(
        0, block_counts[0, 0], slot_step, start_state
    )
    rounded_left = part_left.astype(jnp.bfloat16)
    rounded_right = part_right.astype(jnp.bfloat16)
    own_left, own_right = (
        lax.psum_scatter(
            rounded_left.astype(jnp.float32).astype(jnp.bfloat16),
            "blk",
            scatter_dimension=0,
            tiled=True,
        ).astype(jnp.float32),
        lax.psum_scatter(
            rounded_right.astype(jnp.float32).astype(jnp.bfloat16),
            "blk",
            scatter_dimension=0,
            tiled=True,
        ).astype(jnp.float32),
    )
    left_grad = own_left.astype(jnp.bfloat16)
    right_grad = own_right.astype(jnp.bfloat16)
    grad_local = jnp.dot(left_grad, w_left.T, preferred_element_type=jnp.float32) + jnp.dot(
        right_grad, w_right.T, preferred_element_type=jnp.float32
    )
    weight_left = lax.dot_general(
        local_emb, left_grad, (((0,), (0,)), ((), ())), preferred_element_type=jnp.float32
    )
    weight_right = lax.dot_general(
        local_emb, right_grad, (((0,), (0,)), ((), ())), preferred_element_type=jnp.float32
    )
    summed = lax.psum((weight_left, weight_right, sum_bias, sum_middle, sum_final), ("grp", "blk"))
    devices = lax.axis_size("grp") * lax.axis_size("blk")
    scale = 1.0 / math.sqrt(devices * B_DEV * PANEL)
    return (
        grad_local[None],
        summed[0] * scale,
        summed[1] * scale,
        summed[2] * scale,
        summed[3] * scale,
        summed[4] * scale,
    )


def solution(mesh):
    return jax.shard_map(
        local,
        mesh=mesh,
        in_specs=(
            P("grp", "blk", None),
            P("grp", "blk"),
            P("grp", "blk", None),
            P("grp", "blk"),
            P("grp", "blk", None),
            P(),
            P(),
            P(),
            P(),
            P(),
        ),
        out_specs=(P("grp", "blk", None), P(), P(), P(), P(), P()),
        check_vma=False,
    )
```

profile of v0, /device:TPU:1, one launch (start us, length us, event | category | flops | bytes accessed | tf_op | source)
XLA Modules:
  0.0 782.7 jit_solution(16809696372307641489)
XLA Ops:
  10.7 14.7 %all-reduce = s32[2048]{0:T(1024)S(1)} all-reduce(s32[2048]{0:T(1024)S(1)} %bitcast_dynamic-update-slice_fusion), channel_id=1, replica_groups=mesh['grp'=8,'blk'=32] {'blk'}, use_global_device_ids=true, to_apply=%add | all-reduce | flops 2048 | bytes 16384 | tf_op jit(solution)/shard_map/squeeze | solution.py:96
  25.3 40.4 %all-gather.2.cloned.1.call-done = bf16[1,2048,1024]{2,1,0:T(8,128)(2,1)} async-done(((bf16[1,64,1024]{2,1,0:T(8,128)(2,1)}), bf16[1,2048,1024]{2,1,0:T(8,128)(2,1)}) %all-gather.2.cloned.1.call-update) | async-done | bytes 4194320 | tf_op jit(solution)/shard_map/all_gather | solution.py:83
  71.5 90.3 %while.18 = (s32[]{:T(128)}, f32[2048,512]{1,0:T(8,128)}, f32[2048,512]{1,0:T(8,128)}, f32[512]{0:T(512)S(1)}, f32[512,128]{1,0:T(8,128)}, /*index=5*/f32[128]{0...) while((s32[]{:T(128)}, f32[2048,512]{1,0:T(8,128)}, ...), condition=%wide.region_6.7_spmd, body=%wide.region_0.6_spmd.sunk | while | flops 1822642304 | bytes 153014800 | solution.py:141
  78.0 3.4 multiply_convert_fusion.7
  84.6 5.0 convolution_add_fusion.3
  89.7 5.3 multiply_reduce_fusion.7
  94.9 3.9 fusion.52
  107.9 3.4 multiply_convert_fusion.7
  114.5 5.0 convolution_add_fusion.3
  119.5 5.3 multiply_reduce_fusion.7
  124.8 3.9 fusion.52
  137.7 3.4 multiply_convert_fusion.7
  144.3 5.0 convolution_add_fusion.3
  149.3 5.3 multiply_reduce_fusion.7
  154.6 3.9 fusion.52
  161.8 3.8 convert_element_type.34
  165.7 3.8 convert_element_type.33
  169.6 228.2 %reduce-scatter.5.cloned.1.call-done = bf16[64,512]{1,0:T(8,128)(2,1)} async-done(((bf16[2048,512]{1,0:T(8,128)(2,1)}), bf16[64,512]{1,0:T(8,128)(2,1)}) %reduce-scatter.5.cloned.1.call-update) | async-done | bytes 65552 | tf_op jit(solution)/shard_map/reduce_scatter | solution.py:153
  400.3 87.8 %reduce-scatter.3.cloned.1.call-done = bf16[64,512]{1,0:T(8,128)(2,1)} async-done(((bf16[2048,512]{1,0:T(8,128)(2,1)}), bf16[64,512]{1,0:T(8,128)(2,1)}) %reduce-scatter.3.cloned.1.call-update) | async-done | bytes 65552 | tf_op jit(solution)/shard_map/reduce_scatter | solution.py:147
  488.2 2.7 convolution_bitcast_fusion.1
  490.9 77.4 %all-reduce.1 = (f32[512]{0:T(512)S(1)}, f32[128]{0:T(128)S(1)}) all-reduce(f32[512]{0:T(512)S(1)} %get-tuple-element.95, f32[128]{0:T(128)S(1)} %get-tuple-element.97), channel_id=1, replica_groups=mesh['grp'=8,'blk'=32] {'grp','blk'}, use_global_device_ids=true, to_apply=%region_11.12 | all-reduce | flops 640 | bytes 5120 | tf_op jit(solution)/shard_map/psum | solution.py:171
  572.2 194.3 %all-reduce.5.cloned.1.call-done = (f32[1024,512]{0,1:T(8,128)}, f32[1024,512]{0,1:T(8,128)}, f32[512,128]{1,0:T(8,128)}) async-done(((f32[1024,512]{0,1:T(8,128)}, f32[1024,512]{0,1:T(8,128)}, f32[512,128]{1,0:T(8,128)}), (f32[1024,512]{0,1:T(8,128)}, f32[1024,512]{0,1:T(8,128)}, f32[512,128]{1,0:T(8,128)})) %all-reduce.5.cloned.1.call-update) | async-done | bytes 4456464 | tf_op jit(solution)/shard_map/psum | solution.py:171
  766.5 4.2 broadcast_multiply_fusion
  770.7 2.9 copy.16
  (120 shorter events, 48.0 us)
Async XLA Ops:
  7.2 58.6 %all-gather.2.cloned.1.call-start = ((), (), s32[]{:S(2)}) async-start(), calls=%async_computation.2 | async-start | bytes 4325376 | tf_op jit(solution)/shard_map/all_gather | solution.py:83
  7.9 389.8 %reduce-scatter.5.cloned.1.call-start = ((), (), s32[]{:S(2)}) async-start(), calls=%async_computation.4 | async-start | bytes 2162688 | tf_op jit(solution)/shard_map/reduce_scatter | solution.py:153
  65.8 5.7 copy-start.3
  65.8 5.7 copy-start.8
  65.8 5.7 copy-start.9
  65.8 5.7 copy-start.12
  78.0 3.4 copy-start
  78.0 3.4 copy-start.10
  84.6 5.1 copy-start.1
  84.6 5.1 copy-start.11
  107.8 3.4 copy-start
  107.8 3.4 copy-start.10
  114.4 5.1 copy-start.1
  114.4 5.1 copy-start.11
  137.7 3.4 copy-start
  137.7 3.4 copy-start.10
  144.3 5.1 copy-start.1
  144.3 5.1 copy-start.11
  165.6 322.6 %reduce-scatter.3.cloned.1.call-start = ((), (), s32[]{:S(2)}) async-start(), calls=%async_computation.3 | async-start | bytes 2162688 | tf_op jit(solution)/shard_map/reduce_scatter | solution.py:147
  165.7 232.1 %copy-start.4 = (bf16[1,64,1024]{2,1,0:T(8,128)(2,1)S(1)}, bf16[1,64,1024]{2,1,0:T(8,128)(2,1)}, u32[]{:S(2)}) copy-start(bf16[1,64,1024]{2,1,0:T(8,128)(2,1)} %param.12) | copy-start | bytes 393220
  169.5 597.0 %all-reduce.5.cloned.1.call-start = ((), (), s32[]{:S(2)}) async-start(), calls=%async_computation.5 | async-start | bytes 8912896 | tf_op jit(solution)/shard_map/psum | solution.py:171
  400.3 169.5 %copy-start.5 = (bf16[64,512]{1,0:T(8,128)(2,1)S(1)}, bf16[64,512]{1,0:T(8,128)(2,1)}, u32[]{:S(2)}) copy-start(bf16[64,512]{1,0:T(8,128)(2,1)} %reduce-scatter.5.cloned.1.call-done) | copy-start | bytes 196612
  488.2 81.2 %copy-start.7 = (bf16[64,512]{1,0:T(8,128)(2,1)S(1)}, bf16[64,512]{1,0:T(8,128)(2,1)}, u32[]{:S(2)}) copy-start(bf16[64,512]{1,0:T(8,128)(2,1)} %reduce-scatter.3.cloned.1.call-done) | copy-start | bytes 196612
  770.7 4.7 copy-start.6
  (3 other events, 5.9 us)
Sparse Core Ops, SparseCore 0:
  10.5 55.2 all-gather.1
  165.7 231.9 reduce-scatter.4
  402.1 85.9 reduce-scatter.2
  494.4 272.0 all-reduce.4
where the time goes:
time: 785 us; the launch traced here: 783 us
  waiting for transfers between devices  551 us (70%)
  blocking collectives  92.1 us (12%)
  matrix products  51.4 us (7%)
  other arithmetic  46.6 us (6%)
  local copies, waits for them, and re-layouts  19.4 us (2%)
  between operations  14.5 us (2%)
    reduce_scatter x1, waiting for transfers between devices, local(): lax.psum_scatter(rounded_right.astype(jnp.float32).astype(jnp.bfloat16),...  228 us
    psum x1, waiting for transfers between devices, local(): lax.psum((weight_left, weight_right, sum_bias, sum_middle, sum_final), ('...  194 us
    reduce_scatter x1, waiting for transfers between devices, local(): lax.psum_scatter(rounded_left.astype(jnp.float32).astype(jnp.bfloat16), '...  87.8 us
    psum x1, blocking collectives, local(): lax.psum((weight_left, weight_right, sum_bias, sum_middle, sum_final), ('...  77.4 us
    all_gather x1, waiting for transfers between devices, local(): lax.all_gather(embeddings, 'blk', axis=1, tiled=True)  40.4 us
    dot_general x3, matrix products, pair_block(): lax.dot_general(grad_second, w_middle, (((1,), (1,)), ((), ())), preferre...  15.8 us
  transfers between devices with their start and end apart: 4, of which 4 were waited for; matrix products, arithmetic and copies ran while one was open for 2% of the time, Pallas kernels for 0%

commit v1 on v0

v1 whole, which is shorter than its diff:
```python
import math

import jax
import jax.numpy as jnp
from jax import lax
from jax.experimental import pallas as pl
from jax.experimental.pallas import tpu as pltpu
from jax.sharding import PartitionSpec as P

PANEL = 64
B_DEV = 8
ROWS = 8
BF = jnp.bfloat16
F32 = jnp.float32


def pair_kernel(
    flags,
    left_ref,
    right_o,
    right_m,
    right_p,
    targets_ref,
    mask_ref,
    bias_ref,
    wmt_ref,
    wf_ref,
    out_left,
    out_outer,
    out_own,
    out_partner,
    out_mid,
    out_small,
    left_s,
    right_s,
    tsum_s,
    mask_s,
    hid_s,
    slope_s,
    lacc,
    racc,
    mid_acc,
    fin_acc,
):
    hidden = left_ref.shape[1]
    tile = ROWS * PANEL
    left_s[...] = (left_ref[...].astype(F32) + bias_ref[...]) * 0.5
    for k, ref in enumerate((right_o, right_m, right_p)):
        right_s[k * PANEL : (k + 1) * PANEL, :] = ref[0:PANEL, :].astype(F32) * 0.5
    n_src = targets_ref.shape[0]
    pick = lax.rem(lax.broadcasted_iota(jnp.int32, (8, n_src), 1), 3) == lax.broadcasted_iota(
        jnp.int32, (8, n_src), 0
    )
    tsum = jnp.dot(pick.astype(BF), targets_ref[...], preferred_element_type=F32)
    for k in range(3):
        tsum_s[k, 0:1, :] = tsum[k : k + 1, :]
        mask_s[k, 0:1, :] = mask_ref[k : k + 1, :]
    lacc[...] = jnp.zeros_like(lacc)
    racc[...] = jnp.zeros_like(racc)
    mid_acc[...] = jnp.zeros_like(mid_acc)
    fin_acc[...] = jnp.zeros_like(fin_acc)

    def step(i, carry):
        @pl.when(flags[i] > 0)
        def _():
            k = i // 8
            rt = i % 8
            row0 = pl.multiple_of(rt * ROWS, ROWS)
            col0 = pl.multiple_of(k * PANEL, PANEL)
            lanes = pl.ds(pl.multiple_of(rt * tile, tile), tile)
            left8 = left_s[pl.ds(row0, ROWS), :]
            right = right_s[pl.ds(col0, PANEL), :]
            for a in range(ROWS):
                u = right + left8[a : a + 1, :]
                p = jnp.tanh(u) + 1.0
                h = u * p
                hid_s[a * PANEL : (a + 1) * PANEL, :] = h.astype(BF)
                slope_s[a * PANEL : (a + 1) * PANEL, :] = p + h * (2.0 - p)
            hid = hid_s[...]
            wmt = wmt_ref[...]
            pre = lax.dot_general(wmt, hid, (((1,), (1,)), ((), ())), preferred_element_type=F32)
            u = pre * 0.5
            p = jnp.tanh(u) + 1.0
            act = u * p
            wf = wf_ref[...]
            predicted = jnp.sum(act * wf, axis=0, keepdims=True)
            tsum = tsum_s[k, 0:1, lanes]
            count = tsum_s[k, 0:1, 8 * tile : 8 * tile + 128]
            count = jnp.concatenate([count] * (tile // 128), axis=1)
            mask = mask_s[k, 0:1, lanes]
            pair_slope = (16.0 * mask) * (count * predicted - tsum)
            grad_second = ((0.5 * pair_slope) * wf * (p + act * (2.0 - p))).astype(BF)
            fin = act * pair_slope
            fin_acc[...] += sum(fin[:, j * 128 : (j + 1) * 128] for j in range(tile // 128))
            mid_acc[...] += jnp.dot(grad_second, hid, preferred_element_type=F32)
            grad_hidden = lax.dot_general(
                grad_second, wmt, (((0,), (0,)), ((), ())), preferred_element_type=F32
            )
            cols = None
            rows = []
            for a in range(ROWS):
                g = grad_hidden[a * PANEL : (a + 1) * PANEL, :] * slope_s[a * PANEL : (a + 1) * PANEL, :]
                rows.append(jnp.sum(g, axis=0, keepdims=True))
                cols = g if cols is None else cols + g
            racc[pl.ds(col0, PANEL), :] += cols
            lacc[pl.ds(row0, ROWS), :] += jnp.concatenate(rows, axis=0)

        return carry

    lax.fori_loop(0, 24, step, 0)
    left = lacc[...] * 0.5
    out_left[...] = left.astype(BF)
    for k, ref in enumerate((out_outer, out_own, out_partner)):
        ref[...] = (racc[k * PANEL : (k + 1) * PANEL, :] * 0.5).astype(BF)
    for j in range(hidden // 128):
        block = slice(j * 128, (j + 1) * 128)
        out_mid[:, block] = mid_acc[:, block].T.astype(BF)
    out_small[...] = jnp.zeros_like(out_small)
    out_small[0:1, :] = jnp.sum(left, axis=0, keepdims=True).astype(BF)
    out_small[16:17, 0:128] = jnp.sum(fin_acc[...].T, axis=0, keepdims=True).astype(BF)


def pair_grads(flags, left, right_o, right_m, right_p, targets, mask, bias, wmt, wf):
    hidden = left.shape[1]
    upper = wmt.shape[0]
    tile = ROWS * PANEL
    vmem = pl.BlockSpec(memory_space=pltpu.VMEM)
    panel = jax.ShapeDtypeStruct((PANEL, hidden), BF)
    return pl.pallas_call(
        pair_kernel,
        out_shape=(
            panel,
            panel,
            panel,
            panel,
            jax.ShapeDtypeStruct((upper, hidden), BF),
            jax.ShapeDtypeStruct((upper, hidden), BF),
        ),
        in_specs=[pl.BlockSpec(memory_space=pltpu.SMEM)] + [vmem] * 9,
        out_specs=(vmem,) * 6,
        scratch_shapes=[
            pltpu.VMEM((PANEL, hidden), F32),
            pltpu.VMEM((3 * PANEL, hidden), F32),
            pltpu.VMEM((3, 8, targets.shape[1]), F32),
            pltpu.VMEM((3, 8, mask.shape[1]), F32),
            pltpu.VMEM((tile, hidden), BF),
            pltpu.VMEM((tile, hidden), F32),
            pltpu.VMEM((PANEL, hidden), F32),
            pltpu.VMEM((3 * PANEL, hidden), F32),
            pltpu.VMEM((upper, hidden), F32),
            pltpu.VMEM((upper, 128), F32),
        ],
        cost_estimate=pl.CostEstimate(
            flops=10 * 24 * tile * hidden * upper, bytes_accessed=2 << 20, transcendentals=24 * tile * hidden
        ),
        name="pair_grads",
    )(flags, left, right_o, right_m, right_p, targets, mask, bias, wmt, wf)


def place_kernel(pos, *refs):
    *pieces, out = refs
    shape = pieces[0].shape
    for d, ref in enumerate(pieces):
        slot = lax.rem(pos[0] - (0, 1, 3, 2)[d] + 4, 4)
        if len(out.shape) == len(shape):
            out[pl.ds(pl.multiple_of(slot * shape[0], shape[0]), shape[0]), :] = ref[...]
        else:
            out[slot] = ref[...]


def place(pos, pieces, out_shape, name):
    vmem = pl.BlockSpec(memory_space=pltpu.VMEM)
    return pl.pallas_call(
        place_kernel,
        out_shape=jax.ShapeDtypeStruct(out_shape, pieces[0].dtype),
        in_specs=[pl.BlockSpec(memory_space=pltpu.SMEM)] + [vmem] * len(pieces),
        out_specs=vmem,
        name=name,
    )(pos, *pieces)


def finish_kernel(scale, core, mine_ref, theirs_ref, left_ref, right_ref, mid_ref, bias_ref, fin_ref):
    depth = left_ref.shape[0]

    def write(first, second):
        for j in range(4):
            block = slice(j * 128, (j + 1) * 128)
            left_ref[:, block] = first[j, 0:depth, :].astype(F32) * scale
            right_ref[:, block] = second[j, 0:depth, :].astype(F32) * scale
            mid_ref[block, :] = first[j, depth : depth + 128, :].astype(F32) * scale
            bias_ref[:, block] = second[j, depth : depth + 1, :].astype(F32) * scale
        fin_ref[...] = second[0, depth + 16 : depth + 17, :].astype(F32) * scale

    @pl.when(core[0] == 0)
    def _():
        write(mine_ref, theirs_ref)

    @pl.when(core[0] != 0)
    def _():
        write(theirs_ref, mine_ref)


def local(
    embeddings,
    cluster_ids,
    block_list,
    block_counts,
    pair_targets,
    w_left,
    w_right,
    hidden_bias,
    w_middle,
    w_final,
):
    emb = embeddings[0]
    depth = emb.shape[1]
    hidden = w_left.shape[1]
    upper = w_middle.shape[1]
    panels = lax.axis_size("blk")
    groups = lax.axis_size("grp")
    me = lax.axis_index("blk")
    core, x, y = me % 2, (me // 2) % 4, me // 8

    def blk(value, partner):
        return lax.ppermute(value, "blk", [(i, partner(i)) for i in range(panels)])

    def on_core(value):
        return blk(value, lambda i: i ^ 1)

    def on_outer(value):
        return blk(value, lambda i: (i - 1 if i % 2 == 0 else i + 1) % panels)

    def on_x(value, d):
        return blk(value, lambda i: i // 8 * 8 + (i // 2 % 4 + d) % 4 * 2 + i % 2)

    def on_y(value, d):
        return blk(value, lambda i: (i // 8 + d) % 4 * 8 + i % 8)

    def on_z(value, d):
        return lax.ppermute(value, "grp", [(i, (i + d) % groups) for i in range(groups)])

    entry = block_list[0]
    row, col = entry[:, 0], entry[:, 1]
    step = jnp.where(row % 2 == 0, col - row, row - col)
    slot_of = jnp.where(jnp.arange(B_DEV) < block_counts[0, 0], row * 3 + step + 1, -1)
    place_at = (jnp.arange(3 * panels, dtype=jnp.int32)[:, None] == slot_of[None, :]).astype(BF)
    values = jnp.concatenate(
        [pair_targets[0].astype(BF), jnp.ones((B_DEV, 128), BF)], axis=1
    )
    sums = jnp.dot(place_at, values, preferred_element_type=F32).astype(BF)
    targets = lax.all_to_all(sums, "blk", 0, 0, tiled=True)

    left = jnp.dot(emb, w_left, preferred_element_type=F32).astype(BF)
    right = jnp.dot(emb, w_right, preferred_element_type=F32).astype(BF)
    ids = cluster_ids[0].astype(BF)
    ids_row = jnp.pad(ids[None, :], ((0, 15), (0, hidden - PANEL)))
    right_own = jnp.concatenate([right, ids_row], axis=0)
    right_outer = on_outer(right_own)
    right_partner = on_core(right_own)
    col_ids = jnp.stack([right_outer[PANEL, :PANEL], ids, right_partner[PANEL, :PANEL]])
    same = ids[None, :, None] == col_ids[:, None, :]
    at = jnp.arange(PANEL)
    own = (jnp.arange(3) == 1)[:, None, None] & (at[:, None] == at[None, :])[None]
    mask = (same & ~own).reshape(3, PANEL * PANEL).astype(F32)
    flags = jnp.max(mask.reshape(24, ROWS * PANEL), axis=1).astype(jnp.int32)

    lg, r_outer, r_own, r_partner, mid, small = pair_grads(
        flags,
        left,
        right_outer,
        right_own,
        right_partner,
        targets,
        mask,
        hidden_bias[None, :],
        w_middle.T,
        w_final[:, None],
    )

    emb_pair = jnp.concatenate([emb, on_core(emb)], axis=0)
    emb_all = jnp.concatenate([emb_pair] + [on_x(emb_pair, d) for d in (1, 3, 2)], axis=0)

    first = core == 0
    r_own = (r_own.astype(F32) + on_outer(r_outer).astype(F32)).astype(BF)
    sent = jnp.concatenate(
        [jnp.where(first, r_own, lg), r_partner, jnp.where(first, small, mid)], axis=0
    )
    got = on_core(sent)
    rg = (r_own.astype(F32) + got[PANEL : 2 * PANEL].astype(F32)).astype(BF)
    pair_right = (got[:PANEL].astype(F32) + r_partner.astype(F32)).astype(BF)
    extra = jnp.where(first, mid, small).astype(F32) + got[2 * PANEL :].astype(F32)
    both = jnp.concatenate(
        [jnp.where(first, lg, rg), jnp.where(first, got[:PANEL], pair_right), extra.astype(BF)], axis=0
    )
    grad_local = jnp.dot(lg, w_left.T, preferred_element_type=F32) + jnp.dot(
        rg, w_right.T, preferred_element_type=F32
    )

    def column(d):
        return lax.dynamic_slice_in_dim(both, (x + d) % 4 * 128, 128, 1)

    parts = [column(0)] + [on_x(column(d), d) for d in (1, 3, 2)]
    grads = jnp.concatenate([p[: 2 * PANEL] for p in parts], axis=0)
    weight = lax.dot_general(emb_all, grads, (((0,), (0,)), ((), ())), preferred_element_type=F32)
    extra = sum(p[2 * PANEL :].astype(F32) for p in parts)
    total = jnp.concatenate([weight, extra], axis=0).astype(BF)
    piece = total.shape[0] // 4

    def rows(d):
        return lax.dynamic_slice_in_dim(total, (y + d) % 4 * piece, piece, 0)

    parts = [rows(0)] + [on_y(rows(d), d) for d in (1, 3, 2)]
    total = sum(p.astype(F32) for p in parts).astype(BF)
    total = (
        total.astype(F32)
        + lax.ppermute(total, "grp", [(i, i ^ 1) for i in range(groups)]).astype(F32)
    ).astype(BF)
    total = sum(p.astype(F32) for p in [total] + [on_z(total, d) for d in (2, 6, 4)]).astype(BF)

    total = place(
        y[None], [total] + [on_y(total, d) for d in (1, 3, 2)], (4 * piece, 128), "place_rows"
    )
    mine = place(
        x[None], [total] + [on_x(total, d) for d in (1, 3, 2)], (4, 4 * piece, 128), "place_columns"
    )
    theirs = on_core(mine)
    devices = panels * groups
    scale = 1.0 / math.sqrt(devices * B_DEV * PANEL)
    vmem = pl.BlockSpec(memory_space=pltpu.VMEM)
    grad_left, grad_right, grad_middle, grad_bias, grad_final = pl.pallas_call(
        lambda *refs: finish_kernel(scale, *refs),
        out_shape=(
            jax.ShapeDtypeStruct((depth, hidden), F32),
            jax.ShapeDtypeStruct((depth, hidden), F32),
            jax.ShapeDtypeStruct((hidden, upper), F32),
            jax.ShapeDtypeStruct((1, hidden), F32),
            jax.ShapeDtypeStruct((1, upper), F32),
        ),
        in_specs=[pl.BlockSpec(memory_space=pltpu.SMEM), vmem, vmem],
        out_specs=(vmem,) * 5,
        name="finish",
    )(core[None], mine, theirs)
    return (grad_local[None], grad_left, grad_right, grad_bias[0], grad_middle, grad_final[0])


def solution(mesh):
    return jax.shard_map(
        local,
        mesh=mesh,
        in_specs=(
            P("grp", "blk", None),
            P("grp", "blk"),
            P("grp", "blk", None),
            P("grp", "blk"),
            P("grp", "blk", None),
            P(),
            P(),
            P(),
            P(),
            P(),
        ),
        out_specs=(P("grp", "blk", None), P(), P(), P(), P(), P()),
        check_vma=False,
    )
```

time: 785 us -> 143 us (0.18)
  waiting for transfers between devices: 551 us -> 26 us
  blocking collectives: 92.1 us -> 0 us
  starting transfers between devices: 0.16 us -> 60.5 us
  matrix products: 51.4 us -> 5.38 us
  other arithmetic: 46.6 us -> 6.98 us
  Pallas kernels: 0 us -> 26.2 us
  between operations: 14.5 us -> 1.87 us
    reduce_scatter x2 -> x0, waiting for transfers between devices: 316 us -> none  [the longest x1 228 us: local(): lax.psum_scatter(rounded_right.astype(jnp.float32).astype(jnp.bfloat16),...]
    psum x1 -> x0, waiting for transfers between devices: 194 us -> none  [local(): lax.psum((weight_left, weight_right, sum_bias, sum_middle, sum_final), ('...]
    psum x1 -> x0, blocking collectives: 77.4 us -> none  [local(): lax.psum((weight_left, weight_right, sum_bias, sum_middle, sum_final), ('...]
    ppermute x0 -> x25, starting transfers between devices: none -> 56.6 us  [the longest x21 43.9 us: blk(): return lax.ppermute(value, 'blk', [(i, partner(i)) for i in range(panels)])]
    dot_general x19 -> x6, matrix products: 51.4 us -> 5.38 us  [the longest x1 1.27 us: local(): jnp.dot(rg, w_right.T, preferred_element_type=F32)]
    all_gather x1 -> x0, waiting for transfers between devices: 40.4 us -> none  [local(): lax.all_gather(embeddings, 'blk', axis=1, tiled=True)]
    pallas_call x0 -> x4, Pallas kernels: none -> 26.2 us  [the longest x1 17.8 us: pair_grads(): pl.pallas_call(pair_kernel, out_shape=(panel, panel, panel, panel, jax.Sh...]
    ppermute x0 -> x25, waiting for transfers between devices: none -> 23.7 us  [the longest x21 18 us: blk(): return lax.ppermute(value, 'blk', [(i, partner(i)) for i in range(panels)])]
  transfers between devices with their start and end apart: 4 -> 26, of which waited for: 4 -> 16; matrix products, arithmetic and copies ran while one was open for 2% -> 13% of each run, Pallas kernels for 0% -> 12%
where the time goes in v1:
time: 143 us
  starting transfers between devices  60.5 us (42%)
  Pallas kernels  26.2 us (18%)
  waiting for transfers between devices  26 us (18%)
  local copies, waits for them, and re-layouts  16.1 us (11%)
  other arithmetic  6.98 us (5%)
  matrix products  5.38 us (4%)
  between operations  1.87 us (1%)
    ppermute x21, starting transfers between devices, blk(): return lax.ppermute(value, 'blk', [(i, partner(i)) for i in range(panels)])  43.9 us
    ppermute x21, waiting for transfers between devices, blk(): return lax.ppermute(value, 'blk', [(i, partner(i)) for i in range(panels)])  18 us
    pallas_call x1, Pallas kernels, pair_grads(): pl.pallas_call(pair_kernel, out_shape=(panel, panel, panel, panel, jax.Sh...  17.8 us
    ppermute x3, starting transfers between devices, on_z(): lax.ppermute(value, 'grp', [(i, (i + d) % groups) for i in range(groups)])  8.4 us
    unnamed x55, local copies, waits for them, and re-layouts  7.92 us
    pallas_call x1, Pallas kernels, local(): pl.pallas_call(lambda *refs: finish_kernel(scale, *refs), out_shape=(jax....  4.32 us
    ppermute x1, starting transfers between devices, local(): lax.ppermute(total, 'grp', [(i, i ^ 1) for i in range(groups)]).astype(F32)  4.32 us
    pallas_call x2, Pallas kernels, place(): pl.pallas_call(place_kernel, out_shape=jax.ShapeDtypeStruct(out_shape, pi...  4.09 us
  transfers between devices with their start and end apart: 26, of which 16 were waited for; matrix products, arithmetic and copies ran while one was open for 13% of the time, Pallas kernels for 12%

profile of v1, /device:TPU:1, one launch (start us, length us, event | category | flops | bytes accessed | tf_op | source)
XLA Modules:
  0.0 143.1 jit_solution(3676781651491873762)
XLA Ops:
  3.1 3.3 %collective-permute-start.1 = (bf16[80,512]{1,0:T(8,128)(2,1)S(1)}, bf16[80,512]{1,0:T(8,128)(2,1)}, u32[]{:S(2)}, u32[]{:S(2)}) collective-permute-start(bf16[80,512]{1,0:T(8,128)(2,1)S(1)} %fusion.10.right_m), channel_id=1, source_target_pairs={{0,1},{1,0},{2,3},{3,2},{4,5},{5,4},{6,7},{7,6},{8,9},{9,8},{10,11... | collective-permute-start | bytes 245768 | tf_op jit(solution)/shard_map/ppermute | solution.py:225
  6.4 3.6 %collective-permute-start.4 = (bf16[64,1024]{1,0:T(8,128)(2,1)S(1)}, bf16[64,1024]{1,0:T(8,128)(2,1)S(1)}, u32[]{:S(2)}, u32[]{:S(2)}) collective-permute-start(bf16[64,1024]{1,0:T(8,128)(2,1)S(1)} %bitcast.47), channel_id=1, source_target_pairs={{0,1},{1,0},{2,3},{3,2},{4,5},{5,4},{6,7},{7,6},{8,9},{9,8},{10,11... | collective-permute-start | bytes 393224 | tf_op jit(solution)/shard_map/ppermute | solution.py:225
  12.3 3.9 %all-to-all-start = ((bf16[32,3,4224]{2,1,0:T(4,128)(2,1)}), bf16[32,3,4224]{2,1,0:T(4,128)(2,1)S(1)}, u32[]{:S(2)}, u32[]{:S(2)}) async-start(bf16[32,3,4224]{2,1,0:T(4,128)(2,1)} %all_to_all.7), calls=%async_computation | async-start | bytes 2162688 | tf_op jit(solution)/shard_map/all_to_all | solution.py:251
  26.6 2.7 %collective-permute-start.7 = (bf16[128,1024]{1,0:T(8,128)(2,1)}, bf16[128,1024]{1,0:T(8,128)(2,1)}, u32[]{:S(2)}, u32[]{:S(2)}) collective-permute-start(bf16[128,1024]{1,0:T(8,128)(2,1)} %pad_maximum_fusion.1), channel_id=1, source_target_pairs={{0,4},{1,5},{2,6},{3,7},{4,0},{5,1},{6,2},{7,3},{8,12},{9,13},{10,... | collective-permute-start | bytes 786440 | tf_op jit(solution)/shard_map/ppermute | solution.py:225
  31.5 2.4 %all-to-all-done = bf16[32,3,4224]{2,1,0:T(4,128)(2,1)S(1)} async-done(((bf16[32,3,4224]{2,1,0:T(4,128)(2,1)}), bf16[32,3,4224]{2,1,0:T(4,128)(2,1)S(1)}, u32[]{:S(2)}, u32[]{:S(2)}) %all-to-all-start) | async-done | bytes 811040 | tf_op jit(solution)/shard_map/all_to_all | solution.py:251
  35.3 17.8 %pair_grads.1 = (bf16[64,512]{1,0:T(8,128)(2,1)}, bf16[64,512]{1,0:T(8,128)(2,1)}, bf16[64,512]{1,0:T(8,128)(2,1)}, bf16[64,512]{1,0:T(8,128)(2,1)}, bf16[128,512]{1,0:T(8,128)(2,1)}, /*index=5*/bf16[128,512]{1,0:T(8,128)(2,1)}) custom-call(s32[24]{0:T(128)} %convert_element_type.134.flags, bf16[64,512]{1,0:T(8,128)(2,1)} %convolution_convert_fusion.2.left_ref, ...), custom_call_target="tpu_custom_call" | custom-call | flops 8053063680 | bytes 2097152 | tf_op jit(solution)/shard_map/pair_grads/pallas_call | solution.py:129
  55.3 1.8 %collective-permute-done.2 = bf16[64,512]{1,0:T(8,128)(2,1)S(1)} collective-permute-done((bf16[64,512]{1,0:T(8,128)(2,1)}, bf16[64,512]{1,0:T(8,128)(2,1)S(1)}, u32[]{:S(2)}, u32[]{:S(2)}) %collective-permute-start.2) | collective-permute-done | bytes 65568 | tf_op jit(solution)/shard_map/ppermute | solution.py:225
  69.6 6.6 %collective-permute-start.11 = (bf16[288,128]{1,0:T(8,128)(2,1)S(1)}, bf16[288,128]{1,0:T(8,128)(2,1)S(1)}, u32[]{:S(2)}, u32[]{:S(2)}) collective-permute-start(bf16[288,128]{1,0:T(8,128)(2,1)S(1)} %get-tuple-element.28), channel_id=1, source_target_pairs={{0,8},{1,9},{2,10},{3,11},{4,12},{5,13},{6,14},{7,15},{8,16},{9,17... | collective-permute-start | bytes 221192 | tf_op jit(solution)/shard_map/ppermute | solution.py:225
  76.2 2.6 %collective-permute-start.12 = (bf16[288,128]{1,0:T(8,128)(2,1)S(1)}, bf16[288,128]{1,0:T(8,128)(2,1)S(1)}, u32[]{:S(2)}, u32[]{:S(2)}) collective-permute-start(bf16[288,128]{1,0:T(8,128)(2,1)S(1)} %get-tuple-element.29), channel_id=1, source_target_pairs={{0,24},{1,25},{2,26},{3,27},{4,28},{5,29},{6,30},{7,31},{8,0},{9,1... | collective-permute-start | bytes 221192 | tf_op jit(solution)/shard_map/ppermute | solution.py:225
  78.8 2.9 %collective-permute-start.13 = (bf16[288,128]{1,0:T(8,128)(2,1)S(1)}, bf16[288,128]{1,0:T(8,128)(2,1)S(1)}, u32[]{:S(2)}, u32[]{:S(2)}) collective-permute-start(bf16[288,128]{1,0:T(8,128)(2,1)S(1)} %get-tuple-element.30), channel_id=1, source_target_pairs={{0,16},{1,17},{2,18},{3,19},{4,20},{5,21},{6,22},{7,23},{8,24},{9,... | collective-permute-start | bytes 221192 | tf_op jit(solution)/shard_map/ppermute | solution.py:225
  81.9 1.8 %collective-permute-done.13 = bf16[288,128]{1,0:T(8,128)(2,1)S(1)} collective-permute-done((bf16[288,128]{1,0:T(8,128)(2,1)S(1)}, bf16[288,128]{1,0:T(8,128)(2,1)S(1)}, u32[]{:S(2)}, u32[]{:S(2)}) %collective-permute-start.13) | collective-permute-done | bytes 73760 | tf_op jit(solution)/shard_map/ppermute | solution.py:225
  83.9 4.3 %collective-permute-start.14 = (bf16[288,128]{1,0:T(8,128)(2,1)S(1)}, bf16[288,128]{1,0:T(8,128)(2,1)S(1)}, u32[]{:S(2)}, u32[]{:S(2)}) collective-permute-start(bf16[288,128]{1,0:T(8,128)(2,1)S(1)} %add_convert_fusion.3), channel_id=1, source_target_pairs={{0,32},{32,0},{64,96},{96,64},{128,160},{160,128},{192,224},{224,1... | collective-permute-start | bytes 221192 | tf_op jit(solution)/shard_map/ppermute | solution.py:316
  88.3 1.7 %collective-permute-done.14 = bf16[288,128]{1,0:T(8,128)(2,1)S(1)} collective-permute-done((bf16[288,128]{1,0:T(8,128)(2,1)S(1)}, bf16[288,128]{1,0:T(8,128)(2,1)S(1)}, u32[]{:S(2)}, u32[]{:S(2)}) %collective-permute-start.14) | collective-permute-done | bytes 73760 | tf_op jit(solution)/shard_map/ppermute | solution.py:316
  90.0 6.0 %collective-permute-start.17 = (bf16[288,128]{1,0:T(8,128)(2,1)S(1)}, bf16[288,128]{1,0:T(8,128)(2,1)S(1)}, u32[]{:S(2)}, u32[]{:S(2)}) collective-permute-start(bf16[288,128]{1,0:T(8,128)(2,1)S(1)} %add_convert_fusion.2), channel_id=1, source_target_pairs={{0,128},{32,160},{64,192},{96,224},{128,0},{160,32},{192,64},{224,... | collective-permute-start | bytes 221192 | tf_op jit(solution)/shard_map/ppermute | solution.py:240
  96.3 2.1 %collective-permute-start.15 = (bf16[288,128]{1,0:T(8,128)(2,1)S(1)}, bf16[288,128]{1,0:T(8,128)(2,1)S(1)}, u32[]{:S(2)}, u32[]{:S(2)}) collective-permute-start(bf16[288,128]{1,0:T(8,128)(2,1)S(1)} %add_convert_fusion.2), channel_id=1, source_target_pairs={{0,64},{32,96},{64,128},{96,160},{128,192},{160,224},{192,0},{224,... | collective-permute-start | bytes 221192 | tf_op jit(solution)/shard_map/ppermute | solution.py:240
  98.4 1.8 %collective-permute-done.16 = bf16[288,128]{1,0:T(8,128)(2,1)S(1)} collective-permute-done((bf16[288,128]{1,0:T(8,128)(2,1)S(1)}, bf16[288,128]{1,0:T(8,128)(2,1)S(1)}, u32[]{:S(2)}, u32[]{:S(2)}) %collective-permute-start.16) | collective-permute-done | bytes 73760 | tf_op jit(solution)/shard_map/ppermute | solution.py:240
  100.3 2.1 %collective-permute-done.15 = bf16[288,128]{1,0:T(8,128)(2,1)S(1)} collective-permute-done((bf16[288,128]{1,0:T(8,128)(2,1)S(1)}, bf16[288,128]{1,0:T(8,128)(2,1)S(1)}, u32[]{:S(2)}, u32[]{:S(2)}) %collective-permute-start.15) | collective-permute-done | bytes 73760 | tf_op jit(solution)/shard_map/ppermute | solution.py:240
  105.3 2.0 %collective-permute-done.20.refs_3_ = bf16[288,128]{1,0:T(8,128)(2,1)S(1)} collective-permute-done((bf16[288,128]{1,0:T(8,128)(2,1)S(1)}, bf16[288,128]{1,0:T(8,128)(2,1)S(1)}, u32[]{:S(2)}, u32[]{:S(2)}) %collective-permute-start.20) | collective-permute-done | bytes 73760 | tf_op jit(solution)/shard_map/ppermute | solution.py:225
  112.2 2.5 %collective-permute-start.22 = (bf16[1152,128]{1,0:T(8,128)(2,1)}, bf16[1152,128]{1,0:T(8,128)(2,1)S(1)}, u32[]{:S(2)}, u32[]{:S(2)}) collective-permute-start(bf16[1152,128]{1,0:T(8,128)(2,1)} %place_rows.1.refs_0_), channel_id=1, source_target_pairs={{0,6},{1,7},{2,0},{3,1},{4,2},{5,3},{6,4},{7,5},{8,14},{9,15},{10,... | collective-permute-start | bytes 884744 | tf_op jit(solution)/shard_map/ppermute | solution.py:225
  115.3 3.0 %collective-permute-done.23.refs_3_ = bf16[1152,128]{1,0:T(8,128)(2,1)S(1)} collective-permute-done((bf16[1152,128]{1,0:T(8,128)(2,1)}, bf16[1152,128]{1,0:T(8,128)(2,1)S(1)}, u32[]{:S(2)}, u32[]{:S(2)}) %collective-permute-start.23) | collective-permute-done | bytes 294944 | tf_op jit(solution)/shard_map/ppermute | solution.py:225
  118.3 5.1 %collective-permute-done.22.refs_2_ = bf16[1152,128]{1,0:T(8,128)(2,1)S(1)} collective-permute-done((bf16[1152,128]{1,0:T(8,128)(2,1)}, bf16[1152,128]{1,0:T(8,128)(2,1)S(1)}, u32[]{:S(2)}, u32[]{:S(2)}) %collective-permute-start.22) | collective-permute-done | bytes 294944 | tf_op jit(solution)/shard_map/ppermute | solution.py:225
  124.3 2.4 %place_columns.1.refs_1_ = bf16[4,1152,128]{2,1,0:T(8,128)(2,1)} custom-call(s32[1]{0:T(128)} %bitcast.12.pos, bf16[1152,128]{1,0:T(8,128)(2,1)} %place_rows.1.refs_0_, bf16[1152,128]{1,0:T(8,128)(2,1)} %copy-done.11, bf16[1152,128]{1,0:T(8,128)(2,1)} %copy-done.10, bf16[1152,128]{1,0:T(8,128)(2,1)} %copy-done.9), custom_call_target="tpu_custom_call" | custom-call | tf_op jit(solution)/shard_map/place_columns/pallas_call | solution.py:173
  126.6 8.4 %collective-permute-start.24 = (bf16[4,1152,128]{2,1,0:T(8,128)(2,1)}, bf16[4,1152,128]{2,1,0:T(8,128)(2,1)S(1)}, u32[]{:S(2)}, u32[]{:S(2)}) collective-permute-start(bf16[4,1152,128]{2,1,0:T(8,128)(2,1)} %place_columns.1.refs_1_), channel_id=1, source_target_pairs={{0,1},{1,0},{2,3},{3,2},{4,5},{5,4},{6,7},{7,6},{8,9},{9,8},{10,11... | collective-permute-start | bytes 3538952 | tf_op jit(solution)/shard_map/ppermute | solution.py:225
  138.7 4.3 %finish.1 = (f32[1024,512]{1,0:T(8,128)}, f32[1024,512]{1,0:T(8,128)}, f32[512,128]{1,0:T(8,128)}, f32[1,512]{1,0:T(1,128)}, f32[1,128]{1,0:T(1,128)}) custom-call(s32[1]{0:T(128)} %bitcast.11.refs_0_, bf16[4,1152,128]{2,1,0:T(8,128)(2,1)} %place_columns.1.refs_1_, bf16[4,1152,128]{2,1,0:T(8,128)(2,1)} %copy-done.3), custom_call_target="tpu_custom_call" | custom-call | tf_op jit(solution)/shard_map/finish/pallas_call | solution.py:330
  (137 shorter events, 46.0 us)
Async XLA Ops:
  3.1 18.9 %collective-permute-start.1 = (bf16[80,512]{1,0:T(8,128)(2,1)S(1)}, bf16[80,512]{1,0:T(8,128)(2,1)}, u32[]{:S(2)}, u32[]{:S(2)}) collective-permute-start(bf16[80,512]{1,0:T(8,128)(2,1)S(1)} %fusion.10.right_m), channel_id=1, source_target_pairs={{0,1},{1,0},{2,3},{3,2},{4,5},{5,4},{6,7},{7,6},{8,9},{9,8},{10,11... | collective-permute-start | bytes 245768 | tf_op jit(solution)/shard_map/ppermute | solution.py:225
  6.4 16.3 %collective-permute-start = (bf16[80,512]{1,0:T(8,128)(2,1)S(1)}, bf16[80,512]{1,0:T(8,128)(2,1)}, u32[]{:S(2)}, u32[]{:S(2)}) collective-permute-start(bf16[80,512]{1,0:T(8,128)(2,1)S(1)} %fusion.10.right_m), channel_id=1, source_target_pairs={{0,31},{1,2},{2,1},{3,4},{4,3},{5,6},{6,5},{7,8},{8,7},{9,10},{10,... | collective-permute-start | bytes 245768 | tf_op jit(solution)/shard_map/ppermute | solution.py:225
  6.4 19.5 %collective-permute-start.4 = (bf16[64,1024]{1,0:T(8,128)(2,1)S(1)}, bf16[64,1024]{1,0:T(8,128)(2,1)S(1)}, u32[]{:S(2)}, u32[]{:S(2)}) collective-permute-start(bf16[64,1024]{1,0:T(8,128)(2,1)S(1)} %bitcast.47), channel_id=1, source_target_pairs={{0,1},{1,0},{2,3},{3,2},{4,5},{5,4},{6,7},{7,6},{8,9},{9,8},{10,11... | collective-permute-start | bytes 393224 | tf_op jit(solution)/shard_map/ppermute | solution.py:225
  12.3 21.5 %all-to-all-start = ((bf16[32,3,4224]{2,1,0:T(4,128)(2,1)}), bf16[32,3,4224]{2,1,0:T(4,128)(2,1)S(1)}, u32[]{:S(2)}, u32[]{:S(2)}) async-start(bf16[32,3,4224]{2,1,0:T(4,128)(2,1)} %all_to_all.7), calls=%async_computation | async-start | bytes 2162688 | tf_op jit(solution)/shard_map/all_to_all | solution.py:251
  26.6 34.4 %collective-permute-start.7 = (bf16[128,1024]{1,0:T(8,128)(2,1)}, bf16[128,1024]{1,0:T(8,128)(2,1)}, u32[]{:S(2)}, u32[]{:S(2)}) collective-permute-start(bf16[128,1024]{1,0:T(8,128)(2,1)} %pad_maximum_fusion.1), channel_id=1, source_target_pairs={{0,4},{1,5},{2,6},{3,7},{4,0},{5,1},{6,2},{7,3},{8,12},{9,13},{10,... | collective-permute-start | bytes 786440 | tf_op jit(solution)/shard_map/ppermute | solution.py:225
  29.3 30.7 %collective-permute-start.6 = (bf16[128,1024]{1,0:T(8,128)(2,1)}, bf16[128,1024]{1,0:T(8,128)(2,1)}, u32[]{:S(2)}, u32[]{:S(2)}) collective-permute-start(bf16[128,1024]{1,0:T(8,128)(2,1)} %pad_maximum_fusion.1), channel_id=1, source_target_pairs={{0,6},{1,7},{2,0},{3,1},{4,2},{5,3},{6,4},{7,5},{8,14},{9,15},{10,... | collective-permute-start | bytes 786440 | tf_op jit(solution)/shard_map/ppermute | solution.py:225
  30.2 28.8 %collective-permute-start.5 = (bf16[128,1024]{1,0:T(8,128)(2,1)}, bf16[128,1024]{1,0:T(8,128)(2,1)}, u32[]{:S(2)}, u32[]{:S(2)}) collective-permute-start(bf16[128,1024]{1,0:T(8,128)(2,1)} %pad_maximum_fusion.1), channel_id=1, source_target_pairs={{0,2},{1,3},{2,4},{3,5},{4,6},{5,7},{6,0},{7,1},{8,10},{9,11},{10,... | collective-permute-start | bytes 786440 | tf_op jit(solution)/shard_map/ppermute | solution.py:225
  53.1 4.0 %collective-permute-start.2 = (bf16[64,512]{1,0:T(8,128)(2,1)}, bf16[64,512]{1,0:T(8,128)(2,1)S(1)}, u32[]{:S(2)}, u32[]{:S(2)}) collective-permute-start(bf16[64,512]{1,0:T(8,128)(2,1)} %get-tuple-element.19), channel_id=1, source_target_pairs={{0,31},{1,2},{2,1},{3,4},{4,3},{5,6},{6,5},{7,8},{8,7},{9,10},{10,... | collective-permute-start | bytes 196616 | tf_op jit(solution)/shard_map/ppermute | solution.py:225
  62.2 4.4 %collective-permute-start.8 = (bf16[256,128]{1,0:T(8,128)(2,1)S(1)}, bf16[256,128]{1,0:T(8,128)(2,1)S(1)}, u32[]{:S(2)}, u32[]{:S(2)}) collective-permute-start(bf16[256,128]{1,0:T(8,128)(2,1)S(1)} %get-tuple-element.31), channel_id=1, source_target_pairs={{0,2},{1,3},{2,4},{3,5},{4,6},{5,7},{6,0},{7,1},{8,10},{9,11},{10,... | collective-permute-start | bytes 196616 | tf_op jit(solution)/shard_map/ppermute | solution.py:225
  63.6 4.7 %collective-permute-start.10 = (bf16[256,128]{1,0:T(8,128)(2,1)S(1)}, bf16[256,128]{1,0:T(8,128)(2,1)S(1)}, u32[]{:S(2)}, u32[]{:S(2)}) collective-permute-start(bf16[256,128]{1,0:T(8,128)(2,1)S(1)} %get-tuple-element.32), channel_id=1, source_target_pairs={{0,4},{1,5},{2,6},{3,7},{4,0},{5,1},{6,2},{7,3},{8,12},{9,13},{10,... | collective-permute-start | bytes 196616 | tf_op jit(solution)/shard_map/ppermute | solution.py:225
  64.8 3.6 %collective-permute-start.9 = (bf16[256,128]{1,0:T(8,128)(2,1)S(1)}, bf16[256,128]{1,0:T(8,128)(2,1)S(1)}, u32[]{:S(2)}, u32[]{:S(2)}) collective-permute-start(bf16[256,128]{1,0:T(8,128)(2,1)S(1)} %get-tuple-element.33), channel_id=1, source_target_pairs={{0,6},{1,7},{2,0},{3,1},{4,2},{5,3},{6,4},{7,5},{8,14},{9,15},{10,... | collective-permute-start | bytes 196616 | tf_op jit(solution)/shard_map/ppermute | solution.py:225
  69.6 12.1 %collective-permute-start.11 = (bf16[288,128]{1,0:T(8,128)(2,1)S(1)}, bf16[288,128]{1,0:T(8,128)(2,1)S(1)}, u32[]{:S(2)}, u32[]{:S(2)}) collective-permute-start(bf16[288,128]{1,0:T(8,128)(2,1)S(1)} %get-tuple-element.28), channel_id=1, source_target_pairs={{0,8},{1,9},{2,10},{3,11},{4,12},{5,13},{6,14},{7,15},{8,16},{9,17... | collective-permute-start | bytes 221192 | tf_op jit(solution)/shard_map/ppermute | solution.py:225
  76.2 5.7 %collective-permute-start.12 = (bf16[288,128]{1,0:T(8,128)(2,1)S(1)}, bf16[288,128]{1,0:T(8,128)(2,1)S(1)}, u32[]{:S(2)}, u32[]{:S(2)}) collective-permute-start(bf16[288,128]{1,0:T(8,128)(2,1)S(1)} %get-tuple-element.29), channel_id=1, source_target_pairs={{0,24},{1,25},{2,26},{3,27},{4,28},{5,29},{6,30},{7,31},{8,0},{9,1... | collective-permute-start | bytes 221192 | tf_op jit(solution)/shard_map/ppermute | solution.py:225
  78.8 5.0 %collective-permute-start.13 = (bf16[288,128]{1,0:T(8,128)(2,1)S(1)}, bf16[288,128]{1,0:T(8,128)(2,1)S(1)}, u32[]{:S(2)}, u32[]{:S(2)}) collective-permute-start(bf16[288,128]{1,0:T(8,128)(2,1)S(1)} %get-tuple-element.30), channel_id=1, source_target_pairs={{0,16},{1,17},{2,18},{3,19},{4,20},{5,21},{6,22},{7,23},{8,24},{9,... | collective-permute-start | bytes 221192 | tf_op jit(solution)/shard_map/ppermute | solution.py:225
  83.9 6.1 %collective-permute-start.14 = (bf16[288,128]{1,0:T(8,128)(2,1)S(1)}, bf16[288,128]{1,0:T(8,128)(2,1)S(1)}, u32[]{:S(2)}, u32[]{:S(2)}) collective-permute-start(bf16[288,128]{1,0:T(8,128)(2,1)S(1)} %add_convert_fusion.3), channel_id=1, source_target_pairs={{0,32},{32,0},{64,96},{96,64},{128,160},{160,128},{192,224},{224,1... | collective-permute-start | bytes 221192 | tf_op jit(solution)/shard_map/ppermute | solution.py:316
  90.0 8.4 %collective-permute-start.17 = (bf16[288,128]{1,0:T(8,128)(2,1)S(1)}, bf16[288,128]{1,0:T(8,128)(2,1)S(1)}, u32[]{:S(2)}, u32[]{:S(2)}) collective-permute-start(bf16[288,128]{1,0:T(8,128)(2,1)S(1)} %add_convert_fusion.2), channel_id=1, source_target_pairs={{0,128},{32,160},{64,192},{96,224},{128,0},{160,32},{192,64},{224,... | collective-permute-start | bytes 221192 | tf_op jit(solution)/shard_map/ppermute | solution.py:240
  96.1 4.2 %collective-permute-start.16 = (bf16[288,128]{1,0:T(8,128)(2,1)S(1)}, bf16[288,128]{1,0:T(8,128)(2,1)S(1)}, u32[]{:S(2)}, u32[]{:S(2)}) collective-permute-start(bf16[288,128]{1,0:T(8,128)(2,1)S(1)} %add_convert_fusion.2), channel_id=1, source_target_pairs={{0,192},{32,224},{64,0},{96,32},{128,64},{160,96},{192,128},{224,1... | collective-permute-start | bytes 221192 | tf_op jit(solution)/shard_map/ppermute | solution.py:240
  96.3 6.0 %collective-permute-start.15 = (bf16[288,128]{1,0:T(8,128)(2,1)S(1)}, bf16[288,128]{1,0:T(8,128)(2,1)S(1)}, u32[]{:S(2)}, u32[]{:S(2)}) collective-permute-start(bf16[288,128]{1,0:T(8,128)(2,1)S(1)} %add_convert_fusion.2), channel_id=1, source_target_pairs={{0,64},{32,96},{64,128},{96,160},{128,192},{160,224},{192,0},{224,... | collective-permute-start | bytes 221192 | tf_op jit(solution)/shard_map/ppermute | solution.py:240
  102.4 4.8 %collective-permute-start.20 = (bf16[288,128]{1,0:T(8,128)(2,1)S(1)}, bf16[288,128]{1,0:T(8,128)(2,1)S(1)}, u32[]{:S(2)}, u32[]{:S(2)}) collective-permute-start(bf16[288,128]{1,0:T(8,128)(2,1)S(1)} %add_convert_fusion.1.refs_0_), channel_id=1, source_target_pairs={{0,16},{1,17},{2,18},{3,19},{4,20},{5,21},{6,22},{7,23},{8,24},{9,... | collective-permute-start | bytes 221192 | tf_op jit(solution)/shard_map/ppermute | solution.py:225
  103.9 4.7 %collective-permute-start.18 = (bf16[288,128]{1,0:T(8,128)(2,1)S(1)}, bf16[288,128]{1,0:T(8,128)(2,1)S(1)}, u32[]{:S(2)}, u32[]{:S(2)}) collective-permute-start(bf16[288,128]{1,0:T(8,128)(2,1)S(1)} %add_convert_fusion.1.refs_0_), channel_id=1, source_target_pairs={{0,8},{1,9},{2,10},{3,11},{4,12},{5,13},{6,14},{7,15},{8,16},{9,17... | collective-permute-start | bytes 221192 | tf_op jit(solution)/shard_map/ppermute | solution.py:225
  111.0 7.3 %collective-permute-start.23 = (bf16[1152,128]{1,0:T(8,128)(2,1)}, bf16[1152,128]{1,0:T(8,128)(2,1)S(1)}, u32[]{:S(2)}, u32[]{:S(2)}) collective-permute-start(bf16[1152,128]{1,0:T(8,128)(2,1)} %place_rows.1.refs_0_), channel_id=1, source_target_pairs={{0,4},{1,5},{2,6},{3,7},{4,0},{5,1},{6,2},{7,3},{8,12},{9,13},{10,... | collective-permute-start | bytes 884744 | tf_op jit(solution)/shard_map/ppermute | solution.py:225
  112.2 11.2 %collective-permute-start.22 = (bf16[1152,128]{1,0:T(8,128)(2,1)}, bf16[1152,128]{1,0:T(8,128)(2,1)S(1)}, u32[]{:S(2)}, u32[]{:S(2)}) collective-permute-start(bf16[1152,128]{1,0:T(8,128)(2,1)} %place_rows.1.refs_0_), channel_id=1, source_target_pairs={{0,6},{1,7},{2,0},{3,1},{4,2},{5,3},{6,4},{7,5},{8,14},{9,15},{10,... | collective-permute-start | bytes 884744 | tf_op jit(solution)/shard_map/ppermute | solution.py:225
  114.7 8.7 %collective-permute-start.21 = (bf16[1152,128]{1,0:T(8,128)(2,1)}, bf16[1152,128]{1,0:T(8,128)(2,1)S(1)}, u32[]{:S(2)}, u32[]{:S(2)}) collective-permute-start(bf16[1152,128]{1,0:T(8,128)(2,1)} %place_rows.1.refs_0_), channel_id=1, source_target_pairs={{0,2},{1,3},{2,4},{3,5},{4,6},{5,7},{6,0},{7,1},{8,10},{9,11},{10,... | collective-permute-start | bytes 884744 | tf_op jit(solution)/shard_map/ppermute | solution.py:225
  126.6 11.1 %collective-permute-start.24 = (bf16[4,1152,128]{2,1,0:T(8,128)(2,1)}, bf16[4,1152,128]{2,1,0:T(8,128)(2,1)S(1)}, u32[]{:S(2)}, u32[]{:S(2)}) collective-permute-start(bf16[4,1152,128]{2,1,0:T(8,128)(2,1)} %place_columns.1.refs_1_), channel_id=1, source_target_pairs={{0,1},{1,0},{2,3},{3,2},{4,5},{5,4},{6,7},{7,6},{8,9},{9,8},{10,11... | collective-permute-start | bytes 3538952 | tf_op jit(solution)/shard_map/ppermute | solution.py:225
  (27 other events, 135.2 us)

commit v2 on v1

v2 whole, which is shorter than its diff:
```python
import math

import jax
import jax.numpy as jnp
from jax import lax
from jax.experimental import pallas as pl
from jax.experimental.pallas import tpu as pltpu
from jax.sharding import PartitionSpec as P

PANEL = 64
B_DEV = 8
ROWS = 8
CHUNK = 256
BF = jnp.bfloat16
F32 = jnp.float32


def forward(tile_at, left_s, right_s, hid_s, slope_s, rows=range(ROWS)):
    k = tile_at // 8
    left8 = left_s[pl.ds(pl.multiple_of(tile_at % 8 * ROWS, ROWS), ROWS), :]
    right = right_s[pl.ds(pl.multiple_of(k * PANEL, PANEL), PANEL), :]
    for a in rows:
        part = slice(a * PANEL, (a + 1) * PANEL)
        u = right.astype(BF) + jnp.broadcast_to(left8[a : a + 1, :], right.shape).astype(BF)
        p = jnp.tanh(u) + BF(1.0)
        h = u * p
        hid_s[part, :] = h
        slope_s[part, :] = p + h * (BF(2.0) - p)


def backward(
    tile_at, hid_s, slope_s, tsum_s, mask_s, half_s, wmt_ref, wf_ref, lacc, racc, mid_acc, fin_acc
):
    col0 = pl.multiple_of(tile_at // 8 * PANEL, PANEL)
    row0 = pl.multiple_of(tile_at % 8 * ROWS, ROWS)
    wf = wf_ref[...]
    count = tsum_s[tile_at // 8 * 8 + 24, 0:1, 0:CHUNK]
    parts = [slice(c * CHUNK, (c + 1) * CHUNK) for c in range(ROWS * PANEL // CHUNK)]
    pre = [
        jnp.dot(hid_s[part, :], half_s[...], preferred_element_type=F32).T
        for part in parts
    ]
    terms, hiddens, fins = [], [], []
    for part, u in zip(parts, pre):
        p = jnp.tanh(u) + 1.0
        act = u * p
        predicted = jnp.sum(act * wf, axis=0, keepdims=True)
        pair_slope = (16.0 * mask_s[tile_at, 0:1, part]) * (count * predicted - tsum_s[tile_at, 0:1, part])
        grad_second = ((0.5 * pair_slope) * wf * (p + act * (2.0 - p))).astype(BF)
        fin = act * pair_slope
        fins.append(sum(fin[:, j * 128 : (j + 1) * 128] for j in range(CHUNK // 128)))
        hiddens.append(
            lax.dot_general(grad_second, wmt_ref[...], (((0,), (0,)), ((), ())), preferred_element_type=F32)
        )
        terms.append(jnp.dot(grad_second, hid_s[part, :], preferred_element_type=F32))
    fin_acc[...] += sum(fins)
    cols, rows = None, []
    for part, grad_hidden in zip(parts, hiddens):
        for a in range(CHUNK // PANEL):
            at = slice(part.start + a * PANEL, part.start + (a + 1) * PANEL)
            g = grad_hidden[a * PANEL : (a + 1) * PANEL, :] * slope_s[at, :].astype(F32)
            rows.append(jnp.sum(g, axis=0, keepdims=True))
            cols = g if cols is None else cols + g
    mid_acc[...] += sum(terms)
    racc[pl.ds(col0, PANEL), :] += cols
    lacc[pl.ds(row0, ROWS), :] += jnp.concatenate(rows, axis=0)


def pair_kernel(
    core,
    ids_s,
    ids_ref,
    left_ref,
    right_o,
    right_m,
    right_p,
    targets_ref,
    bias_ref,
    wmt_ref,
    wf_ref,
    out_left,
    out_outer,
    out_own,
    out_keep,
    out_sent,
    todo,
    left_s,
    right_s,
    tsum_s,
    mask_s,
    half_s,
    hid_s,
    slope_s,
    lacc,
    racc,
    mid_acc,
    fin_acc,
):
    hidden = left_ref.shape[1]
    tile = ROWS * PANEL
    iota = lambda shape, axis: lax.broadcasted_iota(jnp.int32, shape, axis)
    def scan(i, n):
        k, rt = i // 8, i % 8
        meets = (ids_s[1, rt * ROWS] <= ids_s[k, PANEL - 1]) & (ids_s[k, 0] <= ids_s[1, rt * ROWS + ROWS - 1])
        todo[n] = i
        return n + meets.astype(jnp.int32)

    n_todo = lax.fori_loop(0, 24, scan, 0)
    for extra in range(3):
        todo[n_todo + extra] = 24
    left_s[...] = (left_ref[...].astype(F32) + bias_ref[...]) * 0.5
    for k, ref in enumerate((right_o, right_m, right_p)):
        right_s[k * PANEL : (k + 1) * PANEL, :] = ref[0:PANEL, :].astype(F32) * 0.5
    right_s[3 * PANEL :, :] = jnp.zeros((PANEL, hidden), F32)
    half_s[...] = (wmt_ref[...].astype(F32) * 0.5).T.astype(BF)
    n_src = targets_ref.shape[0]
    tsum = jnp.dot(
        (iota((24, n_src), 1) % 24 == iota((24, n_src), 0)).astype(BF), targets_ref[...], preferred_element_type=F32
    )
    ids = ids_ref[...]
    spread = (iota((PANEL, tile), 0) % ROWS == iota((PANEL, tile), 1) // PANEL).astype(BF)
    repeat = (iota((PANEL, tile), 0) == iota((PANEL, tile), 1) % PANEL).astype(BF)
    row_ids = jnp.where(iota((8, PANEL), 1) // ROWS == iota((8, PANEL), 0), ids[1:2, :], 0.0)
    row_ids = jnp.dot(row_ids.astype(BF), spread, preferred_element_type=F32)
    col_ids = jnp.dot(ids.astype(BF), repeat, preferred_element_type=F32)
    lane = iota((8, tile), 1)
    itself = iota((8, tile), 0) * ROWS + lane // PANEL == lane % PANEL
    for k in range(3):
        same = row_ids == col_ids[k : k + 1, :]
        mask = jnp.where(same & ~itself if k == 1 else same, 1.0, 0.0)
        count = jnp.max(
            jnp.where(iota((8, tile), 1) == k * (PANEL + 1), tsum[8:16, :], 0.0)[0:1], axis=1, keepdims=True
        )
        tsum_s[24 + 8 * k, 0:1, :] = jnp.broadcast_to(count, (1, tile))
        for rt in range(8):
            mask_s[k * 8 + rt, 0:1, :] = mask[rt : rt + 1, :]
            tsum_s[k * 8 + rt, 0:1, :] = tsum[k * 8 + rt : k * 8 + rt + 1, :]
    mask_s[24, 0:1, :] = jnp.zeros((1, tile), F32)
    tsum_s[48, 0:1, :] = jnp.zeros((1, tile), F32)
    lacc[...] = jnp.zeros_like(lacc)
    racc[...] = jnp.zeros_like(racc)
    mid_acc[...] = jnp.zeros_like(mid_acc)
    fin_acc[...] = jnp.zeros_like(fin_acc)
    rest = (tsum_s, mask_s, half_s, wmt_ref, wf_ref, lacc, racc, mid_acc, fin_acc)
    def step(i, carry):
        forward(todo[i], left_s, right_s, hid_s, slope_s)
        backward(todo[i], hid_s, slope_s, *rest)
        return carry

    lax.fori_loop(0, n_todo, step, 0)
    left = lacc[...] * 0.5
    out_left[...] = left.astype(BF)
    outer, own, partner = [
        (racc[k * PANEL : (k + 1) * PANEL, :] * 0.5).astype(BF) for k in range(3)
    ]
    out_outer[...] = outer
    out_own[...] = own
    out_sent[PANEL : 2 * PANEL, :] = partner

    def middle(ref, start):
        for j in range(hidden // 128):
            block = slice(j * 128, (j + 1) * 128)
            ref[start : start + 128, block] = mid_acc[:, block].T.astype(BF)

    def small(ref, start):
        ref[start : start + 128, :] = jnp.zeros((128, hidden), BF)
        ref[start : start + 1, :] = jnp.sum(left, axis=0, keepdims=True).astype(BF)
        ref[start + 16 : start + 17, 0:128] = jnp.sum(fin_acc[...].T, axis=0, keepdims=True).astype(BF)

    @pl.when(core[0] == 0)
    def _():
        out_sent[0:PANEL, :] = own
        small(out_sent, 2 * PANEL)
        middle(out_keep, 0)

    @pl.when(core[0] != 0)
    def _():
        out_sent[0:PANEL, :] = left.astype(BF)
        middle(out_sent, 2 * PANEL)
        small(out_keep, 0)


def pair_grads(core, ids_s, ids, left, right_o, right_m, right_p, targets, bias, wmt, wf):
    hidden = left.shape[1]
    upper = wmt.shape[0]
    tile = ROWS * PANEL
    vmem = pl.BlockSpec(memory_space=pltpu.VMEM)
    panel = jax.ShapeDtypeStruct((PANEL, hidden), BF)
    return pl.pallas_call(
        pair_kernel,
        out_shape=(
            panel,
            panel,
            panel,
            jax.ShapeDtypeStruct((upper, hidden), BF),
            jax.ShapeDtypeStruct((2 * PANEL + upper, hidden), BF),
        ),
        in_specs=[pl.BlockSpec(memory_space=pltpu.SMEM)] * 2 + [vmem] * 9,
        out_specs=(vmem,) * 5,
        scratch_shapes=[
            pltpu.SMEM((32,), jnp.int32),
            pltpu.VMEM((PANEL, hidden), F32),
            pltpu.VMEM((4 * PANEL, hidden), F32),
            pltpu.VMEM((49, 8, tile), F32),
            pltpu.VMEM((25, 8, tile), F32),
            pltpu.VMEM((hidden, upper), BF),
            pltpu.VMEM((tile, hidden), BF),
            pltpu.VMEM((tile, hidden), BF),
            pltpu.VMEM((PANEL, hidden), F32),
            pltpu.VMEM((4 * PANEL, hidden), F32),
            pltpu.VMEM((upper, hidden), F32),
            pltpu.VMEM((upper, 128), F32),
        ],
        compiler_params=pltpu.CompilerParams(vmem_limit_bytes=24 << 20),
        cost_estimate=pl.CostEstimate(
            flops=10 * 24 * tile * hidden * upper, bytes_accessed=2 << 20, transcendentals=24 * tile * hidden
        ),
        name="pair_grads",
    )(core, ids_s, ids, left, right_o, right_m, right_p, targets, bias, wmt, wf)


def send_kernel(blocks, live, targets_ref, out_ref, acc):
    tile = out_ref.shape[1]
    acc[...] = jnp.zeros_like(acc)
    lane = lax.broadcasted_iota(jnp.int32, (1, tile), 1)
    counters = (lane == 0) | (lane == PANEL + 1) | (lane == 2 * (PANEL + 1))

    def slot(i, carry):
        row = blocks[i, 0]
        step = blocks[i, 1] - row
        side = jnp.where((row & 1) == 0, step, -step) + 1
        to = row * 3 + side
        for rt in range(8):
            value = targets_ref[pl.ds(i, 1), rt * tile : (rt + 1) * tile]
            if rt == 0:
                value = jnp.where(counters & (side == 1), 0.0, value)
            acc[to, rt : rt + 1, :] += value
        acc[row * 3 + 1, 0:1, :] += jnp.where(lane == side * (PANEL + 1), 1.0, 0.0)
        return carry

    lax.fori_loop(0, live[0, 0], slot, 0)
    for p in range(acc.shape[0]):
        out_ref[p * 8 : (p + 1) * 8, :] = acc[p].astype(BF)


def send_targets(blocks, live, targets, panels):
    tile = ROWS * PANEL
    smem = pl.BlockSpec(memory_space=pltpu.SMEM)
    vmem = pl.BlockSpec(memory_space=pltpu.VMEM)
    return pl.pallas_call(
        send_kernel,
        out_shape=jax.ShapeDtypeStruct((24 * panels, tile), BF),
        in_specs=[smem, smem, vmem],
        out_specs=vmem,
        scratch_shapes=[pltpu.VMEM((3 * panels, 8, tile), F32)],
        compiler_params=pltpu.CompilerParams(vmem_limit_bytes=8 << 20),
        name="send_targets",
    )(blocks, live, targets)


ORDER = (0, 1, 3, 2)


def finish_kernel(scale, pos, *refs):
    pieces, (left_ref, right_ref, mid_ref, bias_ref, fin_ref, whole) = refs[:8], refs[8:]
    part = whole.shape[2] // 4
    depth = whole.shape[2] - 128
    block = left_ref.shape[0]

    @pl.when(pl.program_id(0) == 0)
    def _():
        for n, ref in enumerate(pieces):
            side = pos[0] if n < 4 else 1 - pos[0]
            column = lax.rem(pos[1] - ORDER[n % 4] + 4, 4)
            for m, dy in enumerate(ORDER):
                row = pl.multiple_of(lax.rem(pos[2] - dy + 4, 4) * part, 32)
                whole[side, column, pl.ds(row, part), :] = ref[m * part : (m + 1) * part, :]
        for j in range(4):
            lanes = slice(j * 128, (j + 1) * 128)
            mid_ref[lanes, :] = whole[0, j, depth : depth + 128, :].astype(F32) * scale
            bias_ref[:, lanes] = whole[1, j, depth : depth + 1, :].astype(F32) * scale
        fin_ref[...] = whole[1, 0, depth + 16 : depth + 17, :].astype(F32) * scale

    rows = pl.ds(pl.multiple_of(pl.program_id(0) * block, block), block)
    for j in range(4):
        lanes = slice(j * 128, (j + 1) * 128)
        left_ref[:, lanes] = whole[0, j, rows, :].astype(F32) * scale
        right_ref[:, lanes] = whole[1, j, rows, :].astype(F32) * scale


def local(
    embeddings,
    cluster_ids,
    block_list,
    block_counts,
    pair_targets,
    w_left,
    w_right,
    hidden_bias,
    w_middle,
    w_final,
):
    emb = embeddings[0]
    depth = emb.shape[1]
    hidden = w_left.shape[1]
    upper = w_middle.shape[1]
    panels = lax.axis_size("blk")
    groups = lax.axis_size("grp")
    me = lax.axis_index("blk")
    core, x, y = me & 1, (me >> 1) & 3, me >> 3

    def blk(value, partner):
        return lax.ppermute(value, "blk", [(i, partner(i)) for i in range(panels)])

    def on_core(value):
        return blk(value, lambda i: i ^ 1)

    def on_outer(value):
        return blk(value, lambda i: (i - 1 if i % 2 == 0 else i + 1) % panels)

    def on_x(value, d):
        return blk(value, lambda i: i // 8 * 8 + (i // 2 % 4 + d) % 4 * 2 + i % 2)

    def on_y(value, d):
        return blk(value, lambda i: (i // 8 + d) % 4 * 8 + i % 8)

    def on_z(value, d):
        return lax.ppermute(value, "grp", [(i, (i + d) % groups) for i in range(groups)])

    sums = send_targets(block_list[0], block_counts, pair_targets[0], panels).reshape(panels, 24, ROWS * PANEL)
    sums, emb, ids = lax.optimization_barrier((sums, emb, cluster_ids[0]))
    with jax.named_scope("to_owner"):
        targets = lax.all_to_all(sums, "blk", 0, 0, tiled=True)
    targets = targets.reshape(24 * panels, ROWS * PANEL)

    left = jnp.dot(emb, w_left, preferred_element_type=F32).astype(BF)
    right = jnp.dot(emb, w_right, preferred_element_type=F32).astype(BF)
    ids = ids.astype(BF)
    ids_row = jnp.pad(ids[None, :], ((0, 15), (0, hidden - PANEL)))
    right_own = jnp.concatenate([right, ids_row], axis=0)
    right_outer = on_outer(right_own)
    right_partner = on_core(right_own)
    col_ids = jnp.stack([right_outer[PANEL, :PANEL], ids, right_partner[PANEL, :PANEL]])
    lg, r_outer, r_own, keep, sent = pair_grads(
        core[None],
        col_ids.astype(jnp.int32),
        jnp.pad(col_ids.astype(F32), ((0, 5), (0, 0))),
        left,
        right_outer,
        right_own,
        right_partner,
        targets,
        hidden_bias[None, :],
        w_middle.T,
        w_final[:, None],
    )

    emb_pair = jnp.concatenate([emb, on_core(emb)], axis=0)
    emb_all = jnp.concatenate([emb_pair] + [on_x(emb_pair, d) for d in ORDER[1:]], axis=0)

    first = core == 0
    got = on_core(sent)
    outer = on_outer(r_outer).astype(F32)
    over = lax.ppermute(r_outer, "blk", [(i, (i + 2) % panels) for i in range(1, panels, 2)]).astype(F32)
    r_partner = sent[PANEL : 2 * PANEL].astype(F32)
    rg = (r_own.astype(F32) + got[PANEL : 2 * PANEL].astype(F32) + outer).astype(BF)
    pair_right = (got[:PANEL].astype(F32) + r_partner + over).astype(BF)
    extra = keep.astype(F32) + got[2 * PANEL :].astype(F32)
    both = jnp.concatenate(
        [jnp.where(first, lg, rg), jnp.where(first, got[:PANEL], pair_right), extra.astype(BF)], axis=0
    )
    grad_local = jnp.dot(lg, w_left.T, preferred_element_type=F32) + jnp.dot(
        rg, w_right.T, preferred_element_type=F32
    )

    def column(d):
        return lax.dynamic_slice_in_dim(both, ((x + d) & 3) * 128, 128, 1)

    parts = [column(0)] + [on_x(column(d), d) for d in ORDER[1:]]
    grads = jnp.concatenate([p[: 2 * PANEL] for p in parts], axis=0)
    weight = lax.dot_general(emb_all, grads, (((0,), (0,)), ((), ())), preferred_element_type=F32)
    extra = sum(p[2 * PANEL :].astype(F32) for p in parts)
    total = jnp.concatenate([weight, extra], axis=0).astype(BF)
    piece = total.shape[0] // 4

    def rows(d):
        return lax.dynamic_slice_in_dim(total, ((y + d) & 3) * piece, piece, 0)

    parts = [rows(0)] + [on_y(rows(d), d) for d in ORDER[1:]]
    total = sum(p.astype(F32) for p in parts).astype(BF)
    total = (
        total.astype(F32)
        + lax.ppermute(total, "grp", [(i, i ^ 1) for i in range(groups)]).astype(F32)
    ).astype(BF)
    total = sum(p.astype(F32) for p in [total] + [on_z(total, d) for d in (2, 6, 4)]).astype(BF)

    total = jnp.concatenate([total] + [on_y(total, d) for d in ORDER[1:]], axis=0)
    mine = [total] + [on_x(total, d) for d in ORDER[1:]]
    theirs = [on_core(p) for p in mine]
    devices = panels * groups
    scale = 1.0 / math.sqrt(devices * B_DEV * PANEL)
    vmem = pl.BlockSpec(memory_space=pltpu.VMEM)
    block = depth // 4
    grad_left, grad_right, grad_middle, grad_bias, grad_final = pl.pallas_call(
        lambda *refs: finish_kernel(scale, *refs),
        grid=(4,),
        out_shape=(
            jax.ShapeDtypeStruct((depth, hidden), F32),
            jax.ShapeDtypeStruct((depth, hidden), F32),
            jax.ShapeDtypeStruct((hidden, upper), F32),
            jax.ShapeDtypeStruct((1, hidden), F32),
            jax.ShapeDtypeStruct((1, upper), F32),
        ),
        in_specs=[pl.BlockSpec(memory_space=pltpu.SMEM)] + [vmem] * 8,
        out_specs=(
            pl.BlockSpec((block, hidden), lambda i: (i, 0)),
            pl.BlockSpec((block, hidden), lambda i: (i, 0)),
            pl.BlockSpec((hidden, upper), lambda i: (0, 0)),
            pl.BlockSpec((1, hidden), lambda i: (0, 0)),
            pl.BlockSpec((1, upper), lambda i: (0, 0)),
        ),
        scratch_shapes=[pltpu.VMEM((2, 4, 4 * piece, 128), BF)],
        compiler_params=pltpu.CompilerParams(vmem_limit_bytes=16 << 20),
        name="finish",
    )(jnp.stack([core, x, y]), *mine, *theirs)
    return (grad_local[None], grad_left, grad_right, grad_bias[0], grad_middle, grad_final[0])


def solution(mesh):
    return jax.shard_map(
        local,
        mesh=mesh,
        in_specs=(
            P("grp", "blk", None),
            P("grp", "blk"),
            P("grp", "blk", None),
            P("grp", "blk"),
            P("grp", "blk", None),
            P(),
            P(),
            P(),
            P(),
            P(),
        ),
        out_specs=(P("grp", "blk", None), P(), P(), P(), P(), P()),
        check_vma=False,
    )
```

time: 143 us -> 127 us (0.89)
  starting transfers between devices: 60.5 us -> 74.8 us
  Pallas kernels: 26.2 us -> 14.5 us
  local copies, waits for them, and re-layouts: 16.1 us -> 8.14 us
  other arithmetic: 6.98 us -> 1.13 us
  matrix products: 5.38 us -> 2.66 us
  waiting for transfers between devices: 26 us -> 23.5 us
    pallas_call x4 -> x3, Pallas kernels: 26.2 us -> 14.5 us  [the longest x1 9.29 us: pair_grads(): pl.pallas_call(pair_kernel, out_shape=(panel, panel, panel, jax.ShapeDtyp...]
    ppermute x21 -> x24, waiting for transfers between devices: 18 us -> 12.7 us  [blk(): return lax.ppermute(value, 'blk', [(i, partner(i)) for i in range(panels)])]
    ppermute x0 -> x1, waiting for transfers between devices: none -> 4.81 us  [local(): lax.ppermute(r_outer, 'blk', [(i, (i + 2) % panels) for i in range(1, pan...]
    all_to_all x1, starting transfers between devices: 3.85 us -> 8.58 us  [local(): targets = lax.all_to_all(sums, 'blk', 0, 0, tiled=True)]
    ppermute x21 -> x24, starting transfers between devices: 43.9 us -> 48 us  [blk(): return lax.ppermute(value, 'blk', [(i, partner(i)) for i in range(panels)])]
    ppermute x0 -> x1, starting transfers between devices: none -> 3.36 us  [local(): lax.ppermute(r_outer, 'blk', [(i, (i + 2) % panels) for i in range(1, pan...]
    unnamed x55 -> x20, local copies, waits for them, and re-layouts: 7.92 us -> 4.61 us
    all_to_all x2 -> x0, local copies, waits for them, and re-layouts: 2.64 us -> none  [local(): targets = lax.all_to_all(sums, 'blk', 0, 0, tiled=True)]
  transfers between devices with their start and end apart: 26 -> 30, of which waited for: 16 -> 11; matrix products, arithmetic and copies ran while one was open for 13% -> 7% of each run, Pallas kernels for 12% -> 7%
where the time goes in v2:
time: 127 us; the launch traced here: 126 us
  starting transfers between devices  74.8 us (59%)
  waiting for transfers between devices  23.5 us (19%)
  Pallas kernels  14.5 us (11%)
  local copies, waits for them, and re-layouts  8.14 us (6%)
  matrix products  2.66 us (2%)
  between operations  1.67 us (1%)
    ppermute x24, starting transfers between devices, blk(): return lax.ppermute(value, 'blk', [(i, partner(i)) for i in range(panels)])  48 us
    ppermute x24, waiting for transfers between devices, blk(): return lax.ppermute(value, 'blk', [(i, partner(i)) for i in range(panels)])  12.7 us
    ppermute x3, starting transfers between devices, on_z(): lax.ppermute(value, 'grp', [(i, (i + d) % groups) for i in range(groups)])  10 us
    pallas_call x1, Pallas kernels, pair_grads(): pl.pallas_call(pair_kernel, out_shape=(panel, panel, panel, jax.ShapeDtyp...  9.29 us
    all_to_all x1, starting transfers between devices, local(): targets = lax.all_to_all(sums, 'blk', 0, 0, tiled=True)  8.58 us
    ppermute x1, waiting for transfers between devices, local(): lax.ppermute(r_outer, 'blk', [(i, (i + 2) % panels) for i in range(1, pan...  4.81 us
    ppermute x1, starting transfers between devices, local(): lax.ppermute(total, 'grp', [(i, i ^ 1) for i in range(groups)]).astype(F32)  4.76 us
    unnamed x20, local copies, waits for them, and re-layouts  4.61 us
  transfers between devices with their start and end apart: 30, of which 11 were waited for; matrix products, arithmetic and copies ran while one was open for 7% of the time, Pallas kernels for 7%

profile of v2, /device:TPU:1, one launch (start us, length us, event | category | flops | bytes accessed | tf_op | source)
XLA Modules:
  0.0 126.4 jit_solution(3584754148945049025)
XLA Ops:
  4.8 8.6 %all-to-all-start = ((bf16[32,24,512]{2,1,0:T(8,128)(2,1)}), bf16[32,24,512]{2,1,0:T(8,128)(2,1)S(1)}, u32[]{:S(2)}, u32[]{:S(2)}) async-start(bf16[32,24,512]{2,1,0:T(8,128)(2,1)} %bitcast.3), calls=%async_computation | async-start | bytes 1572864 | tf_op jit(solution)/shard_map/to_owner/all_to_all | solution.py:333
  15.6 3.8 %collective-permute-start.4 = (bf16[64,1024]{1,0:T(8,128)(2,1)S(1)}, bf16[64,1024]{1,0:T(8,128)(2,1)}, u32[]{:S(2)}, u32[]{:S(2)}) collective-permute-start(bf16[64,1024]{1,0:T(8,128)(2,1)S(1)} %bitcast.31), channel_id=1, source_target_pairs={{0,1},{1,0},{2,3},{3,2},{4,5},{5,4},{6,7},{7,6},{8,9},{9,8},{10,11... | collective-permute-start | bytes 393224 | tf_op jit(solution)/shard_map/ppermute | solution.py:313
  21.6 3.8 %collective-permute-done.right_o = bf16[80,512]{1,0:T(8,128)(2,1)S(1)} collective-permute-done((bf16[80,512]{1,0:T(8,128)(2,1)S(1)}, bf16[80,512]{1,0:T(8,128)(2,1)S(1)}, u32[]{:S(2)}, u32[]{:S(2)}) %collective-permute-start) | collective-permute-done | bytes 81952 | tf_op jit(solution)/shard_map/ppermute | solution.py:313
  27.1 2.4 %collective-permute-start.7 = (bf16[128,1024]{1,0:T(8,128)(2,1)}, bf16[128,1024]{1,0:T(8,128)(2,1)}, u32[]{:S(2)}, u32[]{:S(2)}) collective-permute-start(bf16[128,1024]{1,0:T(8,128)(2,1)} %get-tuple-element.42), channel_id=1, source_target_pairs={{0,4},{1,5},{2,6},{3,7},{4,0},{5,1},{6,2},{7,3},{8,12},{9,13},{10,... | collective-permute-start | bytes 786440 | tf_op jit(solution)/shard_map/ppermute | solution.py:313
  31.0 9.3 %pair_grads.1 = (bf16[64,512]{1,0:T(8,128)(2,1)S(1)}, bf16[64,512]{1,0:T(8,128)(2,1)S(1)}, bf16[64,512]{1,0:T(8,128)(2,1)S(1)}, bf16[128,512]{1,0:T(8,128)(2,1)S(1)}, bf16[256,512]{1,0:T(8,128)(2,1)S(1)}) custom-call(s32[1]{0:T(128)} %bitcast.core, s32[3,64]{1,0:T(4,128)S(1)} %get-tuple-element.32.ids_s, f32[8,64]{1,0:T(8,128)S(1)} %pad_convert_fusion.ids_ref, ...), custom_call_target="tpu_custom_call" | custom-call | flops 8053063680 | bytes 2097152 | tf_op jit(solution)/shard_map/pair_grads/pallas_call | solution.py:189
  40.3 3.6 %collective-permute-start.2 = (bf16[256,512]{1,0:T(8,128)(2,1)S(1)}, bf16[256,512]{1,0:T(8,128)(2,1)S(1)}, u32[]{:S(2)}, u32[]{:S(2)}) collective-permute-start(bf16[256,512]{1,0:T(8,128)(2,1)S(1)} %get-tuple-element.24), channel_id=1, source_target_pairs={{0,1},{1,0},{2,3},{3,2},{4,5},{5,4},{6,7},{7,6},{8,9},{9,8},{10,11... | collective-permute-start | bytes 786440 | tf_op jit(solution)/shard_map/ppermute | solution.py:313
  46.8 3.4 %collective-permute-start.8 = (bf16[64,512]{1,0:T(8,128)(2,1)S(1)}, bf16[64,512]{1,0:T(8,128)(2,1)S(1)}, u32[]{:S(2)}, u32[]{:S(2)}) collective-permute-start(bf16[64,512]{1,0:T(8,128)(2,1)S(1)} %get-tuple-element.25), channel_id=1, source_target_pairs={{1,3},{3,5},{5,7},{7,9},{9,11},{11,13},{13,15},{15,17},{17,19},{19... | collective-permute-start | bytes 196616 | tf_op jit(solution)/shard_map/ppermute | solution.py:364
  50.3 4.8 %collective-permute-done.8 = bf16[64,512]{1,0:T(8,128)(2,1)S(1)} collective-permute-done((bf16[64,512]{1,0:T(8,128)(2,1)S(1)}, bf16[64,512]{1,0:T(8,128)(2,1)S(1)}, u32[]{:S(2)}, u32[]{:S(2)}) %collective-permute-start.8) | collective-permute-done | bytes 65568 | tf_op jit(solution)/shard_map/ppermute | solution.py:364
  55.3 5.4 %collective-permute-start.9 = (bf16[256,128]{1,0:T(8,128)(2,1)S(1)}, bf16[256,128]{1,0:T(8,128)(2,1)S(1)}, u32[]{:S(2)}, u32[]{:S(2)}) collective-permute-start(bf16[256,128]{1,0:T(8,128)(2,1)S(1)} %get-tuple-element.37), channel_id=1, source_target_pairs={{0,2},{1,3},{2,4},{3,5},{4,6},{5,7},{6,0},{7,1},{8,10},{9,11},{10,... | collective-permute-start | bytes 196616 | tf_op jit(solution)/shard_map/ppermute | solution.py:313
  63.4 2.1 %collective-permute-done.11 = bf16[256,128]{1,0:T(8,128)(2,1)S(1)} collective-permute-done((bf16[256,128]{1,0:T(8,128)(2,1)S(1)}, bf16[256,128]{1,0:T(8,128)(2,1)S(1)}, u32[]{:S(2)}, u32[]{:S(2)}) %collective-permute-start.11) | collective-permute-done | bytes 65568 | tf_op jit(solution)/shard_map/ppermute | solution.py:313
  66.6 3.0 %collective-permute-start.12 = (bf16[288,128]{1,0:T(8,128)(2,1)S(1)}, bf16[288,128]{1,0:T(8,128)(2,1)S(1)}, u32[]{:S(2)}, u32[]{:S(2)}) collective-permute-start(bf16[288,128]{1,0:T(8,128)(2,1)S(1)} %get-tuple-element.34), channel_id=1, source_target_pairs={{0,8},{1,9},{2,10},{3,11},{4,12},{5,13},{6,14},{7,15},{8,16},{9,17... | collective-permute-start | bytes 221192 | tf_op jit(solution)/shard_map/ppermute | solution.py:313
  69.6 3.2 %collective-permute-start.14 = (bf16[288,128]{1,0:T(8,128)(2,1)S(1)}, bf16[288,128]{1,0:T(8,128)(2,1)S(1)}, u32[]{:S(2)}, u32[]{:S(2)}) collective-permute-start(bf16[288,128]{1,0:T(8,128)(2,1)S(1)} %get-tuple-element.36), channel_id=1, source_target_pairs={{0,16},{1,17},{2,18},{3,19},{4,20},{5,21},{6,22},{7,23},{8,24},{9,... | collective-permute-start | bytes 221192 | tf_op jit(solution)/shard_map/ppermute | solution.py:313
  72.9 2.3 %collective-permute-done.14 = bf16[288,128]{1,0:T(8,128)(2,1)S(1)} collective-permute-done((bf16[288,128]{1,0:T(8,128)(2,1)S(1)}, bf16[288,128]{1,0:T(8,128)(2,1)S(1)}, u32[]{:S(2)}, u32[]{:S(2)}) %collective-permute-start.14) | collective-permute-done | bytes 73760 | tf_op jit(solution)/shard_map/ppermute | solution.py:313
  75.4 4.8 %collective-permute-start.15 = (bf16[288,128]{1,0:T(8,128)(2,1)S(1)}, bf16[288,128]{1,0:T(8,128)(2,1)S(1)}, u32[]{:S(2)}, u32[]{:S(2)}) collective-permute-start(bf16[288,128]{1,0:T(8,128)(2,1)S(1)} %add_convert_fusion.3), channel_id=1, source_target_pairs={{0,32},{32,0},{64,96},{96,64},{128,160},{160,128},{192,224},{224,1... | collective-permute-start | bytes 221192 | tf_op jit(solution)/shard_map/ppermute | solution.py:393
  82.0 7.7 %collective-permute-start.18 = (bf16[288,128]{1,0:T(8,128)(2,1)S(1)}, bf16[288,128]{1,0:T(8,128)(2,1)S(1)}, u32[]{:S(2)}, u32[]{:S(2)}) collective-permute-start(bf16[288,128]{1,0:T(8,128)(2,1)S(1)} %add_convert_fusion.2), channel_id=1, source_target_pairs={{0,128},{32,160},{64,192},{96,224},{128,0},{160,32},{192,64},{224,... | collective-permute-start | bytes 221192 | tf_op jit(solution)/shard_map/ppermute | solution.py:328
  89.7 2.3 %collective-permute-start.16 = (bf16[288,128]{1,0:T(8,128)(2,1)S(1)}, bf16[288,128]{1,0:T(8,128)(2,1)S(1)}, u32[]{:S(2)}, u32[]{:S(2)}) collective-permute-start(bf16[288,128]{1,0:T(8,128)(2,1)S(1)} %add_convert_fusion.2), channel_id=1, source_target_pairs={{0,64},{32,96},{64,128},{96,160},{128,192},{160,224},{192,0},{224,... | collective-permute-start | bytes 221192 | tf_op jit(solution)/shard_map/ppermute | solution.py:328
  92.0 3.6 %collective-permute-done.17 = bf16[288,128]{1,0:T(8,128)(2,1)S(1)} collective-permute-done((bf16[288,128]{1,0:T(8,128)(2,1)S(1)}, bf16[288,128]{1,0:T(8,128)(2,1)S(1)}, u32[]{:S(2)}, u32[]{:S(2)}) %collective-permute-start.17) | collective-permute-done | bytes 73760 | tf_op jit(solution)/shard_map/ppermute | solution.py:328
  98.9 2.1 %collective-permute-done.21 = bf16[288,128]{1,0:T(8,128)(2,1)S(1)} collective-permute-done((bf16[288,128]{1,0:T(8,128)(2,1)S(1)}, bf16[288,128]{1,0:T(8,128)(2,1)S(1)}, u32[]{:S(2)}, u32[]{:S(2)}) %collective-permute-start.21) | collective-permute-done | bytes 73760 | tf_op jit(solution)/shard_map/ppermute | solution.py:313
  101.3 1.9 %collective-permute-done.19 = bf16[288,128]{1,0:T(8,128)(2,1)S(1)} collective-permute-done((bf16[288,128]{1,0:T(8,128)(2,1)S(1)}, bf16[288,128]{1,0:T(8,128)(2,1)S(1)}, u32[]{:S(2)}, u32[]{:S(2)}) %collective-permute-start.19) | collective-permute-done | bytes 73760 | tf_op jit(solution)/shard_map/ppermute | solution.py:313
  104.7 1.9 %collective-permute-start.23 = (bf16[1152,128]{1,0:T(8,128)(2,1)S(1)}, bf16[1152,128]{1,0:T(8,128)(2,1)S(1)}, u32[]{:S(2)}, u32[]{:S(2)}) collective-permute-start(bf16[1152,128]{1,0:T(8,128)(2,1)S(1)} %pad_maximum_fusion.refs_1_), channel_id=1, source_target_pairs={{0,6},{1,7},{2,0},{3,1},{4,2},{5,3},{6,4},{7,5},{8,14},{9,15},{10,... | collective-permute-start | bytes 884744 | tf_op jit(solution)/shard_map/ppermute | solution.py:313
  106.7 6.1 %collective-permute-start.25 = (bf16[1152,128]{1,0:T(8,128)(2,1)S(1)}, bf16[1152,128]{1,0:T(8,128)(2,1)S(1)}, u32[]{:S(2)}, u32[]{:S(2)}) collective-permute-start(bf16[1152,128]{1,0:T(8,128)(2,1)S(1)} %pad_maximum_fusion.refs_1_), channel_id=1, source_target_pairs={{0,1},{1,0},{2,3},{3,2},{4,5},{5,4},{6,7},{7,6},{8,9},{9,8},{10,11... | collective-permute-start | bytes 884744 | tf_op jit(solution)/shard_map/ppermute | solution.py:313
  112.7 5.5 %collective-permute-start.28 = (bf16[1152,128]{1,0:T(8,128)(2,1)S(1)}, bf16[1152,128]{1,0:T(8,128)(2,1)S(1)}, u32[]{:S(2)}, u32[]{:S(2)}) collective-permute-start(bf16[1152,128]{1,0:T(8,128)(2,1)S(1)} %collective-permute-done.24.refs_4_), channel_id=1, source_target_pairs={{0,1},{1,0},{2,3},{3,2},{4,5},{5,4},{6,7},{7,6},{8,9},{9,8},{10,11... | collective-permute-start | bytes 884744 | tf_op jit(solution)/shard_map/ppermute | solution.py:313
  118.3 1.9 %collective-permute-start.27 = (bf16[1152,128]{1,0:T(8,128)(2,1)S(1)}, bf16[1152,128]{1,0:T(8,128)(2,1)S(1)}, u32[]{:S(2)}, u32[]{:S(2)}) collective-permute-start(bf16[1152,128]{1,0:T(8,128)(2,1)S(1)} %collective-permute-done.23.refs_3_), channel_id=1, source_target_pairs={{0,1},{1,0},{2,3},{3,2},{4,5},{5,4},{6,7},{7,6},{8,9},{9,8},{10,11... | collective-permute-start | bytes 884744 | tf_op jit(solution)/shard_map/ppermute | solution.py:313
  122.9 3.4 %finish.1 = (f32[1024,512]{1,0:T(8,128)}, f32[1024,512]{1,0:T(8,128)}, f32[512,128]{1,0:T(8,128)}, f32[1,512]{1,0:T(1,128)}, f32[1,128]{1,0:T(1,128)}) custom-call(s32[3]{0:T(128)S(1)} %pad_add_fusion.refs_0_, bf16[1152,128]{1,0:T(8,128)(2,1)S(1)} %pad_maximum_fusion.refs_1_, bf16[1152,128]{1,0:T(8,128)(2,1)S(1)} %collective-permute-done.22.refs_2_, ...), custom_call_target="tpu_custom_call" | custom-call | tf_op jit(solution)/shard_map/finish/pallas_call | solution.py:404
  (89 shorter events, 27.9 us)
Async XLA Ops:
  4.8 26.1 %all-to-all-start = ((bf16[32,24,512]{2,1,0:T(8,128)(2,1)}), bf16[32,24,512]{2,1,0:T(8,128)(2,1)S(1)}, u32[]{:S(2)}, u32[]{:S(2)}) async-start(bf16[32,24,512]{2,1,0:T(8,128)(2,1)} %bitcast.3), calls=%async_computation | async-start | bytes 1572864 | tf_op jit(solution)/shard_map/to_owner/all_to_all | solution.py:333
  13.8 7.8 %collective-permute-start.1 = (bf16[80,512]{1,0:T(8,128)(2,1)S(1)}, bf16[80,512]{1,0:T(8,128)(2,1)S(1)}, u32[]{:S(2)}, u32[]{:S(2)}) collective-permute-start(bf16[80,512]{1,0:T(8,128)(2,1)S(1)} %fusion.10.right_m), channel_id=1, source_target_pairs={{0,1},{1,0},{2,3},{3,2},{4,5},{5,4},{6,7},{7,6},{8,9},{9,8},{10,11... | collective-permute-start | bytes 245768 | tf_op jit(solution)/shard_map/ppermute | solution.py:313
  14.1 11.3 %collective-permute-start = (bf16[80,512]{1,0:T(8,128)(2,1)S(1)}, bf16[80,512]{1,0:T(8,128)(2,1)S(1)}, u32[]{:S(2)}, u32[]{:S(2)}) collective-permute-start(bf16[80,512]{1,0:T(8,128)(2,1)S(1)} %fusion.10.right_m), channel_id=1, source_target_pairs={{0,31},{1,2},{2,1},{3,4},{4,3},{5,6},{6,5},{7,8},{8,7},{9,10},{10,... | collective-permute-start | bytes 245768 | tf_op jit(solution)/shard_map/ppermute | solution.py:313
  15.6 9.8 %collective-permute-start.4 = (bf16[64,1024]{1,0:T(8,128)(2,1)S(1)}, bf16[64,1024]{1,0:T(8,128)(2,1)}, u32[]{:S(2)}, u32[]{:S(2)}) collective-permute-start(bf16[64,1024]{1,0:T(8,128)(2,1)S(1)} %bitcast.31), channel_id=1, source_target_pairs={{0,1},{1,0},{2,3},{3,2},{4,5},{5,4},{6,7},{7,6},{8,9},{9,8},{10,11... | collective-permute-start | bytes 393224 | tf_op jit(solution)/shard_map/ppermute | solution.py:313
  27.1 18.7 %collective-permute-start.7 = (bf16[128,1024]{1,0:T(8,128)(2,1)}, bf16[128,1024]{1,0:T(8,128)(2,1)}, u32[]{:S(2)}, u32[]{:S(2)}) collective-permute-start(bf16[128,1024]{1,0:T(8,128)(2,1)} %get-tuple-element.42), channel_id=1, source_target_pairs={{0,4},{1,5},{2,6},{3,7},{4,0},{5,1},{6,2},{7,3},{8,12},{9,13},{10,... | collective-permute-start | bytes 786440 | tf_op jit(solution)/shard_map/ppermute | solution.py:313
  29.5 15.3 %collective-permute-start.6 = (bf16[128,1024]{1,0:T(8,128)(2,1)}, bf16[128,1024]{1,0:T(8,128)(2,1)}, u32[]{:S(2)}, u32[]{:S(2)}) collective-permute-start(bf16[128,1024]{1,0:T(8,128)(2,1)} %get-tuple-element.42), channel_id=1, source_target_pairs={{0,6},{1,7},{2,0},{3,1},{4,2},{5,3},{6,4},{7,5},{8,14},{9,15},{10,... | collective-permute-start | bytes 786440 | tf_op jit(solution)/shard_map/ppermute | solution.py:313
  30.7 13.2 %collective-permute-start.5 = (bf16[128,1024]{1,0:T(8,128)(2,1)}, bf16[128,1024]{1,0:T(8,128)(2,1)}, u32[]{:S(2)}, u32[]{:S(2)}) collective-permute-start(bf16[128,1024]{1,0:T(8,128)(2,1)} %get-tuple-element.42), channel_id=1, source_target_pairs={{0,2},{1,3},{2,4},{3,5},{4,6},{5,7},{6,0},{7,1},{8,10},{9,11},{10,... | collective-permute-start | bytes 786440 | tf_op jit(solution)/shard_map/ppermute | solution.py:313
  40.3 10.0 %collective-permute-start.2 = (bf16[256,512]{1,0:T(8,128)(2,1)S(1)}, bf16[256,512]{1,0:T(8,128)(2,1)S(1)}, u32[]{:S(2)}, u32[]{:S(2)}) collective-permute-start(bf16[256,512]{1,0:T(8,128)(2,1)S(1)} %get-tuple-element.24), channel_id=1, source_target_pairs={{0,1},{1,0},{2,3},{3,2},{4,5},{5,4},{6,7},{7,6},{8,9},{9,8},{10,11... | collective-permute-start | bytes 786440 | tf_op jit(solution)/shard_map/ppermute | solution.py:313
  46.8 8.3 %collective-permute-start.8 = (bf16[64,512]{1,0:T(8,128)(2,1)S(1)}, bf16[64,512]{1,0:T(8,128)(2,1)S(1)}, u32[]{:S(2)}, u32[]{:S(2)}) collective-permute-start(bf16[64,512]{1,0:T(8,128)(2,1)S(1)} %get-tuple-element.25), channel_id=1, source_target_pairs={{1,3},{3,5},{5,7},{7,9},{9,11},{11,13},{13,15},{15,17},{17,19},{19... | collective-permute-start | bytes 196616 | tf_op jit(solution)/shard_map/ppermute | solution.py:364
  50.2 5.0 %collective-permute-start.3 = (bf16[64,512]{1,0:T(8,128)(2,1)S(1)}, bf16[64,512]{1,0:T(8,128)(2,1)S(1)}, u32[]{:S(2)}, u32[]{:S(2)}) collective-permute-start(bf16[64,512]{1,0:T(8,128)(2,1)S(1)} %get-tuple-element.25), channel_id=1, source_target_pairs={{0,31},{1,2},{2,1},{3,4},{4,3},{5,6},{6,5},{7,8},{8,7},{9,10},{10,... | collective-permute-start | bytes 196616 | tf_op jit(solution)/shard_map/ppermute | solution.py:313
  55.3 8.1 %collective-permute-start.9 = (bf16[256,128]{1,0:T(8,128)(2,1)S(1)}, bf16[256,128]{1,0:T(8,128)(2,1)S(1)}, u32[]{:S(2)}, u32[]{:S(2)}) collective-permute-start(bf16[256,128]{1,0:T(8,128)(2,1)S(1)} %get-tuple-element.37), channel_id=1, source_target_pairs={{0,2},{1,3},{2,4},{3,5},{4,6},{5,7},{6,0},{7,1},{8,10},{9,11},{10,... | collective-permute-start | bytes 196616 | tf_op jit(solution)/shard_map/ppermute | solution.py:313
  60.6 4.8 %collective-permute-start.11 = (bf16[256,128]{1,0:T(8,128)(2,1)S(1)}, bf16[256,128]{1,0:T(8,128)(2,1)S(1)}, u32[]{:S(2)}, u32[]{:S(2)}) collective-permute-start(bf16[256,128]{1,0:T(8,128)(2,1)S(1)} %get-tuple-element.38), channel_id=1, source_target_pairs={{0,4},{1,5},{2,6},{3,7},{4,0},{5,1},{6,2},{7,3},{8,12},{9,13},{10,... | collective-permute-start | bytes 196616 | tf_op jit(solution)/shard_map/ppermute | solution.py:313
  66.6 6.1 %collective-permute-start.12 = (bf16[288,128]{1,0:T(8,128)(2,1)S(1)}, bf16[288,128]{1,0:T(8,128)(2,1)S(1)}, u32[]{:S(2)}, u32[]{:S(2)}) collective-permute-start(bf16[288,128]{1,0:T(8,128)(2,1)S(1)} %get-tuple-element.34), channel_id=1, source_target_pairs={{0,8},{1,9},{2,10},{3,11},{4,12},{5,13},{6,14},{7,15},{8,16},{9,17... | collective-permute-start | bytes 221192 | tf_op jit(solution)/shard_map/ppermute | solution.py:313
  69.6 5.6 %collective-permute-start.14 = (bf16[288,128]{1,0:T(8,128)(2,1)S(1)}, bf16[288,128]{1,0:T(8,128)(2,1)S(1)}, u32[]{:S(2)}, u32[]{:S(2)}) collective-permute-start(bf16[288,128]{1,0:T(8,128)(2,1)S(1)} %get-tuple-element.36), channel_id=1, source_target_pairs={{0,16},{1,17},{2,18},{3,19},{4,20},{5,21},{6,22},{7,23},{8,24},{9,... | collective-permute-start | bytes 221192 | tf_op jit(solution)/shard_map/ppermute | solution.py:313
  75.4 6.5 %collective-permute-start.15 = (bf16[288,128]{1,0:T(8,128)(2,1)S(1)}, bf16[288,128]{1,0:T(8,128)(2,1)S(1)}, u32[]{:S(2)}, u32[]{:S(2)}) collective-permute-start(bf16[288,128]{1,0:T(8,128)(2,1)S(1)} %add_convert_fusion.3), channel_id=1, source_target_pairs={{0,32},{32,0},{64,96},{96,64},{128,160},{160,128},{192,224},{224,1... | collective-permute-start | bytes 221192 | tf_op jit(solution)/shard_map/ppermute | solution.py:393
  82.0 10.0 %collective-permute-start.18 = (bf16[288,128]{1,0:T(8,128)(2,1)S(1)}, bf16[288,128]{1,0:T(8,128)(2,1)S(1)}, u32[]{:S(2)}, u32[]{:S(2)}) collective-permute-start(bf16[288,128]{1,0:T(8,128)(2,1)S(1)} %add_convert_fusion.2), channel_id=1, source_target_pairs={{0,128},{32,160},{64,192},{96,224},{128,0},{160,32},{192,64},{224,... | collective-permute-start | bytes 221192 | tf_op jit(solution)/shard_map/ppermute | solution.py:328
  89.6 6.0 %collective-permute-start.17 = (bf16[288,128]{1,0:T(8,128)(2,1)S(1)}, bf16[288,128]{1,0:T(8,128)(2,1)S(1)}, u32[]{:S(2)}, u32[]{:S(2)}) collective-permute-start(bf16[288,128]{1,0:T(8,128)(2,1)S(1)} %add_convert_fusion.2), channel_id=1, source_target_pairs={{0,192},{32,224},{64,0},{96,32},{128,64},{160,96},{192,128},{224,1... | collective-permute-start | bytes 221192 | tf_op jit(solution)/shard_map/ppermute | solution.py:328
  89.7 6.6 %collective-permute-start.16 = (bf16[288,128]{1,0:T(8,128)(2,1)S(1)}, bf16[288,128]{1,0:T(8,128)(2,1)S(1)}, u32[]{:S(2)}, u32[]{:S(2)}) collective-permute-start(bf16[288,128]{1,0:T(8,128)(2,1)S(1)} %add_convert_fusion.2), channel_id=1, source_target_pairs={{0,64},{32,96},{64,128},{96,160},{128,192},{160,224},{192,0},{224,... | collective-permute-start | bytes 221192 | tf_op jit(solution)/shard_map/ppermute | solution.py:328
  96.3 4.8 %collective-permute-start.21 = (bf16[288,128]{1,0:T(8,128)(2,1)S(1)}, bf16[288,128]{1,0:T(8,128)(2,1)S(1)}, u32[]{:S(2)}, u32[]{:S(2)}) collective-permute-start(bf16[288,128]{1,0:T(8,128)(2,1)S(1)} %add_convert_fusion.1), channel_id=1, source_target_pairs={{0,16},{1,17},{2,18},{3,19},{4,20},{5,21},{6,22},{7,23},{8,24},{9,... | collective-permute-start | bytes 221192 | tf_op jit(solution)/shard_map/ppermute | solution.py:313
  103.2 9.5 %collective-permute-start.24 = (bf16[1152,128]{1,0:T(8,128)(2,1)S(1)}, bf16[1152,128]{1,0:T(8,128)(2,1)S(1)}, u32[]{:S(2)}, u32[]{:S(2)}) collective-permute-start(bf16[1152,128]{1,0:T(8,128)(2,1)S(1)} %pad_maximum_fusion.refs_1_), channel_id=1, source_target_pairs={{0,4},{1,5},{2,6},{3,7},{4,0},{5,1},{6,2},{7,3},{8,12},{9,13},{10,... | collective-permute-start | bytes 884744 | tf_op jit(solution)/shard_map/ppermute | solution.py:313
  104.7 13.6 %collective-permute-start.23 = (bf16[1152,128]{1,0:T(8,128)(2,1)S(1)}, bf16[1152,128]{1,0:T(8,128)(2,1)S(1)}, u32[]{:S(2)}, u32[]{:S(2)}) collective-permute-start(bf16[1152,128]{1,0:T(8,128)(2,1)S(1)} %pad_maximum_fusion.refs_1_), channel_id=1, source_target_pairs={{0,6},{1,7},{2,0},{3,1},{4,2},{5,3},{6,4},{7,5},{8,14},{9,15},{10,... | collective-permute-start | bytes 884744 | tf_op jit(solution)/shard_map/ppermute | solution.py:313
  106.6 13.6 %collective-permute-start.22 = (bf16[1152,128]{1,0:T(8,128)(2,1)S(1)}, bf16[1152,128]{1,0:T(8,128)(2,1)S(1)}, u32[]{:S(2)}, u32[]{:S(2)}) collective-permute-start(bf16[1152,128]{1,0:T(8,128)(2,1)S(1)} %pad_maximum_fusion.refs_1_), channel_id=1, source_target_pairs={{0,2},{1,3},{2,4},{3,5},{4,6},{5,7},{6,0},{7,1},{8,10},{9,11},{10,... | collective-permute-start | bytes 884744 | tf_op jit(solution)/shard_map/ppermute | solution.py:313
  106.7 16.2 %collective-permute-start.25 = (bf16[1152,128]{1,0:T(8,128)(2,1)S(1)}, bf16[1152,128]{1,0:T(8,128)(2,1)S(1)}, u32[]{:S(2)}, u32[]{:S(2)}) collective-permute-start(bf16[1152,128]{1,0:T(8,128)(2,1)S(1)} %pad_maximum_fusion.refs_1_), channel_id=1, source_target_pairs={{0,1},{1,0},{2,3},{3,2},{4,5},{5,4},{6,7},{7,6},{8,9},{9,8},{10,11... | collective-permute-start | bytes 884744 | tf_op jit(solution)/shard_map/ppermute | solution.py:313
  112.7 10.2 %collective-permute-start.28 = (bf16[1152,128]{1,0:T(8,128)(2,1)S(1)}, bf16[1152,128]{1,0:T(8,128)(2,1)S(1)}, u32[]{:S(2)}, u32[]{:S(2)}) collective-permute-start(bf16[1152,128]{1,0:T(8,128)(2,1)S(1)} %collective-permute-done.24.refs_4_), channel_id=1, source_target_pairs={{0,1},{1,0},{2,3},{3,2},{4,5},{5,4},{6,7},{7,6},{8,9},{9,8},{10,11... | collective-permute-start | bytes 884744 | tf_op jit(solution)/shard_map/ppermute | solution.py:313
  (14 other events, 126.4 us)

commit v3 on v2

--- a/solution.py
+++ b/solution.py
@@ -15,108 +15,44 @@
 F32 = jnp.float32
 
 
-def forward(tile_at, left_s, right_s, hid_s, slope_s, rows=range(ROWS)):
-    k = tile_at // 8
-    left8 = left_s[pl.ds(pl.multiple_of(tile_at % 8 * ROWS, ROWS), ROWS), :]
-    right = right_s[pl.ds(pl.multiple_of(k * PANEL, PANEL), PANEL), :]
-    for a in rows:
-        part = slice(a * PANEL, (a + 1) * PANEL)
-        u = right.astype(BF) + jnp.broadcast_to(left8[a : a + 1, :], right.shape).astype(BF)
-        p = jnp.tanh(u) + BF(1.0)
-        h = u * p
-        hid_s[part, :] = h
-        slope_s[part, :] = p + h * (BF(2.0) - p)
-
-
-def backward(
-    tile_at, hid_s, slope_s, tsum_s, mask_s, half_s, wmt_ref, wf_ref, lacc, racc, mid_acc, fin_acc
-):
-    col0 = pl.multiple_of(tile_at // 8 * PANEL, PANEL)
-    row0 = pl.multiple_of(tile_at % 8 * ROWS, ROWS)
-    wf = wf_ref[...]
-    count = tsum_s[tile_at // 8 * 8 + 24, 0:1, 0:CHUNK]
-    parts = [slice(c * CHUNK, (c + 1) * CHUNK) for c in range(ROWS * PANEL // CHUNK)]
-    pre = [
-        jnp.dot(hid_s[part, :], half_s[...], preferred_element_type=F32).T
-        for part in parts
-    ]
-    terms, hiddens, fins = [], [], []
-    for part, u in zip(parts, pre):
-        p = jnp.tanh(u) + 1.0
-        act = u * p
-        predicted = jnp.sum(act * wf, axis=0, keepdims=True)
-        pair_slope = (16.0 * mask_s[tile_at, 0:1, part]) * (count * predicted - tsum_s[tile_at, 0:1, part])
-        grad_second = ((0.5 * pair_slope) * wf * (p + act * (2.0 - p))).astype(BF)
-        fin = act * pair_slope
-        fins.append(sum(fin[:, j * 128 : (j + 1) * 128] for j in range(CHUNK // 128)))
-        hiddens.append(
-            lax.dot_general(grad_second, wmt_ref[...], (((0,), (0,)), ((), ())), preferred_element_type=F32)
-        )
-        terms.append(jnp.dot(grad_second, hid_s[part, :], preferred_element_type=F32))
-    fin_acc[...] += sum(fins)
-    cols, rows = None, []
-    for part, grad_hidden in zip(parts, hiddens):
-        for a in range(CHUNK // PANEL):
-            at = slice(part.start + a * PANEL, part.start + (a + 1) * PANEL)
-            g = grad_hidden[a * PANEL : (a + 1) * PANEL, :] * slope_s[at, :].astype(F32)
-            rows.append(jnp.sum(g, axis=0, keepdims=True))
-            cols = g if cols is None else cols + g
-    mid_acc[...] += sum(terms)
-    racc[pl.ds(col0, PANEL), :] += cols
-    lacc[pl.ds(row0, ROWS), :] += jnp.concatenate(rows, axis=0)
-
-
-def pair_kernel(
-    core,
-    ids_s,
-    ids_ref,
-    left_ref,
-    right_o,
-    right_m,
-    right_p,
-    targets_ref,
-    bias_ref,
-    wmt_ref,
-    wf_ref,
-    out_left,
-    out_outer,
-    out_own,
-    out_keep,
-    out_sent,
-    todo,
-    left_s,
-    right_s,
-    tsum_s,
-    mask_s,
-    half_s,
-    hid_s,
-    slope_s,
-    lacc,
-    racc,
-    mid_acc,
-    fin_acc,
-):
-    hidden = left_ref.shape[1]
-    tile = ROWS * PANEL
-    iota = lambda shape, axis: lax.broadcasted_iota(jnp.int32, shape, axis)
+def list_tiles(ids_s, todo):
     def scan(i, n):
         k, rt = i // 8, i % 8
         meets = (ids_s[1, rt * ROWS] <= ids_s[k, PANEL - 1]) & (ids_s[k, 0] <= ids_s[1, rt * ROWS + ROWS - 1])
         todo[n] = i
         return n + meets.astype(jnp.int32)
 
-    n_todo = lax.fori_loop(0, 24, scan, 0)
-    for extra in range(3):
-        todo[n_todo + extra] = 24
+    return lax.fori_loop(0, 24, scan, 0)
+
+
+def halve(left_ref, bias_ref, rights, left_s, right_s):
     left_s[...] = (left_ref[...].astype(F32) + bias_ref[...]) * 0.5
-    for k, ref in enumerate((right_o, right_m, right_p)):
-        right_s[k * PANEL : (k + 1) * PANEL, :] = ref[0:PANEL, :].astype(F32) * 0.5
-    right_s[3 * PANEL :, :] = jnp.zeros((PANEL, hidden), F32)
-    half_s[...] = (wmt_ref[...].astype(F32) * 0.5).T.astype(BF)
-    n_src = targets_ref.shape[0]
-    tsum = jnp.dot(
-        (iota((24, n_src), 1) % 24 == iota((24, n_src), 0)).astype(BF), targets_ref[...], preferred_element_type=F32
-    )
+    for k, ref in enumerate(rights):
+        right_s[k * PANEL : (k + 1) * PANEL, :] = (ref[0:PANEL, :].astype(F32) * 0.5).astype(BF)
+
+
+def hidden_layer(tile_at, left_s, right_s, hid_s, slope_s=None):
+    left8 = left_s[pl.ds(pl.multiple_of(tile_at % 8 * ROWS, ROWS), ROWS), :]
+    right = right_s[pl.ds(pl.multiple_of(tile_at // 8 * PANEL, PANEL), PANEL), :]
+    for a in range(ROWS):
+        part = slice(a * PANEL, (a + 1) * PANEL)
+        u = right + jnp.broadcast_to(left8[a : a + 1, :], right.shape).astype(BF)
+        p = jnp.tanh(u) + BF(1.0)
+        h = u * p
+        hid_s[part, :] = h
+        if slope_s is not None:
+            slope_s[part, :] = p + h * (BF(2.0) - p)
+
+
+def forward_kernel(
+    ids_s, ids_ref, left_ref, right_o, right_m, right_p, bias_ref, wm_ref, wf_ref, kept_ref, rows_ref,
+    todo, left_s, right_s, half_s, hid_s, mask_s, kept_s, rows_s, sems,
+):
+    tile = ROWS * PANEL
+    iota = lambda shape, axis: lax.broadcasted_iota(jnp.int32, shape, axis)
+    n_todo = list_tiles(ids_s, todo)
+    halve(left_ref, bias_ref, (right_o, right_m, right_p), left_s, right_s)
+    half_s[...] = (wm_ref[...].astype(F32) * 0.5).astype(BF)
     ids = ids_ref[...]
     spread = (iota((PANEL, tile), 0) % ROWS == iota((PANEL, tile), 1) // PANEL).astype(BF)
     repeat = (iota((PANEL, tile), 0) == iota((PANEL, tile), 1) % PANEL).astype(BF)
@@ -127,24 +63,126 @@
     itself = iota((8, tile), 0) * ROWS + lane // PANEL == lane % PANEL
     for k in range(3):
         same = row_ids == col_ids[k : k + 1, :]
-        mask = jnp.where(same & ~itself if k == 1 else same, 1.0, 0.0)
-        count = jnp.max(
-            jnp.where(iota((8, tile), 1) == k * (PANEL + 1), tsum[8:16, :], 0.0)[0:1], axis=1, keepdims=True
-        )
-        tsum_s[24 + 8 * k, 0:1, :] = jnp.broadcast_to(count, (1, tile))
+        mask = jnp.where(same & ~itself if k == 1 else same, 16.0, 0.0)
         for rt in range(8):
             mask_s[k * 8 + rt, 0:1, :] = mask[rt : rt + 1, :]
-            tsum_s[k * 8 + rt, 0:1, :] = tsum[k * 8 + rt : k * 8 + rt + 1, :]
-    mask_s[24, 0:1, :] = jnp.zeros((1, tile), F32)
-    tsum_s[48, 0:1, :] = jnp.zeros((1, tile), F32)
+
+    def put(i):
+        return (
+            pltpu.make_async_copy(kept_s.at[i & 1], kept_ref.at[todo[i]], sems.at[0, i & 1]),
+            pltpu.make_async_copy(rows_s.at[i & 1], rows_ref.at[todo[i]], sems.at[1, i & 1]),
+        )
+
+    def step(i, carry):
+        tile_at = todo[i]
+        hidden_layer(tile_at, left_s, right_s, hid_s)
+
+        @pl.when(i >= 2)
+        def _():
+            for copy in put(i - 2):
+                copy.wait()
+
+        wf = wf_ref[...]
+        upper = wf.shape[0]
+        rows_s[i & 1, 1:2, :] = mask_s[tile_at, 0:1, :]
+        for c in range(tile // CHUNK):
+            part = slice(c * CHUNK, (c + 1) * CHUNK)
+            u = jnp.dot(hid_s[part, :], half_s[...], preferred_element_type=F32).T
+            p = jnp.tanh(u) + 1.0
+            act = u * p
+            rows_s[i & 1, 0:1, part] = jnp.sum(act * wf, axis=0, keepdims=True)
+            kept_s[i & 1, 0:upper, part] = ((0.5 * wf) * (p + act * (2.0 - p))).astype(BF)
+            kept_s[i & 1, upper:, part] = act.astype(BF)
+        for copy in put(i):
+            copy.start()
+        return carry
+
+    lax.fori_loop(0, n_todo, step, 0)
+
+    def drain(i, carry):
+        for copy in put(i):
+            copy.wait()
+        return carry
+
+    lax.fori_loop(jnp.maximum(n_todo - 2, 0), n_todo, drain, 0)
+
+
+def backward_kernel(
+    core, ids_s, left_ref, right_o, right_m, right_p, kept_ref, rows_ref, targets_ref, bias_ref, wmt_ref,
+    out_left, out_outer, out_own, out_keep, out_sent,
+    todo, left_s, right_s, tsum_s, hid_s, slope_s, lacc, racc, mid_acc, fin_acc, kept_s, rows_s, sems,
+):
+    hidden = left_ref.shape[1]
+    tile = ROWS * PANEL
+    iota = lambda shape, axis: lax.broadcasted_iota(jnp.int32, shape, axis)
+    n_todo = list_tiles(ids_s, todo)
+
+    def fetch(i):
+        return (
+            pltpu.make_async_copy(kept_ref.at[todo[i]], kept_s.at[i & 1], sems.at[0, i & 1]),
+            pltpu.make_async_copy(rows_ref.at[todo[i]], rows_s.at[i & 1], sems.at[1, i & 1]),
+        )
+
+    @pl.when(n_todo > 0)
+    def _():
+        for copy in fetch(0):
+            copy.start()
+
+    halve(left_ref, bias_ref, (right_o, right_m, right_p), left_s, right_s)
+    n_src = targets_ref.shape[0]
+    tsum = jnp.dot(
+        (iota((24, n_src), 1) % 24 == iota((24, n_src), 0)).astype(BF), targets_ref[...], preferred_element_type=F32
+    )
+    for k in range(3):
+        count = jnp.max(
+            jnp.where(iota((1, tile), 1) == k * (PANEL + 1), tsum[8:9, :], 0.0), axis=1, keepdims=True
+        )
+        tsum_s[24 + k, 0:1, :] = jnp.broadcast_to(count, (1, tile))
+    for i in range(24):
+        tsum_s[i, 0:1, :] = tsum[i : i + 1, :]
     lacc[...] = jnp.zeros_like(lacc)
     racc[...] = jnp.zeros_like(racc)
     mid_acc[...] = jnp.zeros_like(mid_acc)
     fin_acc[...] = jnp.zeros_like(fin_acc)
-    rest = (tsum_s, mask_s, half_s, wmt_ref, wf_ref, lacc, racc, mid_acc, fin_acc)
+
     def step(i, carry):
-        forward(todo[i], left_s, right_s, hid_s, slope_s)
-        backward(todo[i], hid_s, slope_s, *rest)
+        tile_at = todo[i]
+        col0 = pl.multiple_of(tile_at // 8 * PANEL, PANEL)
+        row0 = pl.multiple_of(tile_at % 8 * ROWS, ROWS)
+
+        @pl.when(i + 1 < n_todo)
+        def _():
+            for copy in fetch(i + 1):
+                copy.start()
+
+        for copy in fetch(i):
+            copy.wait()
+        slope = rows_s[i & 1, 1:2, :] * (
+            tsum_s[tile_at // 8 + 24, 0:1, :] * rows_s[i & 1, 0:1, :] - tsum_s[tile_at, 0:1, :]
+        )
+        upper = wmt_ref.shape[0]
+        seconds, hiddens, fins = [], [], []
+        parts = [slice(c * CHUNK, (c + 1) * CHUNK) for c in range(tile // CHUNK)]
+        for part in parts:
+            seconds.append((kept_s[i & 1, 0:upper, part].astype(F32) * slope[:, part]).astype(BF))
+            hiddens.append(
+                lax.dot_general(seconds[-1], wmt_ref[...], (((0,), (0,)), ((), ())), preferred_element_type=F32)
+            )
+            fin = kept_s[i & 1, upper:, part].astype(F32) * slope[:, part]
+            fins.append(sum(fin[:, j * 128 : (j + 1) * 128] for j in range(CHUNK // 128)))
+        fin_acc[...] += sum(fins)
+        hidden_layer(tile_at, left_s, right_s, hid_s, slope_s)
+        terms = [jnp.dot(g, hid_s[part, :], preferred_element_type=F32) for g, part in zip(seconds, parts)]
+        cols, rows = None, []
+        for part, grad_hidden in zip(parts, hiddens):
+            for a in range(CHUNK // PANEL):
+                at = slice(part.start + a * PANEL, part.start + (a + 1) * PANEL)
+                g = grad_hidden[a * PANEL : (a + 1) * PANEL, :] * slope_s[at, :].astype(F32)
+                rows.append(jnp.sum(g, axis=0, keepdims=True))
+                cols = g if cols is None else cols + g
+        mid_acc[...] += sum(terms)
+        racc[pl.ds(col0, PANEL), :] += cols
+        lacc[pl.ds(row0, ROWS), :] += jnp.concatenate(rows, axis=0)
         return carry
 
     lax.fori_loop(0, n_todo, step, 0)
@@ -180,14 +218,45 @@
         small(out_keep, 0)
 
 
-def pair_grads(core, ids_s, ids, left, right_o, right_m, right_p, targets, bias, wmt, wf):
+def pair_forward(ids_s, ids, left, rights, bias, wm, wf):
+    hidden, upper = wm.shape
+    tile = ROWS * PANEL
+    vmem = pl.BlockSpec(memory_space=pltpu.VMEM)
+    return pl.pallas_call(
+        forward_kernel,
+        out_shape=(
+            pltpu.HBM((24, 2 * upper, tile), BF),
+            pltpu.HBM((24, 8, tile), F32),
+        ),
+        in_specs=[pl.BlockSpec(memory_space=pltpu.SMEM)] + [vmem] * 8,
+        out_specs=(pl.BlockSpec(memory_space=pltpu.HBM),) * 2,
+        scratch_shapes=[
+            pltpu.SMEM((32,), jnp.int32),
+            pltpu.VMEM((PANEL, hidden), F32),
+            pltpu.VMEM((3 * PANEL, hidden), BF),
+            pltpu.VMEM((hidden, upper), BF),
+            pltpu.VMEM((tile, hidden), BF),
+            pltpu.VMEM((24, 8, tile), F32),
+            pltpu.VMEM((2, 2 * upper, tile), BF),
+            pltpu.VMEM((2, 8, tile), F32),
+            pltpu.SemaphoreType.DMA((2, 2)),
+        ],
+        compiler_params=pltpu.CompilerParams(vmem_limit_bytes=12 << 20),
+        cost_estimate=pl.CostEstimate(
+            flops=2 * 24 * tile * hidden * upper, bytes_accessed=8 << 20, transcendentals=24 * tile * hidden
+        ),
+        name="pair_forward",
+    )(ids_s, ids, left, *rights, bias, wm, wf)
+
+
+def pair_backward(core, ids_s, left, rights, kept, targets, bias, wmt):
     hidden = left.shape[1]
     upper = wmt.shape[0]
     tile = ROWS * PANEL
     vmem = pl.BlockSpec(memory_space=pltpu.VMEM)
     panel = jax.ShapeDtypeStruct((PANEL, hidden), BF)
     return pl.pallas_call(
-        pair_kernel,
+        backward_kernel,
         out_shape=(
             panel,
             panel,
@@ -195,28 +264,32 @@
             jax.ShapeDtypeStruct((upper, hidden), BF),
             jax.ShapeDtypeStruct((2 * PANEL + upper, hidden), BF),
         ),
-        in_specs=[pl.BlockSpec(memory_space=pltpu.SMEM)] * 2 + [vmem] * 9,
+        in_specs=[pl.BlockSpec(memory_space=pltpu.SMEM)] * 2
+        + [vmem] * 4
+        + [pl.BlockSpec(memory_space=pltpu.HBM)] * 2
+        + [vmem] * 3,
         out_specs=(vmem,) * 5,
         scratch_shapes=[
             pltpu.SMEM((32,), jnp.int32),
             pltpu.VMEM((PANEL, hidden), F32),
-            pltpu.VMEM((4 * PANEL, hidden), F32),
-            pltpu.VMEM((49, 8, tile), F32),
-            pltpu.VMEM((25, 8, tile), F32),
-            pltpu.VMEM((hidden, upper), BF),
+            pltpu.VMEM((3 * PANEL, hidden), BF),
+            pltpu.VMEM((27, 8, tile), F32),
             pltpu.VMEM((tile, hidden), BF),
             pltpu.VMEM((tile, hidden), BF),
             pltpu.VMEM((PANEL, hidden), F32),
-            pltpu.VMEM((4 * PANEL, hidden), F32),
+            pltpu.VMEM((3 * PANEL, hidden), F32),
             pltpu.VMEM((upper, hidden), F32),
             pltpu.VMEM((upper, 128), F32),
+            pltpu.VMEM((2, 2 * upper, tile), BF),
+            pltpu.VMEM((2, 8, tile), F32),
+            pltpu.SemaphoreType.DMA((2, 2)),
         ],
-        compiler_params=pltpu.CompilerParams(vmem_limit_bytes=24 << 20),
+        compiler_params=pltpu.CompilerParams(vmem_limit_bytes=12 << 20),
         cost_estimate=pl.CostEstimate(
-            flops=10 * 24 * tile * hidden * upper, bytes_accessed=2 << 20, transcendentals=24 * tile * hidden
-        ),
-        name="pair_grads",
-    )(core, ids_s, ids, left, right_o, right_m, right_p, targets, bias, wmt, wf)
+            flops=4 * 24 * tile * hidden * upper, bytes_accessed=8 << 20, transcendentals=24 * tile * hidden
+        ),
+        name="pair_backward",
+    )(core, ids_s, left, *rights, *kept, targets, bias, wmt)
 
 
 def send_kernel(blocks, live, targets_ref, out_ref, acc):
@@ -256,6 +329,35 @@
         compiler_params=pltpu.CompilerParams(vmem_limit_bytes=8 << 20),
         name="send_targets",
     )(blocks, live, targets)
+
+
+def slice_kernel(*refs):
+    embs, parts, out = refs[:4], refs[4:8], refs[8]
+    depth = embs[0].shape[1]
+    rows = embs[0].shape[0]
+    total = extra = None
+    for emb, part in zip(embs, parts):
+        term = lax.dot_general(
+            emb[...], part[0:rows, :], (((0,), (0,)), ((), ())), preferred_element_type=F32
+        )
+        more = part[rows:, :].astype(F32)
+        total = term if total is None else total + term
+        extra = more if extra is None else extra + more
+    out[0:depth, :] = total.astype(BF)
+    out[depth:, :] = extra.astype(BF)
+
+
+def weight_slice(embs, parts):
+    rows, depth = embs[0].shape
+    vmem = pl.BlockSpec(memory_space=pltpu.VMEM)
+    return pl.pallas_call(
+        slice_kernel,
+        out_shape=jax.ShapeDtypeStruct((depth + parts[0].shape[0] - rows, parts[0].shape[1]), BF),
+        in_specs=[vmem] * 8,
+        out_specs=vmem,
+        compiler_params=pltpu.CompilerParams(vmem_limit_bytes=16 << 20),
+        name="weight_slice",
+    )(*embs, *parts)
 
 
 ORDER = (0, 1, 3, 2)
@@ -327,36 +429,41 @@
     def on_z(value, d):
         return lax.ppermute(value, "grp", [(i, (i + d) % groups) for i in range(groups)])
 
-    sums = send_targets(block_list[0], block_counts, pair_targets[0], panels).reshape(panels, 24, ROWS * PANEL)
-    sums, emb, ids = lax.optimization_barrier((sums, emb, cluster_ids[0]))
-    with jax.named_scope("to_owner"):
-        targets = lax.all_to_all(sums, "blk", 0, 0, tiled=True)
-    targets = targets.reshape(24 * panels, ROWS * PANEL)
-
-    left = jnp.dot(emb, w_left, preferred_element_type=F32).astype(BF)
     right = jnp.dot(emb, w_right, preferred_element_type=F32).astype(BF)
-    ids = ids.astype(BF)
+    ids = cluster_ids[0].astype(BF)
     ids_row = jnp.pad(ids[None, :], ((0, 15), (0, hidden - PANEL)))
     right_own = jnp.concatenate([right, ids_row], axis=0)
     right_outer = on_outer(right_own)
     right_partner = on_core(right_own)
+
+    sums = send_targets(block_list[0], block_counts, pair_targets[0], panels).reshape(panels, 24, ROWS * PANEL)
+    targets = lax.all_to_all(sums, "blk", 0, 0, tiled=True)
+    targets = targets.reshape(24 * panels, ROWS * PANEL)
+
+    left = jnp.dot(emb, w_left, preferred_element_type=F32).astype(BF)
     col_ids = jnp.stack([right_outer[PANEL, :PANEL], ids, right_partner[PANEL, :PANEL]])
-    lg, r_outer, r_own, keep, sent = pair_grads(
-        core[None],
-        col_ids.astype(jnp.int32),
+    ids_s = col_ids.astype(jnp.int32)
+    rights = (right_outer, right_own, right_partner)
+    kept = pair_forward(
+        ids_s,
         jnp.pad(col_ids.astype(F32), ((0, 5), (0, 0))),
         left,
-        right_outer,
-        right_own,
-        right_partner,
-        targets,
+        rights,
         hidden_bias[None, :],
-        w_middle.T,
+        w_middle,
         w_final[:, None],
     )
 
+    kept = [pltpu.with_memory_space_constraint(k, pltpu.HBM) for k in kept]
+
     emb_pair = jnp.concatenate([emb, on_core(emb)], axis=0)
-    emb_all = jnp.concatenate([emb_pair] + [on_x(emb_pair, d) for d in ORDER[1:]], axis=0)
+    embs = [emb_pair]
+    for d in ORDER[1:]:
+        embs.append(on_x(emb_pair, d))
+
+    lg, r_outer, r_own, keep, sent = pair_backward(
+        core[None], ids_s, left, rights, kept, targets, hidden_bias[None, :], w_middle.T
+    )
 
     first = core == 0
     got = on_core(sent)
@@ -377,10 +484,7 @@
         return lax.dynamic_slice_in_dim(both, ((x + d) & 3) * 128, 128, 1)
 
     parts = [column(0)] + [on_x(column(d), d) for d in ORDER[1:]]
-    grads = jnp.concatenate([p[: 2 * PANEL] for p in parts], axis=0)
-    weight = lax.dot_general(emb_all, grads, (((0,), (0,)), ((), ())), preferred_element_type=F32)
-    extra = sum(p[2 * PANEL :].astype(F32) for p in parts)
-    total = jnp.concatenate([weight, extra], axis=0).astype(BF)
+    total = weight_slice(embs, parts)
     piece = total.shape[0] // 4
 
     def rows(d):
@@ -393,6 +497,7 @@
         + lax.ppermute(total, "grp", [(i, i ^ 1) for i in range(groups)]).astype(F32)
     ).astype(BF)
     total = sum(p.astype(F32) for p in [total] + [on_z(total, d) for d in (2, 6, 4)]).astype(BF)
+    total, grad_local = lax.optimization_barrier((total, grad_local))
 
     total = jnp.concatenate([total] + [on_y(total, d) for d in ORDER[1:]], axis=0)
     mine = [total] + [on_x(total, d) for d in ORDER[1:]]

time: 127 us -> 144 us (1.13)
  Pallas kernels: 14.5 us -> 28.6 us
  local copies, waits for them, and re-layouts: 8.14 us -> 2.13 us
  starting transfers between devices: 74.8 us -> 79 us
  waiting for transfers between devices: 23.5 us -> 26.7 us
  matrix products: 2.66 us -> 4.61 us
    pallas_call x1 -> x3, Pallas kernels: 9.29 us -> 23.6 us  [the longest x1 12.9 us: pair_backward(): pl.pallas_call(backward_kernel, out_shape=(panel, panel, panel, jax.Shape...]
    ppermute x24, waiting for transfers between devices: 12.7 us -> 22.6 us  [blk(): return lax.ppermute(value, 'blk', [(i, partner(i)) for i in range(panels)])]
    ppermute x24, starting transfers between devices: 48 us -> 51.7 us  [blk(): return lax.ppermute(value, 'blk', [(i, partner(i)) for i in range(panels)])]
    ppermute x1, waiting for transfers between devices: 4.81 us -> 1.21 us  [local(): lax.ppermute(r_outer, 'blk', [(i, (i + 2) % panels) for i in range(1, pan...]
    unnamed x20 -> x18, local copies, waits for them, and re-layouts: 4.61 us -> 1.07 us
    ppermute x3, waiting for transfers between devices: 4.24 us -> 1.61 us  [on_z(): lax.ppermute(value, 'grp', [(i, (i + d) % groups) for i in range(groups)])]
    ppermute x3, starting transfers between devices: 10 us -> 7.41 us  [on_z(): lax.ppermute(value, 'grp', [(i, (i + d) % groups) for i in range(groups)])]
    concatenate x2 -> x1, local copies, waits for them, and re-layouts: 2.6 us -> 0.01 us  [local(): jnp.concatenate([total] + [on_y(total, d) for d in ORDER[1:]], axis=0)]
  transfers between devices with their start and end apart: 30 -> 30, of which waited for: 11 -> 14; matrix products, arithmetic and copies ran while one was open for 7% -> 4% of each run, Pallas kernels for 7% -> 7%
where the time goes in v3:
time: 144 us; the launch traced here: 143 us
  starting transfers between devices  79 us (55%)
  Pallas kernels  28.6 us (20%)
  waiting for transfers between devices  26.7 us (19%)
  matrix products  4.61 us (3%)
  local copies, waits for them, and re-layouts  2.13 us (1%)
  between operations  1.57 us (1%)
    ppermute x24, starting transfers between devices, blk(): return lax.ppermute(value, 'blk', [(i, partner(i)) for i in range(panels)])  51.7 us
    ppermute x24, waiting for transfers between devices, blk(): return lax.ppermute(value, 'blk', [(i, partner(i)) for i in range(panels)])  22.6 us
    pallas_call x1, Pallas kernels, pair_backward(): pl.pallas_call(backward_kernel, out_shape=(panel, panel, panel, jax.Shape...  12.9 us
    pallas_call x1, Pallas kernels, pair_forward(): pl.pallas_call(forward_kernel, out_shape=(pltpu.HBM((24, 2 * upper, tile)...  10.2 us
    all_to_all x1, starting transfers between devices, local(): targets = lax.all_to_all(sums, 'blk', 0, 0, tiled=True)  8.75 us
    ppermute x3, starting transfers between devices, on_z(): lax.ppermute(value, 'grp', [(i, (i + d) % groups) for i in range(groups)])  7.41 us
    ppermute x1, starting transfers between devices, local(): lax.ppermute(total, 'grp', [(i, i ^ 1) for i in range(groups)]).astype(F32)  6.98 us
    ppermute x1, starting transfers between devices, local(): lax.ppermute(r_outer, 'blk', [(i, (i + 2) % panels) for i in range(1, pan...  4.21 us
  transfers between devices with their start and end apart: 30, of which 14 were waited for; matrix products, arithmetic and copies ran while one was open for 4% of the time, Pallas kernels for 7%

profile of v3, /device:TPU:1, one launch (start us, length us, event | category | flops | bytes accessed | tf_op | source)
XLA Modules:
  0.0 143.1 jit_solution(6839743085277915067)
XLA Ops:
  3.1 1.7 %send_targets.1 = bf16[768,512]{1,0:T(8,128)(2,1)} custom-call(s32[8,2]{1,0:T(8,128)S(1)} %copy.17.blocks, s32[1,1]{1,0:T(1,128)S(6)} %copy.22.live, f32[8,4096]{1,0:T(8,128)S(1)} %bitcast.24), custom_call_target="tpu_custom_call" | custom-call | tf_op jit(solution)/shard_map/send_targets/pallas_call | solution.py:323
  4.8 8.8 %all-to-all-start = ((bf16[32,24,512]{2,1,0:T(8,128)(2,1)}), bf16[32,24,512]{2,1,0:T(8,128)(2,1)S(1)}, u32[]{:S(2)}, u32[]{:S(2)}) async-start(bf16[32,24,512]{2,1,0:T(8,128)(2,1)} %bitcast.6), calls=%async_computation | async-start | bytes 1572864 | tf_op jit(solution)/shard_map/all_to_all | solution.py:440
  13.9 1.7 %collective-permute-start.4 = (bf16[80,512]{1,0:T(8,128)(2,1)S(1)}, bf16[80,512]{1,0:T(8,128)(2,1)S(1)}, u32[]{:S(2)}, u32[]{:S(2)}) collective-permute-start(bf16[80,512]{1,0:T(8,128)(2,1)S(1)} %fusion.2.right_m), channel_id=1, source_target_pairs={{0,31},{1,2},{2,1},{3,4},{4,3},{5,6},{6,5},{7,8},{8,7},{9,10},{10,... | collective-permute-start | bytes 245768 | tf_op jit(solution)/shard_map/ppermute | solution.py:415
  15.6 3.5 %collective-permute-start.5 = (bf16[80,512]{1,0:T(8,128)(2,1)S(1)}, bf16[80,512]{1,0:T(8,128)(2,1)S(1)}, u32[]{:S(2)}, u32[]{:S(2)}) collective-permute-start(bf16[80,512]{1,0:T(8,128)(2,1)S(1)} %fusion.2.right_m), channel_id=1, source_target_pairs={{0,1},{1,0},{2,3},{3,2},{4,5},{5,4},{6,7},{7,6},{8,9},{9,8},{10,11... | collective-permute-start | bytes 245768 | tf_op jit(solution)/shard_map/ppermute | solution.py:415
  20.9 4.6 %collective-permute-done.4.right_o = bf16[80,512]{1,0:T(8,128)(2,1)S(1)} collective-permute-done((bf16[80,512]{1,0:T(8,128)(2,1)S(1)}, bf16[80,512]{1,0:T(8,128)(2,1)S(1)}, u32[]{:S(2)}, u32[]{:S(2)}) %collective-permute-start.4) | collective-permute-done | bytes 81952 | tf_op jit(solution)/shard_map/ppermute | solution.py:415
  25.6 10.2 %pair_forward.1 = (bf16[24,256,512]{2,1,0:T(8,128)(2,1)}, f32[24,8,512]{2,1,0:T(8,128)}) custom-call(s32[3,64]{1,0:T(4,128)S(1)} %get-tuple-element.34.ids_s, f32[8,64]{1,0:T(8,128)S(1)} %pad_convert_fusion.ids_ref, bf16[64,512]{1,0:T(8,128)(2,1)S(1)} %convolution_convert_fusion.left_ref, bf16[80,512]{1,0:T(8,128)(2,1)S(1)} %collective-permute-done.4.right_o, ...), custom_call_target="tpu_custom_call" | custom-call | flops 1610612736 | bytes 8388608 | tf_op jit(solution)/shard_map/pair_forward/pallas_call | solution.py:225
  35.7 12.9 %pair_backward.1 = (bf16[64,512]{1,0:T(8,128)(2,1)S(1)}, bf16[64,512]{1,0:T(8,128)(2,1)S(1)}, bf16[64,512]{1,0:T(8,128)(2,1)S(1)}, bf16[128,512]{1,0:T(8,128)(2,1)S(1)}, bf16[256,512]{1,0:T(8,128)(2,1)S(1)}) custom-call(s32[1]{0:T(128)} %bitcast.1.core, s32[3,64]{1,0:T(4,128)S(1)} %get-tuple-element.34.ids_s, ...), custom_call_target="tpu_custom_call" | custom-call | flops 3221225472 | bytes 8388608 | tf_op jit(solution)/shard_map/pair_backward/pallas_call | solution.py:258
  51.6 4.2 %collective-permute-start.8 = (bf16[64,512]{1,0:T(8,128)(2,1)S(1)}, bf16[64,512]{1,0:T(8,128)(2,1)S(1)}, u32[]{:S(2)}, u32[]{:S(2)}) collective-permute-start(bf16[64,512]{1,0:T(8,128)(2,1)S(1)} %get-tuple-element.25), channel_id=1, source_target_pairs={{1,3},{3,5},{5,7},{7,9},{9,11},{11,13},{13,15},{15,17},{17,19},{19... | collective-permute-start | bytes 196616 | tf_op jit(solution)/shard_map/ppermute | solution.py:471
  56.8 1.8 %collective-permute-start.2 = (bf16[128,1024]{1,0:T(8,128)(2,1)S(1)}, bf16[128,1024]{1,0:T(8,128)(2,1)S(1)}, u32[]{:S(2)}, u32[]{:S(2)}) collective-permute-start(bf16[128,1024]{1,0:T(8,128)(2,1)S(1)} %pad_maximum_fusion.refs_0_), channel_id=1, source_target_pairs={{0,6},{1,7},{2,0},{3,1},{4,2},{5,3},{6,4},{7,5},{8,14},{9,15},{10,... | collective-permute-start | bytes 786440 | tf_op jit(solution)/shard_map/ppermute | solution.py:415
  62.4 1.6 %collective-permute-done.1.refs_1_ = bf16[128,1024]{1,0:T(8,128)(2,1)S(1)} collective-permute-done((bf16[128,1024]{1,0:T(8,128)(2,1)S(1)}, bf16[128,1024]{1,0:T(8,128)(2,1)S(1)}, u32[]{:S(2)}, u32[]{:S(2)}) %collective-permute-start.1) | collective-permute-done | bytes 262176 | tf_op jit(solution)/shard_map/ppermute | solution.py:415
  64.8 5.1 %collective-permute-done.3.refs_3_ = bf16[128,1024]{1,0:T(8,128)(2,1)S(1)} collective-permute-done((bf16[128,1024]{1,0:T(8,128)(2,1)S(1)}, bf16[128,1024]{1,0:T(8,128)(2,1)S(1)}, u32[]{:S(2)}, u32[]{:S(2)}) %collective-permute-start.3) | collective-permute-done | bytes 262176 | tf_op jit(solution)/shard_map/ppermute | solution.py:415
  73.7 10.0 %collective-permute-start.13 = (bf16[288,128]{1,0:T(8,128)(2,1)S(1)}, bf16[288,128]{1,0:T(8,128)(2,1)S(1)}, u32[]{:S(2)}, u32[]{:S(2)}) collective-permute-start(bf16[288,128]{1,0:T(8,128)(2,1)S(1)} %get-tuple-element.38), channel_id=1, source_target_pairs={{0,24},{1,25},{2,26},{3,27},{4,28},{5,29},{6,30},{7,31},{8,0},{9,1... | collective-permute-start | bytes 221192 | tf_op jit(solution)/shard_map/ppermute | solution.py:415
  85.9 2.5 %collective-permute-done.14 = bf16[288,128]{1,0:T(8,128)(2,1)S(1)} collective-permute-done((bf16[288,128]{1,0:T(8,128)(2,1)S(1)}, bf16[288,128]{1,0:T(8,128)(2,1)S(1)}, u32[]{:S(2)}, u32[]{:S(2)}) %collective-permute-start.14) | collective-permute-done | bytes 73760 | tf_op jit(solution)/shard_map/ppermute | solution.py:415
  88.5 7.0 %collective-permute-start.15 = (bf16[288,128]{1,0:T(8,128)(2,1)S(1)}, bf16[288,128]{1,0:T(8,128)(2,1)S(1)}, u32[]{:S(2)}, u32[]{:S(2)}) collective-permute-start(bf16[288,128]{1,0:T(8,128)(2,1)S(1)} %add_convert_fusion.3), channel_id=1, source_target_pairs={{0,32},{32,0},{64,96},{96,64},{128,160},{160,128},{192,224},{224,1... | collective-permute-start | bytes 221192 | tf_op jit(solution)/shard_map/ppermute | solution.py:497
  97.2 3.2 %collective-permute-start.16 = (bf16[288,128]{1,0:T(8,128)(2,1)S(1)}, bf16[288,128]{1,0:T(8,128)(2,1)S(1)}, u32[]{:S(2)}, u32[]{:S(2)}) collective-permute-start(bf16[288,128]{1,0:T(8,128)(2,1)S(1)} %add_convert_fusion.2), channel_id=1, source_target_pairs={{0,64},{32,96},{64,128},{96,160},{128,192},{160,224},{192,0},{224,... | collective-permute-start | bytes 221192 | tf_op jit(solution)/shard_map/ppermute | solution.py:430
  101.4 3.2 %collective-permute-start.18 = (bf16[288,128]{1,0:T(8,128)(2,1)S(1)}, bf16[288,128]{1,0:T(8,128)(2,1)S(1)}, u32[]{:S(2)}, u32[]{:S(2)}) collective-permute-start(bf16[288,128]{1,0:T(8,128)(2,1)S(1)} %add_convert_fusion.2), channel_id=1, source_target_pairs={{0,128},{32,160},{64,192},{96,224},{128,0},{160,32},{192,64},{224,... | collective-permute-start | bytes 221192 | tf_op jit(solution)/shard_map/ppermute | solution.py:430
  104.6 2.4 %convolution_add_fusion = f32[64,1024]{1,0:T(8,128)} fusion(f32[64,1024]{1,0:T(8,128)S(1)} %fusion.5, bf16[64,512]{1,0:T(8,128)(2,1)S(1)} %get-tuple-element.22, bf16[1024,512]{1,0:T(8,128)(2,1)} %param.15), kind=kOutput, calls=%fused_computation | convolution fusion | flops 67174400 | bytes 1638400 | tf_op jit(solution)/shard_map/dot_general | solution.py:479
  107.0 1.6 %collective-permute-done.18 = bf16[288,128]{1,0:T(8,128)(2,1)S(1)} collective-permute-done((bf16[288,128]{1,0:T(8,128)(2,1)S(1)}, bf16[288,128]{1,0:T(8,128)(2,1)S(1)}, u32[]{:S(2)}, u32[]{:S(2)}) %collective-permute-start.18) | collective-permute-done | bytes 73760 | tf_op jit(solution)/shard_map/ppermute | solution.py:430
  113.3 3.3 %collective-permute-done.21 = bf16[288,128]{1,0:T(8,128)(2,1)S(1)} collective-permute-done((bf16[288,128]{1,0:T(8,128)(2,1)S(1)}, bf16[288,128]{1,0:T(8,128)(2,1)S(1)}, u32[]{:S(2)}, u32[]{:S(2)}) %collective-permute-start.21) | collective-permute-done | bytes 73760 | tf_op jit(solution)/shard_map/ppermute | solution.py:415
  116.7 2.7 %collective-permute-start.23 = (bf16[1152,128]{1,0:T(8,128)(2,1)S(1)}, bf16[1152,128]{1,0:T(8,128)(2,1)S(1)}, u32[]{:S(2)}, u32[]{:S(2)}) collective-permute-start(bf16[1152,128]{1,0:T(8,128)(2,1)S(1)} %constant_dynamic-update-slice_fusion.refs_1_), channel_id=1, source_target_pairs={{0,6},{1,7},{2,0},{3,1},{4,2},{5,3},{6,4},{7,5},{8,14},{9,15},{10,... | collective-permute-start | bytes 884744 | tf_op jit(solution)/shard_map/ppermute | solution.py:415
  119.3 10.9 %collective-permute-start.25 = (bf16[1152,128]{1,0:T(8,128)(2,1)S(1)}, bf16[1152,128]{1,0:T(8,128)(2,1)S(1)}, u32[]{:S(2)}, u32[]{:S(2)}) collective-permute-start(bf16[1152,128]{1,0:T(8,128)(2,1)S(1)} %constant_dynamic-update-slice_fusion.refs_1_), channel_id=1, source_target_pairs={{0,1},{1,0},{2,3},{3,2},{4,5},{5,4},{6,7},{7,6},{8,9},{9,8},{10,11... | collective-permute-start | bytes 884744 | tf_op jit(solution)/shard_map/ppermute | solution.py:415
  130.3 4.7 %collective-permute-start.26 = (bf16[1152,128]{1,0:T(8,128)(2,1)S(1)}, bf16[1152,128]{1,0:T(8,128)(2,1)S(1)}, u32[]{:S(2)}, u32[]{:S(2)}) collective-permute-start(bf16[1152,128]{1,0:T(8,128)(2,1)S(1)} %collective-permute-done.22.refs_2_), channel_id=1, source_target_pairs={{0,1},{1,0},{2,3},{3,2},{4,5},{5,4},{6,7},{7,6},{8,9},{9,8},{10,11... | collective-permute-start | bytes 884744 | tf_op jit(solution)/shard_map/ppermute | solution.py:415
  135.0 2.7 %collective-permute-start.27 = (bf16[1152,128]{1,0:T(8,128)(2,1)S(1)}, bf16[1152,128]{1,0:T(8,128)(2,1)S(1)}, u32[]{:S(2)}, u32[]{:S(2)}) collective-permute-start(bf16[1152,128]{1,0:T(8,128)(2,1)S(1)} %collective-permute-done.23.refs_3_), channel_id=1, source_target_pairs={{0,1},{1,0},{2,3},{3,2},{4,5},{5,4},{6,7},{7,6},{8,9},{9,8},{10,11... | collective-permute-start | bytes 884744 | tf_op jit(solution)/shard_map/ppermute | solution.py:415
  139.7 3.4 %finish.1 = (f32[1024,512]{1,0:T(8,128)}, f32[1024,512]{1,0:T(8,128)}, f32[512,128]{1,0:T(8,128)}, f32[1,512]{1,0:T(1,128)}, f32[1,128]{1,0:T(1,128)}) custom-call(s32[3]{0:T(128)S(1)} %pad_add_fusion.refs_0_, bf16[1152,128]{1,0:T(8,128)(2,1)S(1)} %constant_dynamic-update-slice_fusion.refs_1_, bf16[1152,128]{1,0:T(8,128)(2,1)S(1)} %collective-permute-done.22.refs_2_, ...), custom_call_target="tpu_custom_call" | custom-call | tf_op jit(solution)/shard_map/finish/pallas_call | solution.py:509
  (82 shorter events, 27.8 us)
Async XLA Ops:
  4.8 31.0 %all-to-all-start = ((bf16[32,24,512]{2,1,0:T(8,128)(2,1)}), bf16[32,24,512]{2,1,0:T(8,128)(2,1)S(1)}, u32[]{:S(2)}, u32[]{:S(2)}) async-start(bf16[32,24,512]{2,1,0:T(8,128)(2,1)} %bitcast.6), calls=%async_computation | async-start | bytes 1572864 | tf_op jit(solution)/shard_map/all_to_all | solution.py:440
  13.9 11.6 %collective-permute-start.4 = (bf16[80,512]{1,0:T(8,128)(2,1)S(1)}, bf16[80,512]{1,0:T(8,128)(2,1)S(1)}, u32[]{:S(2)}, u32[]{:S(2)}) collective-permute-start(bf16[80,512]{1,0:T(8,128)(2,1)S(1)} %fusion.2.right_m), channel_id=1, source_target_pairs={{0,31},{1,2},{2,1},{3,4},{4,3},{5,6},{6,5},{7,8},{8,7},{9,10},{10,... | collective-permute-start | bytes 245768 | tf_op jit(solution)/shard_map/ppermute | solution.py:415
  15.6 9.9 %collective-permute-start.5 = (bf16[80,512]{1,0:T(8,128)(2,1)S(1)}, bf16[80,512]{1,0:T(8,128)(2,1)S(1)}, u32[]{:S(2)}, u32[]{:S(2)}) collective-permute-start(bf16[80,512]{1,0:T(8,128)(2,1)S(1)} %fusion.2.right_m), channel_id=1, source_target_pairs={{0,1},{1,0},{2,3},{3,2},{4,5},{5,4},{6,7},{7,6},{8,9},{9,8},{10,11... | collective-permute-start | bytes 245768 | tf_op jit(solution)/shard_map/ppermute | solution.py:415
  48.7 11.2 %collective-permute-start.6 = (bf16[256,512]{1,0:T(8,128)(2,1)S(1)}, bf16[256,512]{1,0:T(8,128)(2,1)S(1)}, u32[]{:S(2)}, u32[]{:S(2)}) collective-permute-start(bf16[256,512]{1,0:T(8,128)(2,1)S(1)} %get-tuple-element.24), channel_id=1, source_target_pairs={{0,1},{1,0},{2,3},{3,2},{4,5},{5,4},{6,7},{7,6},{8,9},{9,8},{10,11... | collective-permute-start | bytes 786440 | tf_op jit(solution)/shard_map/ppermute | solution.py:415
  50.0 5.8 %collective-permute-start = (bf16[64,1024]{1,0:T(8,128)(2,1)S(1)}, bf16[64,1024]{1,0:T(8,128)(2,1)S(1)}, u32[]{:S(2)}, u32[]{:S(2)}) collective-permute-start(bf16[64,1024]{1,0:T(8,128)(2,1)S(1)} %bitcast.28), channel_id=1, source_target_pairs={{0,1},{1,0},{2,3},{3,2},{4,5},{5,4},{6,7},{7,6},{8,9},{9,8},{10,11... | collective-permute-start | bytes 393224 | tf_op jit(solution)/shard_map/ppermute | solution.py:415
  50.1 8.5 %collective-permute-start.7 = (bf16[64,512]{1,0:T(8,128)(2,1)S(1)}, bf16[64,512]{1,0:T(8,128)(2,1)S(1)}, u32[]{:S(2)}, u32[]{:S(2)}) collective-permute-start(bf16[64,512]{1,0:T(8,128)(2,1)S(1)} %get-tuple-element.25), channel_id=1, source_target_pairs={{0,31},{1,2},{2,1},{3,4},{4,3},{5,6},{6,5},{7,8},{8,7},{9,10},{10,... | collective-permute-start | bytes 196616 | tf_op jit(solution)/shard_map/ppermute | solution.py:415
  51.6 8.3 %collective-permute-start.8 = (bf16[64,512]{1,0:T(8,128)(2,1)S(1)}, bf16[64,512]{1,0:T(8,128)(2,1)S(1)}, u32[]{:S(2)}, u32[]{:S(2)}) collective-permute-start(bf16[64,512]{1,0:T(8,128)(2,1)S(1)} %get-tuple-element.25), channel_id=1, source_target_pairs={{1,3},{3,5},{5,7},{7,9},{9,11},{11,13},{13,15},{15,17},{17,19},{19... | collective-permute-start | bytes 196616 | tf_op jit(solution)/shard_map/ppermute | solution.py:471
  55.8 8.1 %collective-permute-start.1 = (bf16[128,1024]{1,0:T(8,128)(2,1)S(1)}, bf16[128,1024]{1,0:T(8,128)(2,1)S(1)}, u32[]{:S(2)}, u32[]{:S(2)}) collective-permute-start(bf16[128,1024]{1,0:T(8,128)(2,1)S(1)} %pad_maximum_fusion.refs_0_), channel_id=1, source_target_pairs={{0,2},{1,3},{2,4},{3,5},{4,6},{5,7},{6,0},{7,1},{8,10},{9,11},{10,... | collective-permute-start | bytes 786440 | tf_op jit(solution)/shard_map/ppermute | solution.py:415
  56.8 8.0 %collective-permute-start.2 = (bf16[128,1024]{1,0:T(8,128)(2,1)S(1)}, bf16[128,1024]{1,0:T(8,128)(2,1)S(1)}, u32[]{:S(2)}, u32[]{:S(2)}) collective-permute-start(bf16[128,1024]{1,0:T(8,128)(2,1)S(1)} %pad_maximum_fusion.refs_0_), channel_id=1, source_target_pairs={{0,6},{1,7},{2,0},{3,1},{4,2},{5,3},{6,4},{7,5},{8,14},{9,15},{10,... | collective-permute-start | bytes 786440 | tf_op jit(solution)/shard_map/ppermute | solution.py:415
  58.6 11.4 %collective-permute-start.3 = (bf16[128,1024]{1,0:T(8,128)(2,1)S(1)}, bf16[128,1024]{1,0:T(8,128)(2,1)S(1)}, u32[]{:S(2)}, u32[]{:S(2)}) collective-permute-start(bf16[128,1024]{1,0:T(8,128)(2,1)S(1)} %pad_maximum_fusion.refs_0_), channel_id=1, source_target_pairs={{0,4},{1,5},{2,6},{3,7},{4,0},{5,1},{6,2},{7,3},{8,12},{9,13},{10,... | collective-permute-start | bytes 786440 | tf_op jit(solution)/shard_map/ppermute | solution.py:415
  60.1 11.4 %collective-permute-start.10 = (bf16[256,128]{1,0:T(8,128)(2,1)S(1)}, bf16[256,128]{1,0:T(8,128)(2,1)S(1)}, u32[]{:S(2)}, u32[]{:S(2)}) collective-permute-start(bf16[256,128]{1,0:T(8,128)(2,1)S(1)} %get-tuple-element.40), channel_id=1, source_target_pairs={{0,6},{1,7},{2,0},{3,1},{4,2},{5,3},{6,4},{7,5},{8,14},{9,15},{10,... | collective-permute-start | bytes 196616 | tf_op jit(solution)/shard_map/ppermute | solution.py:415
  61.0 10.6 %collective-permute-start.11 = (bf16[256,128]{1,0:T(8,128)(2,1)S(1)}, bf16[256,128]{1,0:T(8,128)(2,1)S(1)}, u32[]{:S(2)}, u32[]{:S(2)}) collective-permute-start(bf16[256,128]{1,0:T(8,128)(2,1)S(1)} %get-tuple-element.39), channel_id=1, source_target_pairs={{0,4},{1,5},{2,6},{3,7},{4,0},{5,1},{6,2},{7,3},{8,12},{9,13},{10,... | collective-permute-start | bytes 196616 | tf_op jit(solution)/shard_map/ppermute | solution.py:415
  64.0 9.1 %collective-permute-start.9 = (bf16[256,128]{1,0:T(8,128)(2,1)S(1)}, bf16[256,128]{1,0:T(8,128)(2,1)S(1)}, u32[]{:S(2)}, u32[]{:S(2)}) collective-permute-start(bf16[256,128]{1,0:T(8,128)(2,1)S(1)} %get-tuple-element.41), channel_id=1, source_target_pairs={{0,2},{1,3},{2,4},{3,5},{4,6},{5,7},{6,0},{7,1},{8,10},{9,11},{10,... | collective-permute-start | bytes 196616 | tf_op jit(solution)/shard_map/ppermute | solution.py:415
  73.6 12.3 %collective-permute-start.12 = (bf16[288,128]{1,0:T(8,128)(2,1)S(1)}, bf16[288,128]{1,0:T(8,128)(2,1)S(1)}, u32[]{:S(2)}, u32[]{:S(2)}) collective-permute-start(bf16[288,128]{1,0:T(8,128)(2,1)S(1)} %get-tuple-element.36), channel_id=1, source_target_pairs={{0,8},{1,9},{2,10},{3,11},{4,12},{5,13},{6,14},{7,15},{8,16},{9,17... | collective-permute-start | bytes 221192 | tf_op jit(solution)/shard_map/ppermute | solution.py:415
  73.7 12.2 %collective-permute-start.13 = (bf16[288,128]{1,0:T(8,128)(2,1)S(1)}, bf16[288,128]{1,0:T(8,128)(2,1)S(1)}, u32[]{:S(2)}, u32[]{:S(2)}) collective-permute-start(bf16[288,128]{1,0:T(8,128)(2,1)S(1)} %get-tuple-element.38), channel_id=1, source_target_pairs={{0,24},{1,25},{2,26},{3,27},{4,28},{5,29},{6,30},{7,31},{8,0},{9,1... | collective-permute-start | bytes 221192 | tf_op jit(solution)/shard_map/ppermute | solution.py:415
  88.5 8.7 %collective-permute-start.15 = (bf16[288,128]{1,0:T(8,128)(2,1)S(1)}, bf16[288,128]{1,0:T(8,128)(2,1)S(1)}, u32[]{:S(2)}, u32[]{:S(2)}) collective-permute-start(bf16[288,128]{1,0:T(8,128)(2,1)S(1)} %add_convert_fusion.3), channel_id=1, source_target_pairs={{0,32},{32,0},{64,96},{96,64},{128,160},{160,128},{192,224},{224,1... | collective-permute-start | bytes 221192 | tf_op jit(solution)/shard_map/ppermute | solution.py:497
  97.2 9.8 %collective-permute-start.16 = (bf16[288,128]{1,0:T(8,128)(2,1)S(1)}, bf16[288,128]{1,0:T(8,128)(2,1)S(1)}, u32[]{:S(2)}, u32[]{:S(2)}) collective-permute-start(bf16[288,128]{1,0:T(8,128)(2,1)S(1)} %add_convert_fusion.2), channel_id=1, source_target_pairs={{0,64},{32,96},{64,128},{96,160},{128,192},{160,224},{192,0},{224,... | collective-permute-start | bytes 221192 | tf_op jit(solution)/shard_map/ppermute | solution.py:430
  100.4 6.6 %collective-permute-start.17 = (bf16[288,128]{1,0:T(8,128)(2,1)S(1)}, bf16[288,128]{1,0:T(8,128)(2,1)S(1)}, u32[]{:S(2)}, u32[]{:S(2)}) collective-permute-start(bf16[288,128]{1,0:T(8,128)(2,1)S(1)} %add_convert_fusion.2), channel_id=1, source_target_pairs={{0,192},{32,224},{64,0},{96,32},{128,64},{160,96},{192,128},{224,1... | collective-permute-start | bytes 221192 | tf_op jit(solution)/shard_map/ppermute | solution.py:430
  101.4 7.2 %collective-permute-start.18 = (bf16[288,128]{1,0:T(8,128)(2,1)S(1)}, bf16[288,128]{1,0:T(8,128)(2,1)S(1)}, u32[]{:S(2)}, u32[]{:S(2)}) collective-permute-start(bf16[288,128]{1,0:T(8,128)(2,1)S(1)} %add_convert_fusion.2), channel_id=1, source_target_pairs={{0,128},{32,160},{64,192},{96,224},{128,0},{160,32},{192,64},{224,... | collective-permute-start | bytes 221192 | tf_op jit(solution)/shard_map/ppermute | solution.py:430
  116.6 13.7 %collective-permute-start.22 = (bf16[1152,128]{1,0:T(8,128)(2,1)S(1)}, bf16[1152,128]{1,0:T(8,128)(2,1)S(1)}, u32[]{:S(2)}, u32[]{:S(2)}) collective-permute-start(bf16[1152,128]{1,0:T(8,128)(2,1)S(1)} %constant_dynamic-update-slice_fusion.refs_1_), channel_id=1, source_target_pairs={{0,2},{1,3},{2,4},{3,5},{4,6},{5,7},{6,0},{7,1},{8,10},{9,11},{10,... | collective-permute-start | bytes 884744 | tf_op jit(solution)/shard_map/ppermute | solution.py:415
  116.7 18.3 %collective-permute-start.23 = (bf16[1152,128]{1,0:T(8,128)(2,1)S(1)}, bf16[1152,128]{1,0:T(8,128)(2,1)S(1)}, u32[]{:S(2)}, u32[]{:S(2)}) collective-permute-start(bf16[1152,128]{1,0:T(8,128)(2,1)S(1)} %constant_dynamic-update-slice_fusion.refs_1_), channel_id=1, source_target_pairs={{0,6},{1,7},{2,0},{3,1},{4,2},{5,3},{6,4},{7,5},{8,14},{9,15},{10,... | collective-permute-start | bytes 884744 | tf_op jit(solution)/shard_map/ppermute | solution.py:415
  119.3 18.3 %collective-permute-start.24 = (bf16[1152,128]{1,0:T(8,128)(2,1)S(1)}, bf16[1152,128]{1,0:T(8,128)(2,1)S(1)}, u32[]{:S(2)}, u32[]{:S(2)}) collective-permute-start(bf16[1152,128]{1,0:T(8,128)(2,1)S(1)} %constant_dynamic-update-slice_fusion.refs_1_), channel_id=1, source_target_pairs={{0,4},{1,5},{2,6},{3,7},{4,0},{5,1},{6,2},{7,3},{8,12},{9,13},{10,... | collective-permute-start | bytes 884744 | tf_op jit(solution)/shard_map/ppermute | solution.py:415
  119.3 19.2 %collective-permute-start.25 = (bf16[1152,128]{1,0:T(8,128)(2,1)S(1)}, bf16[1152,128]{1,0:T(8,128)(2,1)S(1)}, u32[]{:S(2)}, u32[]{:S(2)}) collective-permute-start(bf16[1152,128]{1,0:T(8,128)(2,1)S(1)} %constant_dynamic-update-slice_fusion.refs_1_), channel_id=1, source_target_pairs={{0,1},{1,0},{2,3},{3,2},{4,5},{5,4},{6,7},{7,6},{8,9},{9,8},{10,11... | collective-permute-start | bytes 884744 | tf_op jit(solution)/shard_map/ppermute | solution.py:415
  130.3 8.3 %collective-permute-start.26 = (bf16[1152,128]{1,0:T(8,128)(2,1)S(1)}, bf16[1152,128]{1,0:T(8,128)(2,1)S(1)}, u32[]{:S(2)}, u32[]{:S(2)}) collective-permute-start(bf16[1152,128]{1,0:T(8,128)(2,1)S(1)} %collective-permute-done.22.refs_2_), channel_id=1, source_target_pairs={{0,1},{1,0},{2,3},{3,2},{4,5},{5,4},{6,7},{7,6},{8,9},{9,8},{10,11... | collective-permute-start | bytes 884744 | tf_op jit(solution)/shard_map/ppermute | solution.py:415
  (13 other events, 113.6 us)

commit v4 on v2

--- a/solution.py
+++ b/solution.py
@@ -84,6 +84,8 @@
     out_keep,
     out_sent,
     todo,
+    panels_s,
+    sems,
     left_s,
     right_s,
     tsum_s,
@@ -98,7 +100,14 @@
 ):
     hidden = left_ref.shape[1]
     tile = ROWS * PANEL
+    loads = [
+        pltpu.make_async_copy(ref.at[0:PANEL, :], panels_s.at[n], sems.at[n])
+        for n, ref in enumerate((left_ref, right_o, right_m, right_p))
+    ]
+    for copy in loads:
+        copy.start()
     iota = lambda shape, axis: lax.broadcasted_iota(jnp.int32, shape, axis)
+
     def scan(i, n):
         k, rt = i // 8, i % 8
         meets = (ids_s[1, rt * ROWS] <= ids_s[k, PANEL - 1]) & (ids_s[k, 0] <= ids_s[1, rt * ROWS + ROWS - 1])
@@ -108,10 +117,6 @@
     n_todo = lax.fori_loop(0, 24, scan, 0)
     for extra in range(3):
         todo[n_todo + extra] = 24
-    left_s[...] = (left_ref[...].astype(F32) + bias_ref[...]) * 0.5
-    for k, ref in enumerate((right_o, right_m, right_p)):
-        right_s[k * PANEL : (k + 1) * PANEL, :] = ref[0:PANEL, :].astype(F32) * 0.5
-    right_s[3 * PANEL :, :] = jnp.zeros((PANEL, hidden), F32)
     half_s[...] = (wmt_ref[...].astype(F32) * 0.5).T.astype(BF)
     n_src = targets_ref.shape[0]
     tsum = jnp.dot(
@@ -141,7 +146,13 @@
     racc[...] = jnp.zeros_like(racc)
     mid_acc[...] = jnp.zeros_like(mid_acc)
     fin_acc[...] = jnp.zeros_like(fin_acc)
+    for copy in loads:
+        copy.wait()
+    left_s[...] = (panels_s[0].astype(F32) + bias_ref[...]) * 0.5
+    for k in range(3):
+        right_s[k * PANEL : (k + 1) * PANEL, :] = panels_s[k + 1].astype(F32) * 0.5
     rest = (tsum_s, mask_s, half_s, wmt_ref, wf_ref, lacc, racc, mid_acc, fin_acc)
+
     def step(i, carry):
         forward(todo[i], left_s, right_s, hid_s, slope_s)
         backward(todo[i], hid_s, slope_s, *rest)
@@ -195,12 +206,17 @@
             jax.ShapeDtypeStruct((upper, hidden), BF),
             jax.ShapeDtypeStruct((2 * PANEL + upper, hidden), BF),
         ),
-        in_specs=[pl.BlockSpec(memory_space=pltpu.SMEM)] * 2 + [vmem] * 9,
+        in_specs=[pl.BlockSpec(memory_space=pltpu.SMEM)] * 2
+        + [vmem]
+        + [pl.BlockSpec(memory_space=pltpu.HBM)] * 4
+        + [vmem] * 4,
         out_specs=(vmem,) * 5,
         scratch_shapes=[
             pltpu.SMEM((32,), jnp.int32),
+            pltpu.VMEM((4, PANEL, hidden), BF),
+            pltpu.SemaphoreType.DMA((4,)),
             pltpu.VMEM((PANEL, hidden), F32),
-            pltpu.VMEM((4 * PANEL, hidden), F32),
+            pltpu.VMEM((3 * PANEL, hidden), F32),
             pltpu.VMEM((49, 8, tile), F32),
             pltpu.VMEM((25, 8, tile), F32),
             pltpu.VMEM((hidden, upper), BF),
@@ -216,7 +232,7 @@
             flops=10 * 24 * tile * hidden * upper, bytes_accessed=2 << 20, transcendentals=24 * tile * hidden
         ),
         name="pair_grads",
-    )(core, ids_s, ids, left, right_o, right_m, right_p, targets, bias, wmt, wf)
+    )(core, ids_s, ids, *[pltpu.with_memory_space_constraint(v, pltpu.HBM) for v in (left, right_o, right_m, right_p)], targets, bias, wmt, wf)
 
 
 def send_kernel(blocks, live, targets_ref, out_ref, acc):
@@ -256,6 +272,35 @@
         compiler_params=pltpu.CompilerParams(vmem_limit_bytes=8 << 20),
         name="send_targets",
     )(blocks, live, targets)
+
+
+def slice_kernel(*refs):
+    embs, parts, out = refs[:4], refs[4:8], refs[8]
+    depth = embs[0].shape[1]
+    rows = embs[0].shape[0]
+    total = extra = None
+    for emb, part in zip(embs, parts):
+        term = lax.dot_general(
+            emb[...], part[0:rows, :], (((0,), (0,)), ((), ())), preferred_element_type=F32
+        )
+        more = part[rows:, :].astype(F32)
+        total = term if total is None else total + term
+        extra = more if extra is None else extra + more
+    out[0:depth, :] = total.astype(BF)
+    out[depth:, :] = extra.astype(BF)
+
+
+def weight_slice(embs, parts):
+    rows, depth = embs[0].shape
+    vmem = pl.BlockSpec(memory_space=pltpu.VMEM)
+    return pl.pallas_call(
+        slice_kernel,
+        out_shape=jax.ShapeDtypeStruct((depth + parts[0].shape[0] - rows, parts[0].shape[1]), BF),
+        in_specs=[vmem] * 8,
+        out_specs=vmem,
+        compiler_params=pltpu.CompilerParams(vmem_limit_bytes=16 << 20),
+        name="weight_slice",
+    )(*embs, *parts)
 
 
 ORDER = (0, 1, 3, 2)
@@ -328,19 +373,24 @@
         return lax.ppermute(value, "grp", [(i, (i + d) % groups) for i in range(groups)])
 
     sums = send_targets(block_list[0], block_counts, pair_targets[0], panels).reshape(panels, 24, ROWS * PANEL)
-    sums, emb, ids = lax.optimization_barrier((sums, emb, cluster_ids[0]))
-    with jax.named_scope("to_owner"):
-        targets = lax.all_to_all(sums, "blk", 0, 0, tiled=True)
+    targets = lax.all_to_all(sums, "blk", 0, 0, tiled=True)
     targets = targets.reshape(24 * panels, ROWS * PANEL)
 
-    left = jnp.dot(emb, w_left, preferred_element_type=F32).astype(BF)
     right = jnp.dot(emb, w_right, preferred_element_type=F32).astype(BF)
-    ids = ids.astype(BF)
+    ids = cluster_ids[0].astype(BF)
     ids_row = jnp.pad(ids[None, :], ((0, 15), (0, hidden - PANEL)))
     right_own = jnp.concatenate([right, ids_row], axis=0)
     right_outer = on_outer(right_own)
     right_partner = on_core(right_own)
+
+    left = jnp.dot(emb, w_left, preferred_element_type=F32).astype(BF)
     col_ids = jnp.stack([right_outer[PANEL, :PANEL], ids, right_partner[PANEL, :PANEL]])
+
+    emb_pair = jnp.concatenate([emb, on_core(emb)], axis=0)
+    embs = [emb_pair]
+    for d in ORDER[1:]:
+        embs.append(on_x(emb_pair, d))
+
     lg, r_outer, r_own, keep, sent = pair_grads(
         core[None],
         col_ids.astype(jnp.int32),
@@ -354,9 +404,6 @@
         w_middle.T,
         w_final[:, None],
     )
-
-    emb_pair = jnp.concatenate([emb, on_core(emb)], axis=0)
-    emb_all = jnp.concatenate([emb_pair] + [on_x(emb_pair, d) for d in ORDER[1:]], axis=0)
 
     first = core == 0
     got = on_core(sent)
@@ -377,10 +424,7 @@
         return lax.dynamic_slice_in_dim(both, ((x + d) & 3) * 128, 128, 1)
 
     parts = [column(0)] + [on_x(column(d), d) for d in ORDER[1:]]
-    grads = jnp.concatenate([p[: 2 * PANEL] for p in parts], axis=0)
-    weight = lax.dot_general(emb_all, grads, (((0,), (0,)), ((), ())), preferred_element_type=F32)
-    extra = sum(p[2 * PANEL :].astype(F32) for p in parts)
-    total = jnp.concatenate([weight, extra], axis=0).astype(BF)
+    total = weight_slice(embs, parts)
     piece = total.shape[0] // 4
 
     def rows(d):
@@ -393,6 +437,7 @@
         + lax.ppermute(total, "grp", [(i, i ^ 1) for i in range(groups)]).astype(F32)
     ).astype(BF)
     total = sum(p.astype(F32) for p in [total] + [on_z(total, d) for d in (2, 6, 4)]).astype(BF)
+    total, grad_local = lax.optimization_barrier((total, grad_local))
 
     total = jnp.concatenate([total] + [on_y(total, d) for d in ORDER[1:]], axis=0)
     mine = [total] + [on_x(total, d) for d in ORDER[1:]]

time: 127 us -> 124 us (0.976)
  starting transfers between devices: 74.8 us -> 62.6 us
  waiting for transfers between devices: 23.5 us -> 32.4 us
  local copies, waits for them, and re-layouts: 8.14 us -> 2.07 us
  Pallas kernels: 14.5 us -> 18.9 us
  matrix products: 2.66 us -> 5.23 us
    ppermute x24, waiting for transfers between devices: 12.7 us -> 22.8 us  [blk(): return lax.ppermute(value, 'blk', [(i, partner(i)) for i in range(panels)])]
    ppermute x24, starting transfers between devices: 48 us -> 41.4 us  [blk(): return lax.ppermute(value, 'blk', [(i, partner(i)) for i in range(panels)])]
    ppermute x3, starting transfers between devices: 10 us -> 5.91 us  [on_z(): lax.ppermute(value, 'grp', [(i, (i + d) % groups) for i in range(groups)])]
    pallas_call x1, Pallas kernels: 9.29 us -> 13.4 us  [pair_grads(): pl.pallas_call(pair_kernel, out_shape=(panel, panel, panel, jax.ShapeDtyp...]
    unnamed x20 -> x24, local copies, waits for them, and re-layouts: 4.61 us -> 1.1 us
    all_to_all x1, waiting for transfers between devices: 0.01 us -> 2.88 us  [local(): targets = lax.all_to_all(sums, 'blk', 0, 0, tiled=True)]
    concatenate x2 -> x1, local copies, waits for them, and re-layouts: 2.6 us -> 0.02 us  [local(): jnp.concatenate([total] + [on_y(total, d) for d in ORDER[1:]], axis=0)]
    ppermute x1, waiting for transfers between devices: 4.81 us -> 2.34 us  [local(): lax.ppermute(r_outer, 'blk', [(i, (i + 2) % panels) for i in range(1, pan...]
  transfers between devices with their start and end apart: 30 -> 30, of which waited for: 11 -> 11; matrix products, arithmetic and copies ran while one was open for 7% -> 5% of each run, Pallas kernels for 7% -> 0%
where the time goes in v4:
time: 124 us; the launch traced here: 123 us
  starting transfers between devices  62.6 us (50%)
  waiting for transfers between devices  32.4 us (26%)
  Pallas kernels  18.9 us (15%)
  matrix products  5.23 us (4%)
  local copies, waits for them, and re-layouts  2.07 us (2%)
  between operations  1.69 us (1%)
    ppermute x24, starting transfers between devices, blk(): return lax.ppermute(value, 'blk', [(i, partner(i)) for i in range(panels)])  41.4 us
    ppermute x24, waiting for transfers between devices, blk(): return lax.ppermute(value, 'blk', [(i, partner(i)) for i in range(panels)])  22.8 us
    pallas_call x1, Pallas kernels, pair_grads(): pl.pallas_call(pair_kernel, out_shape=(panel, panel, panel, jax.ShapeDtyp...  13.4 us
    all_to_all x1, starting transfers between devices, local(): targets = lax.all_to_all(sums, 'blk', 0, 0, tiled=True)  8.75 us
    ppermute x3, starting transfers between devices, on_z(): lax.ppermute(value, 'grp', [(i, (i + d) % groups) for i in range(groups)])  5.91 us
    ppermute x1, starting transfers between devices, local(): lax.ppermute(total, 'grp', [(i, i ^ 1) for i in range(groups)]).astype(F32)  4.02 us
    pallas_call x1, Pallas kernels, local(): pl.pallas_call(lambda *refs: finish_kernel(scale, *refs), grid=(4,), out_...  3.38 us
    ppermute x3, waiting for transfers between devices, on_z(): lax.ppermute(value, 'grp', [(i, (i + d) % groups) for i in range(groups)])  3.1 us
  transfers between devices with their start and end apart: 30, of which 11 were waited for; matrix products, arithmetic and copies ran while one was open for 5% of the time, Pallas kernels for 0%

profile of v4, /device:TPU:1, one launch (start us, length us, event | category | flops | bytes accessed | tf_op | source)
XLA Modules:
  0.0 123.3 jit_solution(1333575204122024915)
XLA Ops:
  3.1 1.7 %send_targets.1 = bf16[768,512]{1,0:T(8,128)(2,1)} custom-call(s32[8,2]{1,0:T(8,128)S(1)} %copy.16.blocks, s32[1,1]{1,0:T(1,128)S(6)} %copy.22.live, f32[8,4096]{1,0:T(8,128)S(1)} %bitcast.24), custom_call_target="tpu_custom_call" | custom-call | tf_op jit(solution)/shard_map/send_targets/pallas_call | solution.py:266
  4.8 8.8 %all-to-all-start = ((bf16[32,24,512]{2,1,0:T(8,128)(2,1)}), bf16[32,24,512]{2,1,0:T(8,128)(2,1)S(1)}, u32[]{:S(2)}, u32[]{:S(2)}) async-start(bf16[32,24,512]{2,1,0:T(8,128)(2,1)} %bitcast.4), calls=%async_computation | async-start | bytes 1572864 | tf_op jit(solution)/shard_map/all_to_all | solution.py:376
  15.7 2.1 %convolution_convert_fusion.left_ref = bf16[64,512]{1,0:T(8,128)(2,1)} fusion(bf16[1024,512]{1,0:T(8,128)(2,1)} %param.15, bf16[1,64,1024]{2,1,0:T(8,128)(2,1)S(1)} %copy-done.3), kind=kOutput, calls=%fused_computation.1 | convolution fusion | flops 67141632 | bytes 1245184 | tf_op jit(solution)/shard_map/dot_general | solution.py:386
  18.2 7.4 %collective-permute-done.4.right_o = bf16[80,512]{1,0:T(8,128)(2,1)S(1)} collective-permute-done((bf16[80,512]{1,0:T(8,128)(2,1)S(1)}, bf16[80,512]{1,0:T(8,128)(2,1)S(1)}, u32[]{:S(2)}, u32[]{:S(2)}) %collective-permute-start.4) | collective-permute-done | bytes 81952 | tf_op jit(solution)/shard_map/ppermute | solution.py:358
  25.6 2.9 %all-to-all-done = bf16[32,24,512]{2,1,0:T(8,128)(2,1)S(1)} async-done(((bf16[32,24,512]{2,1,0:T(8,128)(2,1)}), bf16[32,24,512]{2,1,0:T(8,128)(2,1)S(1)}, u32[]{:S(2)}, u32[]{:S(2)}) %all-to-all-start) | async-done | bytes 786464 | tf_op jit(solution)/shard_map/all_to_all | solution.py:376
  28.5 13.4 %pair_grads.1 = (bf16[64,512]{1,0:T(8,128)(2,1)S(1)}, bf16[64,512]{1,0:T(8,128)(2,1)S(1)}, bf16[64,512]{1,0:T(8,128)(2,1)S(1)}, bf16[128,512]{1,0:T(8,128)(2,1)S(1)}, bf16[256,512]{1,0:T(8,128)(2,1)S(1)}) custom-call(s32[1]{0:T(128)} %bitcast.1.core, s32[3,64]{1,0:T(4,128)S(1)} %get-tuple-element.30.ids_s, f32[8,64]{1,0:T(8,128)S(1)} %pad_convert_fusion.ids_ref, ...), custom_call_target="tpu_custom_call" | custom-call | flops 8053063680 | bytes 2097152 | tf_op jit(solution)/shard_map/pair_grads/pallas_call | solution.py:200
  42.4 2.6 %collective-permute-start.8 = (bf16[64,512]{1,0:T(8,128)(2,1)S(1)}, bf16[64,512]{1,0:T(8,128)(2,1)S(1)}, u32[]{:S(2)}, u32[]{:S(2)}) collective-permute-start(bf16[64,512]{1,0:T(8,128)(2,1)S(1)} %get-tuple-element.21), channel_id=1, source_target_pairs={{1,3},{3,5},{5,7},{7,9},{9,11},{11,13},{13,15},{15,17},{17,19},{19... | collective-permute-start | bytes 196616 | tf_op jit(solution)/shard_map/ppermute | solution.py:411
  45.1 2.9 %collective-permute-start.3 = (bf16[128,1024]{1,0:T(8,128)(2,1)S(1)}, bf16[128,1024]{1,0:T(8,128)(2,1)S(1)}, u32[]{:S(2)}, u32[]{:S(2)}) collective-permute-start(bf16[128,1024]{1,0:T(8,128)(2,1)S(1)} %pad_maximum_fusion.refs_0_), channel_id=1, source_target_pairs={{0,4},{1,5},{2,6},{3,7},{4,0},{5,1},{6,2},{7,3},{8,12},{9,13},{10,... | collective-permute-start | bytes 786440 | tf_op jit(solution)/shard_map/ppermute | solution.py:358
  48.4 2.3 %collective-permute-done.8 = bf16[64,512]{1,0:T(8,128)(2,1)S(1)} collective-permute-done((bf16[64,512]{1,0:T(8,128)(2,1)S(1)}, bf16[64,512]{1,0:T(8,128)(2,1)S(1)}, u32[]{:S(2)}, u32[]{:S(2)}) %collective-permute-start.8) | collective-permute-done | bytes 65568 | tf_op jit(solution)/shard_map/ppermute | solution.py:411
  51.0 1.6 %collective-permute-start.11 = (bf16[256,128]{1,0:T(8,128)(2,1)S(1)}, bf16[256,128]{1,0:T(8,128)(2,1)S(1)}, u32[]{:S(2)}, u32[]{:S(2)}) collective-permute-start(bf16[256,128]{1,0:T(8,128)(2,1)S(1)} %get-tuple-element.35), channel_id=1, source_target_pairs={{0,4},{1,5},{2,6},{3,7},{4,0},{5,1},{6,2},{7,3},{8,12},{9,13},{10,... | collective-permute-start | bytes 196616 | tf_op jit(solution)/shard_map/ppermute | solution.py:358
  52.6 6.8 %collective-permute-start.10 = (bf16[256,128]{1,0:T(8,128)(2,1)S(1)}, bf16[256,128]{1,0:T(8,128)(2,1)S(1)}, u32[]{:S(2)}, u32[]{:S(2)}) collective-permute-start(bf16[256,128]{1,0:T(8,128)(2,1)S(1)} %get-tuple-element.36), channel_id=1, source_target_pairs={{0,6},{1,7},{2,0},{3,1},{4,2},{5,3},{6,4},{7,5},{8,14},{9,15},{10,... | collective-permute-start | bytes 196616 | tf_op jit(solution)/shard_map/ppermute | solution.py:358
  59.9 4.3 %collective-permute-done.1.refs_1_ = bf16[128,1024]{1,0:T(8,128)(2,1)S(1)} collective-permute-done((bf16[128,1024]{1,0:T(8,128)(2,1)S(1)}, bf16[128,1024]{1,0:T(8,128)(2,1)S(1)}, u32[]{:S(2)}, u32[]{:S(2)}) %collective-permute-start.1) | collective-permute-done | bytes 262176 | tf_op jit(solution)/shard_map/ppermute | solution.py:358
  66.2 5.9 %collective-permute-start.14 = (bf16[288,128]{1,0:T(8,128)(2,1)S(1)}, bf16[288,128]{1,0:T(8,128)(2,1)S(1)}, u32[]{:S(2)}, u32[]{:S(2)}) collective-permute-start(bf16[288,128]{1,0:T(8,128)(2,1)S(1)} %get-tuple-element.33), channel_id=1, source_target_pairs={{0,16},{1,17},{2,18},{3,19},{4,20},{5,21},{6,22},{7,23},{8,24},{9,... | collective-permute-start | bytes 221192 | tf_op jit(solution)/shard_map/ppermute | solution.py:358
  73.3 3.2 %collective-permute-done.14 = bf16[288,128]{1,0:T(8,128)(2,1)S(1)} collective-permute-done((bf16[288,128]{1,0:T(8,128)(2,1)S(1)}, bf16[288,128]{1,0:T(8,128)(2,1)S(1)}, u32[]{:S(2)}, u32[]{:S(2)}) %collective-permute-start.14) | collective-permute-done | bytes 73760 | tf_op jit(solution)/shard_map/ppermute | solution.py:358
  76.6 4.0 %collective-permute-start.15 = (bf16[288,128]{1,0:T(8,128)(2,1)S(1)}, bf16[288,128]{1,0:T(8,128)(2,1)S(1)}, u32[]{:S(2)}, u32[]{:S(2)}) collective-permute-start(bf16[288,128]{1,0:T(8,128)(2,1)S(1)} %add_convert_fusion.3), channel_id=1, source_target_pairs={{0,32},{32,0},{64,96},{96,64},{128,160},{160,128},{192,224},{224,1... | collective-permute-start | bytes 221192 | tf_op jit(solution)/shard_map/ppermute | solution.py:437
  82.4 3.5 %collective-permute-start.18 = (bf16[288,128]{1,0:T(8,128)(2,1)S(1)}, bf16[288,128]{1,0:T(8,128)(2,1)S(1)}, u32[]{:S(2)}, u32[]{:S(2)}) collective-permute-start(bf16[288,128]{1,0:T(8,128)(2,1)S(1)} %add_convert_fusion.2), channel_id=1, source_target_pairs={{0,128},{32,160},{64,192},{96,224},{128,0},{160,32},{192,64},{224,... | collective-permute-start | bytes 221192 | tf_op jit(solution)/shard_map/ppermute | solution.py:373
  85.9 1.6 %collective-permute-start.17 = (bf16[288,128]{1,0:T(8,128)(2,1)S(1)}, bf16[288,128]{1,0:T(8,128)(2,1)S(1)}, u32[]{:S(2)}, u32[]{:S(2)}) collective-permute-start(bf16[288,128]{1,0:T(8,128)(2,1)S(1)} %add_convert_fusion.2), channel_id=1, source_target_pairs={{0,192},{32,224},{64,0},{96,32},{128,64},{160,96},{192,128},{224,1... | collective-permute-start | bytes 221192 | tf_op jit(solution)/shard_map/ppermute | solution.py:373
  88.3 2.4 %convolution_add_fusion = f32[64,1024]{1,0:T(8,128)} fusion(f32[64,1024]{1,0:T(8,128)S(1)} %fusion.5, bf16[64,512]{1,0:T(8,128)(2,1)S(1)} %get-tuple-element.18, bf16[1024,512]{1,0:T(8,128)(2,1)} %param.15), kind=kOutput, calls=%fused_computation | convolution fusion | flops 67174400 | bytes 1638400 | tf_op jit(solution)/shard_map/dot_general | solution.py:419
  90.6 3.1 %collective-permute-done.16 = bf16[288,128]{1,0:T(8,128)(2,1)S(1)} collective-permute-done((bf16[288,128]{1,0:T(8,128)(2,1)S(1)}, bf16[288,128]{1,0:T(8,128)(2,1)S(1)}, u32[]{:S(2)}, u32[]{:S(2)}) %collective-permute-start.16) | collective-permute-done | bytes 73760 | tf_op jit(solution)/shard_map/ppermute | solution.py:373
  93.8 1.8 %collective-permute-start.21 = (bf16[288,128]{1,0:T(8,128)(2,1)S(1)}, bf16[288,128]{1,0:T(8,128)(2,1)S(1)}, u32[]{:S(2)}, u32[]{:S(2)}) collective-permute-start(bf16[288,128]{1,0:T(8,128)(2,1)S(1)} %add_convert_fusion.1), channel_id=1, source_target_pairs={{0,16},{1,17},{2,18},{3,19},{4,20},{5,21},{6,22},{7,23},{8,24},{9,... | collective-permute-start | bytes 221192 | tf_op jit(solution)/shard_map/ppermute | solution.py:358
  97.1 4.1 %collective-permute-done.19 = bf16[288,128]{1,0:T(8,128)(2,1)S(1)} collective-permute-done((bf16[288,128]{1,0:T(8,128)(2,1)S(1)}, bf16[288,128]{1,0:T(8,128)(2,1)S(1)}, u32[]{:S(2)}, u32[]{:S(2)}) %collective-permute-start.19) | collective-permute-done | bytes 73760 | tf_op jit(solution)/shard_map/ppermute | solution.py:358
  103.8 6.2 %collective-permute-start.25 = (bf16[1152,128]{1,0:T(8,128)(2,1)S(1)}, bf16[1152,128]{1,0:T(8,128)(2,1)S(1)}, u32[]{:S(2)}, u32[]{:S(2)}) collective-permute-start(bf16[1152,128]{1,0:T(8,128)(2,1)S(1)} %constant_dynamic-update-slice_fusion.refs_1_), channel_id=1, source_target_pairs={{0,1},{1,0},{2,3},{3,2},{4,5},{5,4},{6,7},{7,6},{8,9},{9,8},{10,11... | collective-permute-start | bytes 884744 | tf_op jit(solution)/shard_map/ppermute | solution.py:358
  110.0 5.6 %collective-permute-start.28 = (bf16[1152,128]{1,0:T(8,128)(2,1)S(1)}, bf16[1152,128]{1,0:T(8,128)(2,1)S(1)}, u32[]{:S(2)}, u32[]{:S(2)}) collective-permute-start(bf16[1152,128]{1,0:T(8,128)(2,1)S(1)} %collective-permute-done.24.refs_4_), channel_id=1, source_target_pairs={{0,1},{1,0},{2,3},{3,2},{4,5},{5,4},{6,7},{7,6},{8,9},{9,8},{10,11... | collective-permute-start | bytes 884744 | tf_op jit(solution)/shard_map/ppermute | solution.py:358
  119.9 3.4 %finish.1 = (f32[1024,512]{1,0:T(8,128)}, f32[1024,512]{1,0:T(8,128)}, f32[512,128]{1,0:T(8,128)}, f32[1,512]{1,0:T(1,128)}, f32[1,128]{1,0:T(1,128)}) custom-call(s32[3]{0:T(128)S(1)} %pad_add_fusion.refs_0_, bf16[1152,128]{1,0:T(8,128)(2,1)S(1)} %constant_dynamic-update-slice_fusion.refs_1_, bf16[1152,128]{1,0:T(8,128)(2,1)S(1)} %collective-permute-done.22.refs_2_, ...), custom_call_target="tpu_custom_call" | custom-call | tf_op jit(solution)/shard_map/finish/pallas_call | solution.py:449
  (87 shorter events, 20.0 us)
Async XLA Ops:
  4.8 23.7 %all-to-all-start = ((bf16[32,24,512]{2,1,0:T(8,128)(2,1)}), bf16[32,24,512]{2,1,0:T(8,128)(2,1)S(1)}, u32[]{:S(2)}, u32[]{:S(2)}) async-start(bf16[32,24,512]{2,1,0:T(8,128)(2,1)} %bitcast.4), calls=%async_computation | async-start | bytes 1572864 | tf_op jit(solution)/shard_map/all_to_all | solution.py:376
  14.2 11.3 %collective-permute-start.4 = (bf16[80,512]{1,0:T(8,128)(2,1)S(1)}, bf16[80,512]{1,0:T(8,128)(2,1)S(1)}, u32[]{:S(2)}, u32[]{:S(2)}) collective-permute-start(bf16[80,512]{1,0:T(8,128)(2,1)S(1)} %fusion.2.right_m), channel_id=1, source_target_pairs={{0,31},{1,2},{2,1},{3,4},{4,3},{5,6},{6,5},{7,8},{8,7},{9,10},{10,... | collective-permute-start | bytes 245768 | tf_op jit(solution)/shard_map/ppermute | solution.py:358
  41.8 8.9 %collective-permute-start.6 = (bf16[256,512]{1,0:T(8,128)(2,1)S(1)}, bf16[256,512]{1,0:T(8,128)(2,1)S(1)}, u32[]{:S(2)}, u32[]{:S(2)}) collective-permute-start(bf16[256,512]{1,0:T(8,128)(2,1)S(1)} %get-tuple-element.20), channel_id=1, source_target_pairs={{0,1},{1,0},{2,3},{3,2},{4,5},{5,4},{6,7},{7,6},{8,9},{9,8},{10,11... | collective-permute-start | bytes 786440 | tf_op jit(solution)/shard_map/ppermute | solution.py:358
  42.4 8.3 %collective-permute-start.8 = (bf16[64,512]{1,0:T(8,128)(2,1)S(1)}, bf16[64,512]{1,0:T(8,128)(2,1)S(1)}, u32[]{:S(2)}, u32[]{:S(2)}) collective-permute-start(bf16[64,512]{1,0:T(8,128)(2,1)S(1)} %get-tuple-element.21), channel_id=1, source_target_pairs={{1,3},{3,5},{5,7},{7,9},{9,11},{11,13},{13,15},{15,17},{17,19},{19... | collective-permute-start | bytes 196616 | tf_op jit(solution)/shard_map/ppermute | solution.py:411
  45.0 5.8 %collective-permute-start.7 = (bf16[64,512]{1,0:T(8,128)(2,1)S(1)}, bf16[64,512]{1,0:T(8,128)(2,1)S(1)}, u32[]{:S(2)}, u32[]{:S(2)}) collective-permute-start(bf16[64,512]{1,0:T(8,128)(2,1)S(1)} %get-tuple-element.21), channel_id=1, source_target_pairs={{0,31},{1,2},{2,1},{3,4},{4,3},{5,6},{6,5},{7,8},{8,7},{9,10},{10,... | collective-permute-start | bytes 196616 | tf_op jit(solution)/shard_map/ppermute | solution.py:358
  45.1 14.3 %collective-permute-start.3 = (bf16[128,1024]{1,0:T(8,128)(2,1)S(1)}, bf16[128,1024]{1,0:T(8,128)(2,1)S(1)}, u32[]{:S(2)}, u32[]{:S(2)}) collective-permute-start(bf16[128,1024]{1,0:T(8,128)(2,1)S(1)} %pad_maximum_fusion.refs_0_), channel_id=1, source_target_pairs={{0,4},{1,5},{2,6},{3,7},{4,0},{5,1},{6,2},{7,3},{8,12},{9,13},{10,... | collective-permute-start | bytes 786440 | tf_op jit(solution)/shard_map/ppermute | solution.py:358
  48.0 11.9 %collective-permute-start.2 = (bf16[128,1024]{1,0:T(8,128)(2,1)S(1)}, bf16[128,1024]{1,0:T(8,128)(2,1)S(1)}, u32[]{:S(2)}, u32[]{:S(2)}) collective-permute-start(bf16[128,1024]{1,0:T(8,128)(2,1)S(1)} %pad_maximum_fusion.refs_0_), channel_id=1, source_target_pairs={{0,6},{1,7},{2,0},{3,1},{4,2},{5,3},{6,4},{7,5},{8,14},{9,15},{10,... | collective-permute-start | bytes 786440 | tf_op jit(solution)/shard_map/ppermute | solution.py:358
  50.7 13.5 %collective-permute-start.1 = (bf16[128,1024]{1,0:T(8,128)(2,1)S(1)}, bf16[128,1024]{1,0:T(8,128)(2,1)S(1)}, u32[]{:S(2)}, u32[]{:S(2)}) collective-permute-start(bf16[128,1024]{1,0:T(8,128)(2,1)S(1)} %pad_maximum_fusion.refs_0_), channel_id=1, source_target_pairs={{0,2},{1,3},{2,4},{3,5},{4,6},{5,7},{6,0},{7,1},{8,10},{9,11},{10,... | collective-permute-start | bytes 786440 | tf_op jit(solution)/shard_map/ppermute | solution.py:358
  51.0 13.2 %collective-permute-start.11 = (bf16[256,128]{1,0:T(8,128)(2,1)S(1)}, bf16[256,128]{1,0:T(8,128)(2,1)S(1)}, u32[]{:S(2)}, u32[]{:S(2)}) collective-permute-start(bf16[256,128]{1,0:T(8,128)(2,1)S(1)} %get-tuple-element.35), channel_id=1, source_target_pairs={{0,4},{1,5},{2,6},{3,7},{4,0},{5,1},{6,2},{7,3},{8,12},{9,13},{10,... | collective-permute-start | bytes 196616 | tf_op jit(solution)/shard_map/ppermute | solution.py:358
  52.6 11.7 %collective-permute-start.10 = (bf16[256,128]{1,0:T(8,128)(2,1)S(1)}, bf16[256,128]{1,0:T(8,128)(2,1)S(1)}, u32[]{:S(2)}, u32[]{:S(2)}) collective-permute-start(bf16[256,128]{1,0:T(8,128)(2,1)S(1)} %get-tuple-element.36), channel_id=1, source_target_pairs={{0,6},{1,7},{2,0},{3,1},{4,2},{5,3},{6,4},{7,5},{8,14},{9,15},{10,... | collective-permute-start | bytes 196616 | tf_op jit(solution)/shard_map/ppermute | solution.py:358
  59.4 6.2 %collective-permute-start.9 = (bf16[256,128]{1,0:T(8,128)(2,1)S(1)}, bf16[256,128]{1,0:T(8,128)(2,1)S(1)}, u32[]{:S(2)}, u32[]{:S(2)}) collective-permute-start(bf16[256,128]{1,0:T(8,128)(2,1)S(1)} %get-tuple-element.37), channel_id=1, source_target_pairs={{0,2},{1,3},{2,4},{3,5},{4,6},{5,7},{6,0},{7,1},{8,10},{9,11},{10,... | collective-permute-start | bytes 196616 | tf_op jit(solution)/shard_map/ppermute | solution.py:358
  66.1 7.2 %collective-permute-start.12 = (bf16[288,128]{1,0:T(8,128)(2,1)S(1)}, bf16[288,128]{1,0:T(8,128)(2,1)S(1)}, u32[]{:S(2)}, u32[]{:S(2)}) collective-permute-start(bf16[288,128]{1,0:T(8,128)(2,1)S(1)} %get-tuple-element.32), channel_id=1, source_target_pairs={{0,8},{1,9},{2,10},{3,11},{4,12},{5,13},{6,14},{7,15},{8,16},{9,17... | collective-permute-start | bytes 221192 | tf_op jit(solution)/shard_map/ppermute | solution.py:358
  66.2 10.3 %collective-permute-start.14 = (bf16[288,128]{1,0:T(8,128)(2,1)S(1)}, bf16[288,128]{1,0:T(8,128)(2,1)S(1)}, u32[]{:S(2)}, u32[]{:S(2)}) collective-permute-start(bf16[288,128]{1,0:T(8,128)(2,1)S(1)} %get-tuple-element.33), channel_id=1, source_target_pairs={{0,16},{1,17},{2,18},{3,19},{4,20},{5,21},{6,22},{7,23},{8,24},{9,... | collective-permute-start | bytes 221192 | tf_op jit(solution)/shard_map/ppermute | solution.py:358
  76.6 5.8 %collective-permute-start.15 = (bf16[288,128]{1,0:T(8,128)(2,1)S(1)}, bf16[288,128]{1,0:T(8,128)(2,1)S(1)}, u32[]{:S(2)}, u32[]{:S(2)}) collective-permute-start(bf16[288,128]{1,0:T(8,128)(2,1)S(1)} %add_convert_fusion.3), channel_id=1, source_target_pairs={{0,32},{32,0},{64,96},{96,64},{128,160},{160,128},{192,224},{224,1... | collective-permute-start | bytes 221192 | tf_op jit(solution)/shard_map/ppermute | solution.py:437
  82.4 8.3 %collective-permute-start.18 = (bf16[288,128]{1,0:T(8,128)(2,1)S(1)}, bf16[288,128]{1,0:T(8,128)(2,1)S(1)}, u32[]{:S(2)}, u32[]{:S(2)}) collective-permute-start(bf16[288,128]{1,0:T(8,128)(2,1)S(1)} %add_convert_fusion.2), channel_id=1, source_target_pairs={{0,128},{32,160},{64,192},{96,224},{128,0},{160,32},{192,64},{224,... | collective-permute-start | bytes 221192 | tf_op jit(solution)/shard_map/ppermute | solution.py:373
  85.9 4.8 %collective-permute-start.17 = (bf16[288,128]{1,0:T(8,128)(2,1)S(1)}, bf16[288,128]{1,0:T(8,128)(2,1)S(1)}, u32[]{:S(2)}, u32[]{:S(2)}) collective-permute-start(bf16[288,128]{1,0:T(8,128)(2,1)S(1)} %add_convert_fusion.2), channel_id=1, source_target_pairs={{0,192},{32,224},{64,0},{96,32},{128,64},{160,96},{192,128},{224,1... | collective-permute-start | bytes 221192 | tf_op jit(solution)/shard_map/ppermute | solution.py:373
  87.4 6.3 %collective-permute-start.16 = (bf16[288,128]{1,0:T(8,128)(2,1)S(1)}, bf16[288,128]{1,0:T(8,128)(2,1)S(1)}, u32[]{:S(2)}, u32[]{:S(2)}) collective-permute-start(bf16[288,128]{1,0:T(8,128)(2,1)S(1)} %add_convert_fusion.2), channel_id=1, source_target_pairs={{0,64},{32,96},{64,128},{96,160},{128,192},{160,224},{192,0},{224,... | collective-permute-start | bytes 221192 | tf_op jit(solution)/shard_map/ppermute | solution.py:373
  93.8 7.5 %collective-permute-start.21 = (bf16[288,128]{1,0:T(8,128)(2,1)S(1)}, bf16[288,128]{1,0:T(8,128)(2,1)S(1)}, u32[]{:S(2)}, u32[]{:S(2)}) collective-permute-start(bf16[288,128]{1,0:T(8,128)(2,1)S(1)} %add_convert_fusion.1), channel_id=1, source_target_pairs={{0,16},{1,17},{2,18},{3,19},{4,20},{5,21},{6,22},{7,23},{8,24},{9,... | collective-permute-start | bytes 221192 | tf_op jit(solution)/shard_map/ppermute | solution.py:358
  95.6 5.6 %collective-permute-start.20 = (bf16[288,128]{1,0:T(8,128)(2,1)S(1)}, bf16[288,128]{1,0:T(8,128)(2,1)S(1)}, u32[]{:S(2)}, u32[]{:S(2)}) collective-permute-start(bf16[288,128]{1,0:T(8,128)(2,1)S(1)} %add_convert_fusion.1), channel_id=1, source_target_pairs={{0,24},{1,25},{2,26},{3,27},{4,28},{5,29},{6,30},{7,31},{8,0},{9,1... | collective-permute-start | bytes 221192 | tf_op jit(solution)/shard_map/ppermute | solution.py:358
  101.3 8.7 %collective-permute-start.24 = (bf16[1152,128]{1,0:T(8,128)(2,1)S(1)}, bf16[1152,128]{1,0:T(8,128)(2,1)S(1)}, u32[]{:S(2)}, u32[]{:S(2)}) collective-permute-start(bf16[1152,128]{1,0:T(8,128)(2,1)S(1)} %constant_dynamic-update-slice_fusion.refs_1_), channel_id=1, source_target_pairs={{0,4},{1,5},{2,6},{3,7},{4,0},{5,1},{6,2},{7,3},{8,12},{9,13},{10,... | collective-permute-start | bytes 884744 | tf_op jit(solution)/shard_map/ppermute | solution.py:358
  102.4 13.2 %collective-permute-start.23 = (bf16[1152,128]{1,0:T(8,128)(2,1)S(1)}, bf16[1152,128]{1,0:T(8,128)(2,1)S(1)}, u32[]{:S(2)}, u32[]{:S(2)}) collective-permute-start(bf16[1152,128]{1,0:T(8,128)(2,1)S(1)} %constant_dynamic-update-slice_fusion.refs_1_), channel_id=1, source_target_pairs={{0,6},{1,7},{2,0},{3,1},{4,2},{5,3},{6,4},{7,5},{8,14},{9,15},{10,... | collective-permute-start | bytes 884744 | tf_op jit(solution)/shard_map/ppermute | solution.py:358
  103.2 14.0 %collective-permute-start.22 = (bf16[1152,128]{1,0:T(8,128)(2,1)S(1)}, bf16[1152,128]{1,0:T(8,128)(2,1)S(1)}, u32[]{:S(2)}, u32[]{:S(2)}) collective-permute-start(bf16[1152,128]{1,0:T(8,128)(2,1)S(1)} %constant_dynamic-update-slice_fusion.refs_1_), channel_id=1, source_target_pairs={{0,2},{1,3},{2,4},{3,5},{4,6},{5,7},{6,0},{7,1},{8,10},{9,11},{10,... | collective-permute-start | bytes 884744 | tf_op jit(solution)/shard_map/ppermute | solution.py:358
  103.8 14.9 %collective-permute-start.25 = (bf16[1152,128]{1,0:T(8,128)(2,1)S(1)}, bf16[1152,128]{1,0:T(8,128)(2,1)S(1)}, u32[]{:S(2)}, u32[]{:S(2)}) collective-permute-start(bf16[1152,128]{1,0:T(8,128)(2,1)S(1)} %constant_dynamic-update-slice_fusion.refs_1_), channel_id=1, source_target_pairs={{0,1},{1,0},{2,3},{3,2},{4,5},{5,4},{6,7},{7,6},{8,9},{9,8},{10,11... | collective-permute-start | bytes 884744 | tf_op jit(solution)/shard_map/ppermute | solution.py:358
  110.0 8.7 %collective-permute-start.28 = (bf16[1152,128]{1,0:T(8,128)(2,1)S(1)}, bf16[1152,128]{1,0:T(8,128)(2,1)S(1)}, u32[]{:S(2)}, u32[]{:S(2)}) collective-permute-start(bf16[1152,128]{1,0:T(8,128)(2,1)S(1)} %collective-permute-done.24.refs_4_), channel_id=1, source_target_pairs={{0,1},{1,0},{2,3},{3,2},{4,5},{5,4},{6,7},{7,6},{8,9},{9,8},{10,11... | collective-permute-start | bytes 884744 | tf_op jit(solution)/shard_map/ppermute | solution.py:358
  (16 other events, 137.1 us)

commit v5 on v4

--- a/solution.py
+++ b/solution.py
@@ -29,12 +29,11 @@
 
 
 def backward(
-    tile_at, hid_s, slope_s, tsum_s, mask_s, half_s, wmt_ref, wf_ref, lacc, racc, mid_acc, fin_acc
+    tile_at, hid_s, slope_s, info_s, half_s, wmt_ref, wf_ref, lacc, racc, mid_acc, fin_acc
 ):
     col0 = pl.multiple_of(tile_at // 8 * PANEL, PANEL)
     row0 = pl.multiple_of(tile_at % 8 * ROWS, ROWS)
     wf = wf_ref[...]
-    count = tsum_s[tile_at // 8 * 8 + 24, 0:1, 0:CHUNK]
     parts = [slice(c * CHUNK, (c + 1) * CHUNK) for c in range(ROWS * PANEL // CHUNK)]
     pre = [
         jnp.dot(hid_s[part, :], half_s[...], preferred_element_type=F32).T
@@ -45,7 +44,9 @@
         p = jnp.tanh(u) + 1.0
         act = u * p
         predicted = jnp.sum(act * wf, axis=0, keepdims=True)
-        pair_slope = (16.0 * mask_s[tile_at, 0:1, part]) * (count * predicted - tsum_s[tile_at, 0:1, part])
+        pair_slope = info_s[tile_at, 1:2, part] * (
+            info_s[tile_at, 2:3, part] * predicted - info_s[tile_at, 0:1, part]
+        )
         grad_second = ((0.5 * pair_slope) * wf * (p + act * (2.0 - p))).astype(BF)
         fin = act * pair_slope
         fins.append(sum(fin[:, j * 128 : (j + 1) * 128] for j in range(CHUNK // 128)))
@@ -88,8 +89,7 @@
     sems,
     left_s,
     right_s,
-    tsum_s,
-    mask_s,
+    info_s,
     half_s,
     hid_s,
     slope_s,
@@ -101,22 +101,31 @@
     hidden = left_ref.shape[1]
     tile = ROWS * PANEL
     loads = [
-        pltpu.make_async_copy(ref.at[0:PANEL, :], panels_s.at[n], sems.at[n])
-        for n, ref in enumerate((left_ref, right_o, right_m, right_p))
+        pltpu.make_async_copy(ref.at[0:PANEL, :], panels_s.at[n], sems.at[m])
+        for m, (n, ref) in enumerate(
+            ((0, left_ref), (1 + 2 * core[0], right_o), (2, right_m), (3 - 2 * core[0], right_p))
+        )
     ]
     for copy in loads:
         copy.start()
     iota = lambda shape, axis: lax.broadcasted_iota(jnp.int32, shape, axis)
+    begin = jnp.sum(jnp.where((ids_ref[...] < ids_s[1, PANEL // 2].astype(F32)) & (iota((8, PANEL), 0) < 3), 1, 0))
+    shift = PANEL - (begin & (PANEL - 1))
 
     def scan(i, n):
-        k, rt = i // 8, i % 8
-        meets = (ids_s[1, rt * ROWS] <= ids_s[k, PANEL - 1]) & (ids_s[k, 0] <= ids_s[1, rt * ROWS + ROWS - 1])
+        j, rt = i // 8, i % 8
+        start = jnp.maximum(j * PANEL - shift, 0)
+        end = jnp.minimum(j * PANEL - shift + PANEL - 1, 3 * PANEL - 1)
+        last = jnp.maximum(end, 0)
+        meets = (
+            (end >= 0)
+            & (ids_s[1, rt * ROWS] <= ids_s[last // PANEL, last % PANEL])
+            & (ids_s[start // PANEL, start % PANEL] <= ids_s[1, rt * ROWS + ROWS - 1])
+        )
         todo[n] = i
         return n + meets.astype(jnp.int32)
 
-    n_todo = lax.fori_loop(0, 24, scan, 0)
-    for extra in range(3):
-        todo[n_todo + extra] = 24
+    n_todo = lax.fori_loop(0, 32, scan, 0)
     half_s[...] = (wmt_ref[...].astype(F32) * 0.5).T.astype(BF)
     n_src = targets_ref.shape[0]
     tsum = jnp.dot(
@@ -130,18 +139,22 @@
     col_ids = jnp.dot(ids.astype(BF), repeat, preferred_element_type=F32)
     lane = iota((8, tile), 1)
     itself = iota((8, tile), 0) * ROWS + lane // PANEL == lane % PANEL
+    infos = []
     for k in range(3):
         same = row_ids == col_ids[k : k + 1, :]
-        mask = jnp.where(same & ~itself if k == 1 else same, 1.0, 0.0)
+        mask = jnp.where(same & ~itself if k == 1 else same, 16.0, 0.0)
         count = jnp.max(
-            jnp.where(iota((8, tile), 1) == k * (PANEL + 1), tsum[8:16, :], 0.0)[0:1], axis=1, keepdims=True
+            jnp.where(iota((1, tile), 1) == k * (PANEL + 1), tsum[8:9, :], 0.0), axis=1, keepdims=True
         )
-        tsum_s[24 + 8 * k, 0:1, :] = jnp.broadcast_to(count, (1, tile))
-        for rt in range(8):
-            mask_s[k * 8 + rt, 0:1, :] = mask[rt : rt + 1, :]
-            tsum_s[k * 8 + rt, 0:1, :] = tsum[k * 8 + rt : k * 8 + rt + 1, :]
-    mask_s[24, 0:1, :] = jnp.zeros((1, tile), F32)
-    tsum_s[48, 0:1, :] = jnp.zeros((1, tile), F32)
+        infos.append((tsum[k * 8 : k * 8 + 8, :], mask, jnp.broadcast_to(count, (8, tile))))
+    ahead, behind = lax.rem(shift, tile), lax.rem(shift + tile - PANEL, tile)
+    for j in range(4):
+        for n in range(3):
+            here = pltpu.roll(infos[j][n], ahead, 1) if j < 3 else jnp.zeros((8, tile), F32)
+            before = pltpu.roll(infos[j - 1][n], behind, 1) if j > 0 else jnp.zeros((8, tile), F32)
+            moved = jnp.where(lane % PANEL >= shift, here, before)
+            for rt in range(8):
+                info_s[j * 8 + rt, n : n + 1, :] = moved[rt : rt + 1, :]
     lacc[...] = jnp.zeros_like(lacc)
     racc[...] = jnp.zeros_like(racc)
     mid_acc[...] = jnp.zeros_like(mid_acc)
@@ -149,9 +162,10 @@
     for copy in loads:
         copy.wait()
     left_s[...] = (panels_s[0].astype(F32) + bias_ref[...]) * 0.5
-    for k in range(3):
-        right_s[k * PANEL : (k + 1) * PANEL, :] = panels_s[k + 1].astype(F32) * 0.5
-    rest = (tsum_s, mask_s, half_s, wmt_ref, wf_ref, lacc, racc, mid_acc, fin_acc)
+    place = (iota((4 * PANEL, 3 * PANEL), 0) == iota((4 * PANEL, 3 * PANEL), 1) + shift).astype(BF)
+    rights = jnp.concatenate([panels_s[k + 1] for k in range(3)], axis=0)
+    right_s[...] = jnp.dot(place, rights, preferred_element_type=F32) * 0.5
+    rest = (info_s, half_s, wmt_ref, wf_ref, lacc, racc, mid_acc, fin_acc)
 
     def step(i, carry):
         forward(todo[i], left_s, right_s, hid_s, slope_s)
@@ -161,9 +175,17 @@
     lax.fori_loop(0, n_todo, step, 0)
     left = lacc[...] * 0.5
     out_left[...] = left.astype(BF)
-    outer, own, partner = [
-        (racc[k * PANEL : (k + 1) * PANEL, :] * 0.5).astype(BF) for k in range(3)
-    ]
+    back = (iota((3 * PANEL, 4 * PANEL), 1) == iota((3 * PANEL, 4 * PANEL), 0) + shift).astype(BF)
+    total = racc[...] * 0.5
+    high = total.astype(BF)
+    low = (total - high.astype(F32)).astype(BF)
+    right_s[0 : 3 * PANEL, :] = jnp.dot(back, high, preferred_element_type=F32) + jnp.dot(
+        back, low, preferred_element_type=F32
+    )
+    at = pl.multiple_of(2 * PANEL * core[0], PANEL)
+    outer = right_s[pl.ds(at, PANEL), :].astype(BF)
+    own = right_s[PANEL : 2 * PANEL, :].astype(BF)
+    partner = right_s[pl.ds(pl.multiple_of(2 * PANEL - at, PANEL), PANEL), :].astype(BF)
     out_outer[...] = outer
     out_own[...] = own
     out_sent[PANEL : 2 * PANEL, :] = partner
@@ -212,13 +234,12 @@
         + [vmem] * 4,
         out_specs=(vmem,) * 5,
         scratch_shapes=[
-            pltpu.SMEM((32,), jnp.int32),
+            pltpu.SMEM((40,), jnp.int32),
             pltpu.VMEM((4, PANEL, hidden), BF),
             pltpu.SemaphoreType.DMA((4,)),
             pltpu.VMEM((PANEL, hidden), F32),
-            pltpu.VMEM((3 * PANEL, hidden), F32),
-            pltpu.VMEM((49, 8, tile), F32),
-            pltpu.VMEM((25, 8, tile), F32),
+            pltpu.VMEM((4 * PANEL, hidden), F32),
+            pltpu.VMEM((32, 8, tile), F32),
             pltpu.VMEM((hidden, upper), BF),
             pltpu.VMEM((tile, hidden), BF),
             pltpu.VMEM((tile, hidden), BF),
@@ -242,9 +263,8 @@
     counters = (lane == 0) | (lane == PANEL + 1) | (lane == 2 * (PANEL + 1))
 
     def slot(i, carry):
-        row = blocks[i, 0]
-        step = blocks[i, 1] - row
-        side = jnp.where((row & 1) == 0, step, -step) + 1
+        row = blocks[0, i]
+        side = blocks[1, i] - row + 1
         to = row * 3 + side
         for rt in range(8):
             value = targets_ref[pl.ds(i, 1), rt * tile : (rt + 1) * tile]
@@ -372,7 +392,7 @@
     def on_z(value, d):
         return lax.ppermute(value, "grp", [(i, (i + d) % groups) for i in range(groups)])
 
-    sums = send_targets(block_list[0], block_counts, pair_targets[0], panels).reshape(panels, 24, ROWS * PANEL)
+    sums = send_targets(block_list[0].T, block_counts, pair_targets[0], panels).reshape(panels, 24, ROWS * PANEL)
     targets = lax.all_to_all(sums, "blk", 0, 0, tiled=True)
     targets = targets.reshape(24 * panels, ROWS * PANEL)
 
@@ -384,7 +404,11 @@
     right_partner = on_core(right_own)
 
     left = jnp.dot(emb, w_left, preferred_element_type=F32).astype(BF)
-    col_ids = jnp.stack([right_outer[PANEL, :PANEL], ids, right_partner[PANEL, :PANEL]])
+    outer_ids = right_outer[PANEL, :PANEL]
+    partner_ids = right_partner[PANEL, :PANEL]
+    before = jnp.where(me == 0, BF(-1), jnp.where(core == 0, outer_ids, partner_ids))
+    after = jnp.where(me == panels - 1, BF(127), jnp.where(core == 0, partner_ids, outer_ids))
+    col_ids = jnp.stack([before, ids, after])
 
     emb_pair = jnp.concatenate([emb, on_core(emb)], axis=0)
     embs = [emb_pair]

time: 124 us -> 122 us (0.984)
  waiting for transfers between devices: 32.4 us -> 34.1 us
    ppermute x3, starting transfers between devices: 5.91 us -> 11 us  [on_z(): lax.ppermute(value, 'grp', [(i, (i + d) % groups) for i in range(groups)])]
    ppermute x1, starting transfers between devices: 4.02 us -> 1.08 us  [local(): lax.ppermute(total, 'grp', [(i, i ^ 1) for i in range(groups)]).astype(F32)]
    ppermute x24, starting transfers between devices: 41.4 us -> 38.7 us  [blk(): return lax.ppermute(value, 'blk', [(i, partner(i)) for i in range(panels)])]
    ppermute x24, waiting for transfers between devices: 22.8 us -> 24.7 us  [blk(): return lax.ppermute(value, 'blk', [(i, partner(i)) for i in range(panels)])]
  transfers between devices with their start and end apart: 30 -> 30, of which waited for: 11 -> 12; matrix products, arithmetic and copies ran while one was open for 5% -> 4% of each run, Pallas kernels for 0% -> 0%
where the time goes in v5:
time: 122 us
  starting transfers between devices  61.4 us (50%)
  waiting for transfers between devices  34.1 us (28%)
  Pallas kernels  18.5 us (15%)
  matrix products  4.01 us (3%)
  local copies, waits for them, and re-layouts  1.99 us (2%)
  between operations  1.72 us (1%)
    ppermute x24, starting transfers between devices, blk(): return lax.ppermute(value, 'blk', [(i, partner(i)) for i in range(panels)])  38.7 us
    ppermute x24, waiting for transfers between devices, blk(): return lax.ppermute(value, 'blk', [(i, partner(i)) for i in range(panels)])  24.7 us
    pallas_call x1, Pallas kernels, pair_grads(): pl.pallas_call(pair_kernel, out_shape=(panel, panel, panel, jax.ShapeDtyp...  13 us
    ppermute x3, starting transfers between devices, on_z(): lax.ppermute(value, 'grp', [(i, (i + d) % groups) for i in range(groups)])  11 us
    all_to_all x1, starting transfers between devices, local(): targets = lax.all_to_all(sums, 'blk', 0, 0, tiled=True)  8.75 us
    pallas_call x1, Pallas kernels, local(): pl.pallas_call(lambda *refs: finish_kernel(scale, *refs), grid=(4,), out_...  3.38 us
    all_to_all x1, waiting for transfers between devices, local(): targets = lax.all_to_all(sums, 'blk', 0, 0, tiled=True)  2.87 us
    ppermute x1, waiting for transfers between devices, local(): lax.ppermute(r_outer, 'blk', [(i, (i + 2) % panels) for i in range(1, pan...  2.67 us
  transfers between devices with their start and end apart: 30, of which 12 were waited for; matrix products, arithmetic and copies ran while one was open for 4% of the time, Pallas kernels for 0%

profile of v5, /device:TPU:1, one launch (start us, length us, event | category | flops | bytes accessed | tf_op | source)
XLA Modules:
  0.0 122.1 jit_solution(7257463562694741247)
XLA Ops:
  3.0 1.6 %send_targets.1 = bf16[768,512]{1,0:T(8,128)(2,1)} custom-call(s32[2,8]{1,0:T(2,128)S(1)} %bitcast.28, s32[1,1]{1,0:T(1,128)S(6)} %copy.21.live, f32[8,4096]{1,0:T(8,128)S(1)} %bitcast.27), custom_call_target="tpu_custom_call" | custom-call | tf_op jit(solution)/shard_map/send_targets/pallas_call | solution.py:286
  4.6 8.8 %all-to-all-start = ((bf16[32,24,512]{2,1,0:T(8,128)(2,1)}), bf16[32,24,512]{2,1,0:T(8,128)(2,1)S(1)}, u32[]{:S(2)}, u32[]{:S(2)}) async-start(bf16[32,24,512]{2,1,0:T(8,128)(2,1)} %bitcast.5), calls=%async_computation | async-start | bytes 1572864 | tf_op jit(solution)/shard_map/all_to_all | solution.py:396
  14.1 1.5 %collective-permute-start.4 = (bf16[80,512]{1,0:T(8,128)(2,1)S(1)}, bf16[80,512]{1,0:T(8,128)(2,1)S(1)}, u32[]{:S(2)}, u32[]{:S(2)}) collective-permute-start(bf16[80,512]{1,0:T(8,128)(2,1)S(1)} %fusion.2.right_m), channel_id=1, source_target_pairs={{0,31},{1,2},{2,1},{3,4},{4,3},{5,6},{6,5},{7,8},{8,7},{9,10},{10,... | collective-permute-start | bytes 245768 | tf_op jit(solution)/shard_map/ppermute | solution.py:378
  16.8 8.6 %collective-permute-done.4.right_o = bf16[80,512]{1,0:T(8,128)(2,1)S(1)} collective-permute-done((bf16[80,512]{1,0:T(8,128)(2,1)S(1)}, bf16[80,512]{1,0:T(8,128)(2,1)S(1)}, u32[]{:S(2)}, u32[]{:S(2)}) %collective-permute-start.4) | collective-permute-done | bytes 81952 | tf_op jit(solution)/shard_map/ppermute | solution.py:378
  25.4 2.9 %all-to-all-done = bf16[32,24,512]{2,1,0:T(8,128)(2,1)S(1)} async-done(((bf16[32,24,512]{2,1,0:T(8,128)(2,1)}), bf16[32,24,512]{2,1,0:T(8,128)(2,1)S(1)}, u32[]{:S(2)}, u32[]{:S(2)}) %all-to-all-start) | async-done | bytes 786464 | tf_op jit(solution)/shard_map/all_to_all | solution.py:396
  28.3 13.0 %pair_grads.1 = (bf16[64,512]{1,0:T(8,128)(2,1)S(1)}, bf16[64,512]{1,0:T(8,128)(2,1)S(1)}, bf16[64,512]{1,0:T(8,128)(2,1)S(1)}, bf16[128,512]{1,0:T(8,128)(2,1)S(1)}, bf16[256,512]{1,0:T(8,128)(2,1)S(1)}) custom-call(s32[1]{0:T(128)} %bitcast.1.core, s32[3,64]{1,0:T(4,128)S(1)} %get-tuple-element.30.ids_s, f32[8,64]{1,0:T(8,128)S(1)} %pad_convert_fusion.ids_ref, ...), custom_call_target="tpu_custom_call" | custom-call | flops 8053063680 | bytes 2097152 | tf_op jit(solution)/shard_map/pair_grads/pallas_call | solution.py:222
  41.3 2.4 %collective-permute-start.6 = (bf16[256,512]{1,0:T(8,128)(2,1)S(1)}, bf16[256,512]{1,0:T(8,128)(2,1)S(1)}, u32[]{:S(2)}, u32[]{:S(2)}) collective-permute-start(bf16[256,512]{1,0:T(8,128)(2,1)S(1)} %get-tuple-element.20), channel_id=1, source_target_pairs={{0,1},{1,0},{2,3},{3,2},{4,5},{5,4},{6,7},{7,6},{8,9},{9,8},{10,11... | collective-permute-start | bytes 786440 | tf_op jit(solution)/shard_map/ppermute | solution.py:378
  43.8 1.9 %collective-permute-start.8 = (bf16[64,512]{1,0:T(8,128)(2,1)S(1)}, bf16[64,512]{1,0:T(8,128)(2,1)S(1)}, u32[]{:S(2)}, u32[]{:S(2)}) collective-permute-start(bf16[64,512]{1,0:T(8,128)(2,1)S(1)} %get-tuple-element.21), channel_id=1, source_target_pairs={{1,3},{3,5},{5,7},{7,9},{9,11},{11,13},{13,15},{15,17},{17,19},{19... | collective-permute-start | bytes 196616 | tf_op jit(solution)/shard_map/ppermute | solution.py:435
  45.8 2.1 %collective-permute-start.3 = (bf16[128,1024]{1,0:T(8,128)(2,1)S(1)}, bf16[128,1024]{1,0:T(8,128)(2,1)S(1)}, u32[]{:S(2)}, u32[]{:S(2)}) collective-permute-start(bf16[128,1024]{1,0:T(8,128)(2,1)S(1)} %pad_maximum_fusion.refs_0_), channel_id=1, source_target_pairs={{0,4},{1,5},{2,6},{3,7},{4,0},{5,1},{6,2},{7,3},{8,12},{9,13},{10,... | collective-permute-start | bytes 786440 | tf_op jit(solution)/shard_map/ppermute | solution.py:378
  47.9 1.5 %collective-permute-start.2 = (bf16[128,1024]{1,0:T(8,128)(2,1)S(1)}, bf16[128,1024]{1,0:T(8,128)(2,1)S(1)}, u32[]{:S(2)}, u32[]{:S(2)}) collective-permute-start(bf16[128,1024]{1,0:T(8,128)(2,1)S(1)} %pad_maximum_fusion.refs_0_), channel_id=1, source_target_pairs={{0,6},{1,7},{2,0},{3,1},{4,2},{5,3},{6,4},{7,5},{8,14},{9,15},{10,... | collective-permute-start | bytes 786440 | tf_op jit(solution)/shard_map/ppermute | solution.py:378
  49.4 2.7 %collective-permute-done.8 = bf16[64,512]{1,0:T(8,128)(2,1)S(1)} collective-permute-done((bf16[64,512]{1,0:T(8,128)(2,1)S(1)}, bf16[64,512]{1,0:T(8,128)(2,1)S(1)}, u32[]{:S(2)}, u32[]{:S(2)}) %collective-permute-start.8) | collective-permute-done | bytes 65568 | tf_op jit(solution)/shard_map/ppermute | solution.py:435
  52.4 6.9 %collective-permute-start.10 = (bf16[256,128]{1,0:T(8,128)(2,1)S(1)}, bf16[256,128]{1,0:T(8,128)(2,1)S(1)}, u32[]{:S(2)}, u32[]{:S(2)}) collective-permute-start(bf16[256,128]{1,0:T(8,128)(2,1)S(1)} %get-tuple-element.36), channel_id=1, source_target_pairs={{0,6},{1,7},{2,0},{3,1},{4,2},{5,3},{6,4},{7,5},{8,14},{9,15},{10,... | collective-permute-start | bytes 196616 | tf_op jit(solution)/shard_map/ppermute | solution.py:378
  60.7 4.8 %collective-permute-done.1.refs_1_ = bf16[128,1024]{1,0:T(8,128)(2,1)S(1)} collective-permute-done((bf16[128,1024]{1,0:T(8,128)(2,1)S(1)}, bf16[128,1024]{1,0:T(8,128)(2,1)S(1)}, u32[]{:S(2)}, u32[]{:S(2)}) %collective-permute-start.1) | collective-permute-done | bytes 262176 | tf_op jit(solution)/shard_map/ppermute | solution.py:378
  70.2 3.9 %collective-permute-done.12 = bf16[288,128]{1,0:T(8,128)(2,1)S(1)} collective-permute-done((bf16[288,128]{1,0:T(8,128)(2,1)S(1)}, bf16[288,128]{1,0:T(8,128)(2,1)S(1)}, u32[]{:S(2)}, u32[]{:S(2)}) %collective-permute-start.12) | collective-permute-done | bytes 73760 | tf_op jit(solution)/shard_map/ppermute | solution.py:378
  75.7 1.8 %collective-permute-done.15 = bf16[288,128]{1,0:T(8,128)(2,1)S(1)} collective-permute-done((bf16[288,128]{1,0:T(8,128)(2,1)S(1)}, bf16[288,128]{1,0:T(8,128)(2,1)S(1)}, u32[]{:S(2)}, u32[]{:S(2)}) %collective-permute-start.15) | collective-permute-done | bytes 73760 | tf_op jit(solution)/shard_map/ppermute | solution.py:461
  77.5 8.6 %collective-permute-start.18 = (bf16[288,128]{1,0:T(8,128)(2,1)S(1)}, bf16[288,128]{1,0:T(8,128)(2,1)S(1)}, u32[]{:S(2)}, u32[]{:S(2)}) collective-permute-start(bf16[288,128]{1,0:T(8,128)(2,1)S(1)} %add_convert_fusion.2), channel_id=1, source_target_pairs={{0,128},{32,160},{64,192},{96,224},{128,0},{160,32},{192,64},{224,... | collective-permute-start | bytes 221192 | tf_op jit(solution)/shard_map/ppermute | solution.py:393
  86.1 2.4 %collective-permute-start.16 = (bf16[288,128]{1,0:T(8,128)(2,1)S(1)}, bf16[288,128]{1,0:T(8,128)(2,1)S(1)}, u32[]{:S(2)}, u32[]{:S(2)}) collective-permute-start(bf16[288,128]{1,0:T(8,128)(2,1)S(1)} %add_convert_fusion.2), channel_id=1, source_target_pairs={{0,64},{32,96},{64,128},{96,160},{128,192},{160,224},{192,0},{224,... | collective-permute-start | bytes 221192 | tf_op jit(solution)/shard_map/ppermute | solution.py:393
  88.5 2.4 %convolution_add_fusion = f32[64,1024]{1,0:T(8,128)} fusion(f32[64,1024]{1,0:T(8,128)S(1)} %fusion.5, bf16[64,512]{1,0:T(8,128)(2,1)S(1)} %get-tuple-element.18, bf16[1024,512]{1,0:T(8,128)(2,1)} %param.15), kind=kOutput, calls=%fused_computation | convolution fusion | flops 67174400 | bytes 1638400 | tf_op jit(solution)/shard_map/dot_general | solution.py:443
  93.0 2.5 %collective-permute-start.20 = (bf16[288,128]{1,0:T(8,128)(2,1)S(1)}, bf16[288,128]{1,0:T(8,128)(2,1)S(1)}, u32[]{:S(2)}, u32[]{:S(2)}) collective-permute-start(bf16[288,128]{1,0:T(8,128)(2,1)S(1)} %add_convert_fusion.1), channel_id=1, source_target_pairs={{0,24},{1,25},{2,26},{3,27},{4,28},{5,29},{6,30},{7,31},{8,0},{9,1... | collective-permute-start | bytes 221192 | tf_op jit(solution)/shard_map/ppermute | solution.py:378
  96.0 3.9 %collective-permute-done.19 = bf16[288,128]{1,0:T(8,128)(2,1)S(1)} collective-permute-done((bf16[288,128]{1,0:T(8,128)(2,1)S(1)}, bf16[288,128]{1,0:T(8,128)(2,1)S(1)}, u32[]{:S(2)}, u32[]{:S(2)}) %collective-permute-start.19) | collective-permute-done | bytes 73760 | tf_op jit(solution)/shard_map/ppermute | solution.py:378
  101.6 6.6 %collective-permute-start.25 = (bf16[1152,128]{1,0:T(8,128)(2,1)S(1)}, bf16[1152,128]{1,0:T(8,128)(2,1)S(1)}, u32[]{:S(2)}, u32[]{:S(2)}) collective-permute-start(bf16[1152,128]{1,0:T(8,128)(2,1)S(1)} %constant_dynamic-update-slice_fusion.refs_1_), channel_id=1, source_target_pairs={{0,1},{1,0},{2,3},{3,2},{4,5},{5,4},{6,7},{7,6},{8,9},{9,8},{10,11... | collective-permute-start | bytes 884744 | tf_op jit(solution)/shard_map/ppermute | solution.py:378
  108.3 6.2 %collective-permute-start.28 = (bf16[1152,128]{1,0:T(8,128)(2,1)S(1)}, bf16[1152,128]{1,0:T(8,128)(2,1)S(1)}, u32[]{:S(2)}, u32[]{:S(2)}) collective-permute-start(bf16[1152,128]{1,0:T(8,128)(2,1)S(1)} %collective-permute-done.24.refs_4_), channel_id=1, source_target_pairs={{0,1},{1,0},{2,3},{3,2},{4,5},{5,4},{6,7},{7,6},{8,9},{9,8},{10,11... | collective-permute-start | bytes 884744 | tf_op jit(solution)/shard_map/ppermute | solution.py:378
  114.5 3.0 %collective-permute-start.26 = (bf16[1152,128]{1,0:T(8,128)(2,1)S(1)}, bf16[1152,128]{1,0:T(8,128)(2,1)S(1)}, u32[]{:S(2)}, u32[]{:S(2)}) collective-permute-start(bf16[1152,128]{1,0:T(8,128)(2,1)S(1)} %collective-permute-done.22.refs_2_), channel_id=1, source_target_pairs={{0,1},{1,0},{2,3},{3,2},{4,5},{5,4},{6,7},{7,6},{8,9},{9,8},{10,11... | collective-permute-start | bytes 884744 | tf_op jit(solution)/shard_map/ppermute | solution.py:378
  118.7 3.4 %finish.1 = (f32[1024,512]{1,0:T(8,128)}, f32[1024,512]{1,0:T(8,128)}, f32[512,128]{1,0:T(8,128)}, f32[1,512]{1,0:T(1,128)}, f32[1,128]{1,0:T(1,128)}) custom-call(s32[3]{0:T(128)S(1)} %pad_add_fusion.refs_0_, bf16[1152,128]{1,0:T(8,128)(2,1)S(1)} %constant_dynamic-update-slice_fusion.refs_1_, bf16[1152,128]{1,0:T(8,128)(2,1)S(1)} %collective-permute-done.22.refs_2_, ...), custom_call_target="tpu_custom_call" | custom-call | tf_op jit(solution)/shard_map/finish/pallas_call | solution.py:473
  (89 shorter events, 17.2 us)
Async XLA Ops:
  4.6 23.7 %all-to-all-start = ((bf16[32,24,512]{2,1,0:T(8,128)(2,1)}), bf16[32,24,512]{2,1,0:T(8,128)(2,1)S(1)}, u32[]{:S(2)}, u32[]{:S(2)}) async-start(bf16[32,24,512]{2,1,0:T(8,128)(2,1)} %bitcast.5), calls=%async_computation | async-start | bytes 1572864 | tf_op jit(solution)/shard_map/all_to_all | solution.py:396
  14.1 11.3 %collective-permute-start.4 = (bf16[80,512]{1,0:T(8,128)(2,1)S(1)}, bf16[80,512]{1,0:T(8,128)(2,1)S(1)}, u32[]{:S(2)}, u32[]{:S(2)}) collective-permute-start(bf16[80,512]{1,0:T(8,128)(2,1)S(1)} %fusion.2.right_m), channel_id=1, source_target_pairs={{0,31},{1,2},{2,1},{3,4},{4,3},{5,6},{6,5},{7,8},{8,7},{9,10},{10,... | collective-permute-start | bytes 245768 | tf_op jit(solution)/shard_map/ppermute | solution.py:378
  41.3 10.8 %collective-permute-start.6 = (bf16[256,512]{1,0:T(8,128)(2,1)S(1)}, bf16[256,512]{1,0:T(8,128)(2,1)S(1)}, u32[]{:S(2)}, u32[]{:S(2)}) collective-permute-start(bf16[256,512]{1,0:T(8,128)(2,1)S(1)} %get-tuple-element.20), channel_id=1, source_target_pairs={{0,1},{1,0},{2,3},{3,2},{4,5},{5,4},{6,7},{7,6},{8,9},{9,8},{10,11... | collective-permute-start | bytes 786440 | tf_op jit(solution)/shard_map/ppermute | solution.py:378
  43.8 8.3 %collective-permute-start.8 = (bf16[64,512]{1,0:T(8,128)(2,1)S(1)}, bf16[64,512]{1,0:T(8,128)(2,1)S(1)}, u32[]{:S(2)}, u32[]{:S(2)}) collective-permute-start(bf16[64,512]{1,0:T(8,128)(2,1)S(1)} %get-tuple-element.21), channel_id=1, source_target_pairs={{1,3},{3,5},{5,7},{7,9},{9,11},{11,13},{13,15},{15,17},{17,19},{19... | collective-permute-start | bytes 196616 | tf_op jit(solution)/shard_map/ppermute | solution.py:435
  45.7 6.4 %collective-permute-start.7 = (bf16[64,512]{1,0:T(8,128)(2,1)S(1)}, bf16[64,512]{1,0:T(8,128)(2,1)S(1)}, u32[]{:S(2)}, u32[]{:S(2)}) collective-permute-start(bf16[64,512]{1,0:T(8,128)(2,1)S(1)} %get-tuple-element.21), channel_id=1, source_target_pairs={{0,31},{1,2},{2,1},{3,4},{4,3},{5,6},{6,5},{7,8},{8,7},{9,10},{10,... | collective-permute-start | bytes 196616 | tf_op jit(solution)/shard_map/ppermute | solution.py:378
  45.8 13.5 %collective-permute-start.3 = (bf16[128,1024]{1,0:T(8,128)(2,1)S(1)}, bf16[128,1024]{1,0:T(8,128)(2,1)S(1)}, u32[]{:S(2)}, u32[]{:S(2)}) collective-permute-start(bf16[128,1024]{1,0:T(8,128)(2,1)S(1)} %pad_maximum_fusion.refs_0_), channel_id=1, source_target_pairs={{0,4},{1,5},{2,6},{3,7},{4,0},{5,1},{6,2},{7,3},{8,12},{9,13},{10,... | collective-permute-start | bytes 786440 | tf_op jit(solution)/shard_map/ppermute | solution.py:378
  47.9 12.8 %collective-permute-start.2 = (bf16[128,1024]{1,0:T(8,128)(2,1)S(1)}, bf16[128,1024]{1,0:T(8,128)(2,1)S(1)}, u32[]{:S(2)}, u32[]{:S(2)}) collective-permute-start(bf16[128,1024]{1,0:T(8,128)(2,1)S(1)} %pad_maximum_fusion.refs_0_), channel_id=1, source_target_pairs={{0,6},{1,7},{2,0},{3,1},{4,2},{5,3},{6,4},{7,5},{8,14},{9,15},{10,... | collective-permute-start | bytes 786440 | tf_op jit(solution)/shard_map/ppermute | solution.py:378
  52.1 13.4 %collective-permute-start.1 = (bf16[128,1024]{1,0:T(8,128)(2,1)S(1)}, bf16[128,1024]{1,0:T(8,128)(2,1)S(1)}, u32[]{:S(2)}, u32[]{:S(2)}) collective-permute-start(bf16[128,1024]{1,0:T(8,128)(2,1)S(1)} %pad_maximum_fusion.refs_0_), channel_id=1, source_target_pairs={{0,2},{1,3},{2,4},{3,5},{4,6},{5,7},{6,0},{7,1},{8,10},{9,11},{10,... | collective-permute-start | bytes 786440 | tf_op jit(solution)/shard_map/ppermute | solution.py:378
  52.3 13.2 %collective-permute-start.11 = (bf16[256,128]{1,0:T(8,128)(2,1)S(1)}, bf16[256,128]{1,0:T(8,128)(2,1)S(1)}, u32[]{:S(2)}, u32[]{:S(2)}) collective-permute-start(bf16[256,128]{1,0:T(8,128)(2,1)S(1)} %get-tuple-element.35), channel_id=1, source_target_pairs={{0,4},{1,5},{2,6},{3,7},{4,0},{5,1},{6,2},{7,3},{8,12},{9,13},{10,... | collective-permute-start | bytes 196616 | tf_op jit(solution)/shard_map/ppermute | solution.py:378
  52.4 13.1 %collective-permute-start.10 = (bf16[256,128]{1,0:T(8,128)(2,1)S(1)}, bf16[256,128]{1,0:T(8,128)(2,1)S(1)}, u32[]{:S(2)}, u32[]{:S(2)}) collective-permute-start(bf16[256,128]{1,0:T(8,128)(2,1)S(1)} %get-tuple-element.36), channel_id=1, source_target_pairs={{0,6},{1,7},{2,0},{3,1},{4,2},{5,3},{6,4},{7,5},{8,14},{9,15},{10,... | collective-permute-start | bytes 196616 | tf_op jit(solution)/shard_map/ppermute | solution.py:378
  59.3 7.7 %collective-permute-start.9 = (bf16[256,128]{1,0:T(8,128)(2,1)S(1)}, bf16[256,128]{1,0:T(8,128)(2,1)S(1)}, u32[]{:S(2)}, u32[]{:S(2)}) collective-permute-start(bf16[256,128]{1,0:T(8,128)(2,1)S(1)} %get-tuple-element.37), channel_id=1, source_target_pairs={{0,2},{1,3},{2,4},{3,5},{4,6},{5,7},{6,0},{7,1},{8,10},{9,11},{10,... | collective-permute-start | bytes 196616 | tf_op jit(solution)/shard_map/ppermute | solution.py:378
  67.5 6.7 %collective-permute-start.12 = (bf16[288,128]{1,0:T(8,128)(2,1)S(1)}, bf16[288,128]{1,0:T(8,128)(2,1)S(1)}, u32[]{:S(2)}, u32[]{:S(2)}) collective-permute-start(bf16[288,128]{1,0:T(8,128)(2,1)S(1)} %get-tuple-element.32), channel_id=1, source_target_pairs={{0,8},{1,9},{2,10},{3,11},{4,12},{5,13},{6,14},{7,15},{8,16},{9,17... | collective-permute-start | bytes 221192 | tf_op jit(solution)/shard_map/ppermute | solution.py:378
  67.6 6.6 %collective-permute-start.14 = (bf16[288,128]{1,0:T(8,128)(2,1)S(1)}, bf16[288,128]{1,0:T(8,128)(2,1)S(1)}, u32[]{:S(2)}, u32[]{:S(2)}) collective-permute-start(bf16[288,128]{1,0:T(8,128)(2,1)S(1)} %get-tuple-element.33), channel_id=1, source_target_pairs={{0,16},{1,17},{2,18},{3,19},{4,20},{5,21},{6,22},{7,23},{8,24},{9,... | collective-permute-start | bytes 221192 | tf_op jit(solution)/shard_map/ppermute | solution.py:378
  68.9 5.2 %collective-permute-start.13 = (bf16[288,128]{1,0:T(8,128)(2,1)S(1)}, bf16[288,128]{1,0:T(8,128)(2,1)S(1)}, u32[]{:S(2)}, u32[]{:S(2)}) collective-permute-start(bf16[288,128]{1,0:T(8,128)(2,1)S(1)} %get-tuple-element.34), channel_id=1, source_target_pairs={{0,24},{1,25},{2,26},{3,27},{4,28},{5,29},{6,30},{7,31},{8,0},{9,1... | collective-permute-start | bytes 221192 | tf_op jit(solution)/shard_map/ppermute | solution.py:378
  77.5 13.3 %collective-permute-start.18 = (bf16[288,128]{1,0:T(8,128)(2,1)S(1)}, bf16[288,128]{1,0:T(8,128)(2,1)S(1)}, u32[]{:S(2)}, u32[]{:S(2)}) collective-permute-start(bf16[288,128]{1,0:T(8,128)(2,1)S(1)} %add_convert_fusion.2), channel_id=1, source_target_pairs={{0,128},{32,160},{64,192},{96,224},{128,0},{160,32},{192,64},{224,... | collective-permute-start | bytes 221192 | tf_op jit(solution)/shard_map/ppermute | solution.py:393
  86.1 5.4 %collective-permute-start.17 = (bf16[288,128]{1,0:T(8,128)(2,1)S(1)}, bf16[288,128]{1,0:T(8,128)(2,1)S(1)}, u32[]{:S(2)}, u32[]{:S(2)}) collective-permute-start(bf16[288,128]{1,0:T(8,128)(2,1)S(1)} %add_convert_fusion.2), channel_id=1, source_target_pairs={{0,192},{32,224},{64,0},{96,32},{128,64},{160,96},{192,128},{224,1... | collective-permute-start | bytes 221192 | tf_op jit(solution)/shard_map/ppermute | solution.py:393
  86.1 6.8 %collective-permute-start.16 = (bf16[288,128]{1,0:T(8,128)(2,1)S(1)}, bf16[288,128]{1,0:T(8,128)(2,1)S(1)}, u32[]{:S(2)}, u32[]{:S(2)}) collective-permute-start(bf16[288,128]{1,0:T(8,128)(2,1)S(1)} %add_convert_fusion.2), channel_id=1, source_target_pairs={{0,64},{32,96},{64,128},{96,160},{128,192},{160,224},{192,0},{224,... | collective-permute-start | bytes 221192 | tf_op jit(solution)/shard_map/ppermute | solution.py:393
  92.9 7.0 %collective-permute-start.21 = (bf16[288,128]{1,0:T(8,128)(2,1)S(1)}, bf16[288,128]{1,0:T(8,128)(2,1)S(1)}, u32[]{:S(2)}, u32[]{:S(2)}) collective-permute-start(bf16[288,128]{1,0:T(8,128)(2,1)S(1)} %add_convert_fusion.1), channel_id=1, source_target_pairs={{0,16},{1,17},{2,18},{3,19},{4,20},{5,21},{6,22},{7,23},{8,24},{9,... | collective-permute-start | bytes 221192 | tf_op jit(solution)/shard_map/ppermute | solution.py:378
  93.0 6.9 %collective-permute-start.20 = (bf16[288,128]{1,0:T(8,128)(2,1)S(1)}, bf16[288,128]{1,0:T(8,128)(2,1)S(1)}, u32[]{:S(2)}, u32[]{:S(2)}) collective-permute-start(bf16[288,128]{1,0:T(8,128)(2,1)S(1)} %add_convert_fusion.1), channel_id=1, source_target_pairs={{0,24},{1,25},{2,26},{3,27},{4,28},{5,29},{6,30},{7,31},{8,0},{9,1... | collective-permute-start | bytes 221192 | tf_op jit(solution)/shard_map/ppermute | solution.py:378
  100.0 8.3 %collective-permute-start.24 = (bf16[1152,128]{1,0:T(8,128)(2,1)S(1)}, bf16[1152,128]{1,0:T(8,128)(2,1)S(1)}, u32[]{:S(2)}, u32[]{:S(2)}) collective-permute-start(bf16[1152,128]{1,0:T(8,128)(2,1)S(1)} %constant_dynamic-update-slice_fusion.refs_1_), channel_id=1, source_target_pairs={{0,4},{1,5},{2,6},{3,7},{4,0},{5,1},{6,2},{7,3},{8,12},{9,13},{10,... | collective-permute-start | bytes 884744 | tf_op jit(solution)/shard_map/ppermute | solution.py:378
  100.1 14.4 %collective-permute-start.23 = (bf16[1152,128]{1,0:T(8,128)(2,1)S(1)}, bf16[1152,128]{1,0:T(8,128)(2,1)S(1)}, u32[]{:S(2)}, u32[]{:S(2)}) collective-permute-start(bf16[1152,128]{1,0:T(8,128)(2,1)S(1)} %constant_dynamic-update-slice_fusion.refs_1_), channel_id=1, source_target_pairs={{0,6},{1,7},{2,0},{3,1},{4,2},{5,3},{6,4},{7,5},{8,14},{9,15},{10,... | collective-permute-start | bytes 884744 | tf_op jit(solution)/shard_map/ppermute | solution.py:378
  100.2 14.3 %collective-permute-start.22 = (bf16[1152,128]{1,0:T(8,128)(2,1)S(1)}, bf16[1152,128]{1,0:T(8,128)(2,1)S(1)}, u32[]{:S(2)}, u32[]{:S(2)}) collective-permute-start(bf16[1152,128]{1,0:T(8,128)(2,1)S(1)} %constant_dynamic-update-slice_fusion.refs_1_), channel_id=1, source_target_pairs={{0,2},{1,3},{2,4},{3,5},{4,6},{5,7},{6,0},{7,1},{8,10},{9,11},{10,... | collective-permute-start | bytes 884744 | tf_op jit(solution)/shard_map/ppermute | solution.py:378
  101.6 16.0 %collective-permute-start.25 = (bf16[1152,128]{1,0:T(8,128)(2,1)S(1)}, bf16[1152,128]{1,0:T(8,128)(2,1)S(1)}, u32[]{:S(2)}, u32[]{:S(2)}) collective-permute-start(bf16[1152,128]{1,0:T(8,128)(2,1)S(1)} %constant_dynamic-update-slice_fusion.refs_1_), channel_id=1, source_target_pairs={{0,1},{1,0},{2,3},{3,2},{4,5},{5,4},{6,7},{7,6},{8,9},{9,8},{10,11... | collective-permute-start | bytes 884744 | tf_op jit(solution)/shard_map/ppermute | solution.py:378
  108.3 9.3 %collective-permute-start.28 = (bf16[1152,128]{1,0:T(8,128)(2,1)S(1)}, bf16[1152,128]{1,0:T(8,128)(2,1)S(1)}, u32[]{:S(2)}, u32[]{:S(2)}) collective-permute-start(bf16[1152,128]{1,0:T(8,128)(2,1)S(1)} %collective-permute-done.24.refs_4_), channel_id=1, source_target_pairs={{0,1},{1,0},{2,3},{3,2},{4,5},{5,4},{6,7},{7,6},{8,9},{9,8},{10,11... | collective-permute-start | bytes 884744 | tf_op jit(solution)/shard_map/ppermute | solution.py:378
  (18 other events, 147.0 us)
